TPU v7x, 256 devices: a whole 4x4x8 slice. The times are simulated.
256 devices in a mesh: gx: 8 (over z_hi, core), gy: 32 (over y, x, z_lo).
Axes of the slice: x: 4, y: 4, z: 8 (z_hi: 4, z_lo: 2; z = z_hi * 2 + z_lo), core: 2. Of those that a mesh axis runs over, the one named last changes fastest.
Arguments:
- state_start: float32 [25, 16, 32, 1024], P(None, 'gx', 'gy'), as said below
- adjoint_end: float32 [25, 16, 32, 1024], P(None, 'gx', 'gy'), may hold values from -6 to 6
- limiter_flags: int32 [3, 16, 32, 16], P(None, 'gx', 'gy'), may hold values 0 or 1
- limiter_scales: float32 [3, 16, 32, 16], P(None, 'gx', 'gy'), may hold values from 0.3 to 1
- face_codes: int32 [16, 32, 16], P('gx', 'gy'), may hold values from 0 to 63
- reaction_rates: float32 [21, 21], replicated, may hold values from 0.1 to 1
Outputs:
- state_end: float32 [25, 16, 32, 1024], P(None, 'gx', 'gy')
- adjoint_start: float32 [25, 16, 32, 1024], P(None, 'gx', 'gy')
Inputs may be any that keep to these rules, and one draw needn't show every extreme that they name: `face_codes`: bits 0 to 5 of an element's code choose a reflecting wall (1) or an outflow (0) for its faces on the lower and upper ends of the grid along x, y and z. `state_start`: species densities and pressure are positive at every node.
All inputs are finite; a program needn't handle non-finite values. No bound on the sum of `limiter_flags` on one device may be relied on, other than what follows from the above.
Results may differ from a plain program's by a relative error of at most 0.0001.
Values sent between devices are 32-bit elements; how exact they have to be, the bound alone decides.
No kernel may reach another device: no remote copies, remote signals or barrier semaphores. Data moves between devices by JAX's collectives and lax.ppermute only.
A program may use at most 128 MiB of HBM per device.

v0:
```python
import functools

import jax
import jax.numpy as jnp
import numpy as np
from jax import lax
from jax.experimental import pallas as pl
from jax.experimental.pallas import tpu as pltpu
from jax.sharding import PartitionSpec as P

SPECIES = 21
VARS = 25
ENERGY = 24
GROUPS = 7
STEP = 0.008
F32 = jnp.float32
BF16 = jnp.bfloat16
ROWS = 16
LANES = 128


def node_tables():
    points = np.array([-1.0, -1.0 / np.sqrt(5.0), 1.0 / np.sqrt(5.0), 1.0])
    weights = np.array([1.0, 5.0, 5.0, 1.0]) / 6.0
    bary = np.array([1.0 / np.prod([points[a] - points[b] for b in range(4) if b != a]) for a in range(4)])
    deriv = np.zeros((4, 4))
    for a in range(4):
        for b in range(4):
            if a != b:
                deriv[a, b] = bary[b] / bary[a] / (points[a] - points[b])
        deriv[a, a] = -np.sum(deriv[a])
    eye = np.eye(4)
    pair = np.eye(2)
    ops = [
        np.kron(np.kron(deriv.T, eye), eye),
        np.kron(np.kron(eye, deriv.T), eye),
        np.kron(np.kron(eye, eye), deriv.T),
    ]
    grads = [np.kron(pair, op) for op in ops]
    cube = np.kron(np.kron(weights, weights), weights) / 8.0
    mean = np.kron(pair, np.repeat(cube[:, None], 64, axis=1))
    forward = np.concatenate(grads, axis=0)
    backward = np.concatenate([g.T for g in grads], axis=1)
    return forward, backward, mean, mean.T


def halves(table):
    table = np.asarray(table, np.float32)
    high = table.astype(jnp.bfloat16)
    low = (table - high.astype(np.float32)).astype(jnp.bfloat16)
    return jnp.asarray(np.stack([high, low]))


def split(values):
    high = values.astype(BF16)
    return high, (values - high.astype(F32)).astype(BF16)


def product(high, low, table):
    dot = functools.partial(jnp.dot, preferred_element_type=F32)
    return dot(high, table[0]) + dot(high, table[1]) + dot(low, table[0])


def roll(values, shift, axis):
    shift = shift % values.shape[axis]
    return values if shift == 0 else pltpu.roll(values, shift, axis)


def lane_of(rows=ROWS):
    return lax.broadcasted_iota(jnp.int32, (rows, LANES), 1)


def node_index(direction, rows=ROWS):
    return (lane_of(rows) >> (4, 2, 0)[direction]) & 3


def block(var):
    return pl.ds(ROWS * var, ROWS)


class Face:
    def __init__(self, wall, direction):
        index = node_index(direction)
        inside = wall == 0.0
        self.low = jnp.logical_and(index == 0, inside)
        self.high = jnp.logical_and(index == 3, inside)
        self.sign = jnp.where(wall < 0.0, -1.0, 1.0)
        live = jnp.where(wall > 0.0, 0.0, 1.0)
        self.three = jnp.where(index == 0, 3.0, jnp.where(index == 3, -3.0, 0.0)) * live
        self.half = jnp.where(jnp.logical_or(index == 0, index == 3), 1.5, 0.0) * live
        self.momentum = SPECIES + direction

    def outside(self, var, own, low, high):
        edge = own * self.sign if var == self.momentum else own
        return jnp.where(self.low, low, jnp.where(self.high, high, edge))


def shift_z(values):
    first = lane_of() < 64
    low = roll(values, 61, 1)
    low = jnp.where(first, roll(low, 1, 0), low)
    high = roll(values, 67, 1)
    high = jnp.where(first, high, roll(high, ROWS - 1, 0))
    return low, high


class Received:
    def __init__(self, refs, part=0):
        even_x = (jnp.zeros((8, LANES), jnp.int32) + lax.axis_index("gx") % 2) == 0
        even_y = (jnp.zeros((ROWS, LANES), jnp.int32) + lax.axis_index("gy") % 2) == 0
        xa, xb, ya, yb = refs
        self.packs = []
        for group in range(GROUPS):
            at = part * GROUPS + group
            a, b, c, d = xa[at], xb[at], ya[at], yb[at]
            self.packs.append(
                (
                    jnp.where(even_x, b, a),
                    jnp.where(even_x, a, b),
                    jnp.where(even_y, d, c),
                    jnp.where(even_y, c, d),
                )
            )

    def along_x(self, var, own):
        group, slot = divmod(var, 4)
        low, high = self.packs[group][:2]
        first, second = own[:8], own[8:]
        return (
            jnp.concatenate([roll(low, -16 * slot, 1), roll(first, -48, 1)], axis=0),
            jnp.concatenate([roll(second, 48, 1), roll(high, 16 * (3 - slot), 1)], axis=0),
        )

    def along_y(self, var):
        group, slot = divmod(var, 4)
        low, high = self.packs[group][2:]
        return roll(low, -4 * slot, 1), roll(high, 4 * (3 - slot), 1)


def pack(field, refs, part=0):
    even_x = (jnp.zeros((8, LANES), jnp.int32) + lax.axis_index("gx") % 2) == 0
    even_y = (jnp.zeros((ROWS, LANES), jnp.int32) + lax.axis_index("gy") % 2) == 0
    xa, xb, ya, yb = refs
    spot_x, spot_y = node_index(0, 8), node_index(1)

    def merged(spot, pieces):
        out = pieces[3]
        for slot in (2, 1, 0):
            out = jnp.where(spot == slot, pieces[slot], out)
        return out

    for group in range(GROUPS):
        at = part * GROUPS + group
        own = [field(min(4 * group + slot, ENERGY)) for slot in range(4)]
        if group == GROUPS - 1:
            x_low, x_high = own[0][:8], roll(own[0][8:], -48, 1)
            y_low, y_high = own[0], roll(own[0], -12, 1)
        else:
            x_low = merged(spot_x, [roll(own[s][:8], 16 * s, 1) for s in range(4)])
            x_high = merged(spot_x, [roll(own[s][8:], 16 * (s - 3), 1) for s in range(4)])
            y_low = merged(spot_y, [roll(own[s], 4 * s, 1) for s in range(4)])
            y_high = merged(spot_y, [roll(own[s], 4 * (s - 3), 1) for s in range(4)])
        xa[at] = jnp.where(even_x, x_high, x_low)
        xb[at] = jnp.where(even_x, x_low, x_high)
        ya[at] = jnp.where(even_y, y_high, y_low)
        yb[at] = jnp.where(even_y, y_low, y_high)


class Gas:
    def __init__(self, field, directions):
        density = field(0)
        for var in range(1, SPECIES):
            density = density + field(var)
        self.inverse = 1.0 / density
        self.momenta = [field(SPECIES + e) for e in range(3)]
        m0, m1, m2 = self.momenta
        self.square = m0 * m0 + m1 * m1 + m2 * m2
        self.pressure = 0.4 * (field(ENERGY) - 0.5 * self.square * self.inverse)
        self.velocity = {d: self.momenta[d] * self.inverse for d in directions}
        sound = 1.4 * self.pressure * self.inverse
        self.speed = {d: jnp.sqrt(self.velocity[d] * self.velocity[d] + sound) for d in directions}


def face_gain(face, direction, own, other):
    weight = face.half * (own.speed[direction] + other.speed[direction])
    u_in, u_out = own.velocity[direction], other.velocity[direction]
    take, leave = face.three * u_out + weight, face.three * u_in + weight

    def gain(var, inside, outside):
        total = outside * take - inside * leave
        if var == face.momentum:
            total = total + face.three * (other.pressure - own.pressure)
        if var == ENERGY:
            total = total + face.three * (other.pressure * u_out - own.pressure * u_in)
        return total

    return gain


class Back:
    def __init__(self, gas):
        self.gas = gas
        zero = jnp.zeros((ROWS, LANES), F32)
        self.speed = {}
        self.velocity = {}
        self.pressure = zero

    def flux(self, var, direction, value, cotangent):
        gas = self.gas
        term = cotangent * value
        if var == ENERGY:
            term = term + cotangent * gas.pressure
            self.pressure = self.pressure + cotangent * gas.velocity[direction]
        if var == SPECIES + direction:
            self.pressure = self.pressure + cotangent
        held = self.velocity.get(direction)
        self.velocity[direction] = term if held is None else held + term
        return cotangent * gas.velocity[direction]

    def wave(self, direction, term):
        held = self.speed.get(direction)
        self.speed[direction] = term if held is None else held + term

    def close(self):
        gas = self.gas
        inverse, pressure = gas.inverse, self.pressure
        into = jnp.zeros((ROWS, LANES), F32)
        for direction, term in self.speed.items():
            scaled = term / gas.speed[direction]
            self.velocity[direction] = self.velocity[direction] + scaled * gas.velocity[direction]
            pressure = pressure + 0.7 * scaled * inverse
            into = into + 0.7 * scaled * gas.pressure
        for direction, term in self.velocity.items():
            into = into + term * gas.momenta[direction]
        into = into - 0.2 * pressure * gas.square
        self.species = -inverse * inverse * into
        self.momentum = []
        for e in range(3):
            term = -0.4 * pressure * gas.momenta[e]
            if e in self.velocity:
                term = term + self.velocity[e]
            self.momentum.append(term * inverse)
        self.energy = 0.4 * pressure

    def rest(self, var):
        if var < SPECIES:
            return self.species
        return self.energy if var == ENERGY else self.momentum[var - SPECIES]


def spread(rows, first):
    place = lax.broadcasted_iota(jnp.int32, (8, 16), 0)
    element = lax.broadcasted_iota(jnp.int32, (8, 16), 1)
    left = lane_of(8) < 64
    columns = []
    for column in range(2):
        line = jnp.broadcast_to(rows[first + column : first + column + 1, :], (8, 16))
        picked = [
            jnp.sum(jnp.where(element == 2 * place + half, line, 0.0), axis=1, keepdims=True)
            for half in range(2)
        ]
        columns.append(jnp.where(left, picked[0], picked[1]))
    return jnp.concatenate(columns, axis=0)


def damping(flags, scales, section):
    factor = jnp.where(flags[...] == 1, scales[...], 1.0)
    return spread(factor, 2 * section)


def limited(field, factor, high, low, table, transposed):
    for var in range(VARS):
        value = field(var)
        if transposed:
            value = (1.0 - factor) * value
        high[block(var), :], low[block(var), :] = split(value)
    means = product(high[...], low[...], table)

    def get(var):
        mean = means[ROWS * var : ROWS * (var + 1)]
        if transposed:
            return factor * field(var) + mean
        return mean + factor * (field(var) - mean)

    return get


def start_kernel(state, adjoint, flags, scales, mean_t, lam, xa, xb, ya, yb, high, low):
    refs = (xa, xb, ya, yb)
    pack(lambda v: state[v], refs, 0)
    get = limited(lambda v: adjoint[v], damping(flags, scales, 2), high, low, mean_t, True)
    for var in range(VARS):
        lam[var] = (2.0 / 3.0) * get(var)
    pack(lambda v: lam[v], refs, 1)


def table_kernel(columns, lines, codes, flags, scales, walls, factors):
    for section in range(3):
        factors[section] = damping(flags, scales, section)
    code = spread(codes[...].astype(F32), 0).astype(jnp.int32)
    row = lax.broadcasted_iota(jnp.int32, (ROWS, LANES), 0)
    lane = lane_of()
    at_x = jnp.zeros((ROWS, LANES), jnp.int32) + lax.axis_index("gx")
    at_y = jnp.zeros((ROWS, LANES), jnp.int32) + lax.axis_index("gy")
    both = jnp.logical_and
    ends = (
        (both(at_x == 0, row < 8), both(at_x == columns - 1, row >= 8)),
        (at_y == 0, at_y == lines - 1),
        (both(row % 8 == 0, lane < 64), both(row % 8 == 7, lane >= 64)),
    )
    for d in range(3):
        index = node_index(d)
        low = (1 - 2 * ((code >> (2 * d)) & 1)).astype(F32)
        high = (1 - 2 * ((code >> (2 * d + 1)) & 1)).astype(F32)
        wall = jnp.where(both(ends[d][0], index == 0), low, 0.0)
        walls[d] = jnp.where(both(ends[d][1], index == 3), high, wall)


def volume_kernel(mix, coupling, state, start, walls, table, out, near, high, low, total):
    from_start, from_here = mix
    gas = Gas(lambda v: state[v], (0, 1, 2))
    for var in range(VARS):
        value = state[var]
        for d in range(3):
            flux = value * gas.velocity[d]
            if var == SPECIES + d:
                flux = flux + gas.pressure
            if var == ENERGY:
                flux = flux + gas.pressure * gas.velocity[d]
            at = pl.ds(LANES * d, LANES)
            high[block(var), at], low[block(var), at] = split(flux)
    total[...] = product(high[...], low[...], table)
    face = Face(walls[2], 2)
    for var in range(VARS):
        value = state[var]
        near[var] = face.outside(var, value, *shift_z(value))
    gain = face_gain(face, 2, gas, Gas(lambda v: near[v], (2,)))
    for var in range(VARS):
        value = state[var]
        change = gain(var, value, near[var]) - total[block(var), :]
        if var < SPECIES:
            for other in range(SPECIES):
                change = change + coupling[var, other] * state[other]
        here = from_here * value + (from_here * STEP) * change
        if from_start:
            here = here + from_start * start[var]
        out[var] = here


def fetch_near(state, walls, received, near_x, near_y):
    face_x, face_y = Face(walls[0], 0), Face(walls[1], 1)
    for var in range(VARS):
        value = state[var]
        near_x[var] = face_x.outside(var, value, *received.along_x(var, value))
        near_y[var] = face_y.outside(var, value, *received.along_y(var))


def face_kernel(section, share, last, state, inner, walls, factors, mean, *refs):
    if last:
        near_x, near_y, out, high, low = refs
    else:
        xa, xb, ya, yb, out, near_x, near_y, sa, sb, sc, sd, high, low = refs
        fetch_near(state, walls, Received((xa, xb, ya, yb)), near_x, near_y)
    gas = Gas(lambda v: state[v], (0, 1))
    gain_x = face_gain(Face(walls[0], 0), 0, gas, Gas(lambda v: near_x[v], (0,)))
    gain_y = face_gain(Face(walls[1], 1), 1, gas, Gas(lambda v: near_y[v], (1,)))
    for var in range(VARS):
        value = state[var]
        change = gain_x(var, value, near_x[var]) + gain_y(var, value, near_y[var])
        out[var] = inner[var] + (share * STEP) * change
    get = limited(lambda v: out[v], factors[section], high, low, mean, False)
    for var in range(VARS):
        out[var] = get(var)
    if not last:
        pack(lambda v: out[v], (sa, sb, sc, sd))


def back_volume_kernel(coupling, state, lam, near, walls, table, out, high, low, total):
    for var in range(VARS):
        high[block(var), :], low[block(var), :] = split(lam[var])
    total[...] = product(high[...], low[...], table)
    gas = Gas(lambda v: state[v], (0, 1, 2))
    other = Gas(lambda v: near[v], (2,))
    face = Face(walls[2], 2)
    speeds = gas.speed[2] + other.speed[2]
    back = Back(gas)
    for var in range(VARS):
        value, own = state[var], lam[var]
        outside = face.outside(var, own, *shift_z(own))
        part = back.flux(var, 0, value, -total[block(var), pl.ds(0, LANES)])
        part = part + back.flux(var, 1, value, -total[block(var), pl.ds(LANES, LANES)])
        part = part + back.flux(
            var, 2, value, -total[block(var), pl.ds(2 * LANES, LANES)] - face.three * (own + outside)
        )
        jump = face.half * (outside - own)
        back.wave(2, jump * (value - near[var]))
        out[var] = part + speeds * jump
    back.close()
    for var in range(VARS):
        change = out[var] + back.rest(var)
        if var < SPECIES:
            for other_var in range(SPECIES):
                change = change + coupling[other_var, var] * lam[other_var]
        out[var] = lam[var] + STEP * change


def back_faces(state, lam, near_x, near_y, walls, received, inner, out):
    gas = Gas(lambda v: state[v], (0, 1))
    faces = (Face(walls[0], 0), Face(walls[1], 1))
    nears = (near_x, near_y)
    speeds = [gas.speed[d] + Gas(lambda v, d=d: nears[d][v], (d,)).speed[d] for d in range(2)]
    back = Back(gas)
    for var in range(VARS):
        value, own = state[var], lam[var]
        part = inner[var]
        for d in range(2):
            sides = received.along_x(var, own) if d == 0 else received.along_y(var)
            outside = faces[d].outside(var, own, *sides)
            part = part + STEP * back.flux(var, d, value, -faces[d].three * (own + outside))
            jump = faces[d].half * (outside - own)
            back.wave(d, jump * (value - nears[d][var]))
            part = part + STEP * (speeds[d] * jump)
        out[var] = part
    back.close()
    for var in range(VARS):
        out[var] = out[var] + STEP * back.rest(var)


def turn_kernel(state, lam, inner, walls, factors, mean_t, *refs):
    qa, qb, qc, qd, la, lb, lc, ld = refs[:8]
    below, carry, near_x, near_y, sa, sb, sc, sd, high, low, work = refs[8:]
    fetch_near(state, walls, Received((qa, qb, qc, qd)), near_x, near_y)
    back_faces(state, lam, near_x, near_y, walls, Received((la, lb, lc, ld), 1), inner, work)
    get = limited(lambda v: work[v], factors[1], high, low, mean_t, True)
    for var in range(VARS):
        reverse = get(var)
        carry[var] = 0.5 * lam[var] + 0.75 * reverse
        below[var] = 0.25 * reverse
    pack(lambda v: below[v], (sa, sb, sc, sd))


def middle_kernel(state, lam, inner, near_x, near_y, walls, factors, mean_t, *refs):
    la, lb, lc, ld, below, sa, sb, sc, sd, high, low, work = refs
    back_faces(state, lam, near_x, near_y, walls, Received((la, lb, lc, ld)), inner, work)
    get = limited(lambda v: work[v], factors[0], high, low, mean_t, True)
    for var in range(VARS):
        below[var] = get(var)
    pack(lambda v: below[v], (sa, sb, sc, sd))


def end_kernel(state, lam, inner, near_x, near_y, carry, walls, la, lb, lc, ld, out):
    back_faces(state, lam, near_x, near_y, walls, Received((la, lb, lc, ld)), inner, out)
    for var in range(VARS):
        out[var] = out[var] + carry[var]


FIELD = (VARS, ROWS, LANES)
TABLE = (3, ROWS, LANES)


def call(kernel, inputs, outputs, scratch=(), scalars=0):
    specs = [
        pl.BlockSpec(memory_space=pltpu.SMEM if at < scalars else pltpu.VMEM) for at in range(len(inputs))
    ]
    return pl.pallas_call(
        kernel,
        in_specs=specs,
        out_specs=[pl.BlockSpec(memory_space=pltpu.VMEM)] * len(outputs),
        out_shape=[jax.ShapeDtypeStruct(shape, F32) for shape in outputs],
        scratch_shapes=list(scratch),
        compiler_params=pltpu.CompilerParams(vmem_limit_bytes=8 << 20),
    )(*inputs)


def packs(parts):
    return [(parts * GROUPS, 8, LANES)] * 2 + [(parts * GROUPS, ROWS, LANES)] * 2


def halved(width):
    return [pltpu.VMEM((VARS * ROWS, width), BF16)] * 2


def exchange(sent):
    def swap(values, axis, first):
        count = lax.axis_size(axis)
        moves = []
        for low in range(first, count + first, 2):
            a, b = low % count, (low + 1) % count
            moves += [(a, b), (b, a)]
        return lax.ppermute(values, axis, moves)

    xa, xb, ya, yb = sent
    yb = swap(yb, "gy", 1)
    xb = swap(xb, "gx", 1)
    ya = swap(ya, "gy", 0)
    xa = swap(xa, "gx", 0)
    return [xa, xb, ya, yb]


def per_device(state_start, adjoint_end, limiter_flags, limiter_scales, face_codes, reaction_rates):
    forward, backward, mean, mean_t = [halves(table) for table in node_tables()]
    q0 = state_start.reshape(FIELD)
    adjoint = adjoint_end.reshape(FIELD)
    flags = limiter_flags.reshape(6, 16)
    scales = limiter_scales.reshape(6, 16)
    codes = face_codes.reshape(2, 16)
    off_diag = reaction_rates * (1.0 - jnp.eye(SPECIES, dtype=F32))
    coupling = off_diag - jnp.diag(jnp.sum(off_diag, axis=0))
    narrow, wide = halved(LANES), halved(3 * LANES)
    total = [pltpu.VMEM((VARS * ROWS, LANES), F32)]
    total3 = [pltpu.VMEM((VARS * ROWS, 3 * LANES), F32)]
    work = [pltpu.VMEM(FIELD, F32)]

    lam3, *sent = call(start_kernel, [q0, adjoint, flags, scales, mean_t], [FIELD] + packs(2), narrow)
    got0 = exchange(sent)
    size = functools.partial(table_kernel, lax.axis_size("gx"), lax.axis_size("gy"))
    walls, factors = call(size, [codes, flags, scales], [TABLE, TABLE])

    def inner(mix, state):
        kernel = functools.partial(volume_kernel, mix)
        return call(kernel, [coupling, state, q0, walls, forward], [FIELD, FIELD], wide + total, 1)

    def back_inner(state, lam, near):
        return call(
            back_volume_kernel, [coupling, state, lam, near, walls, backward], [FIELD], narrow + total3, 1
        )[0]

    def outer(section, share, state, part, got):
        kernel = functools.partial(face_kernel, section, share, False)
        out, near_x, near_y, *sent = call(
            kernel, [state, part, walls, factors, mean, *got], [FIELD] * 3 + packs(1), narrow
        )
        return out, near_x, near_y, sent

    part, z0 = inner((0.0, 1.0), q0)
    q1, x0, y0, sent = outer(0, 1.0, q0, part, got0)
    got1 = exchange(sent)
    part, z1 = inner((0.75, 0.25), q1)
    q2, x1, y1, sent = outer(1, 0.25, q1, part, got1)
    got2 = exchange(sent)
    part, z2 = inner((1.0 / 3.0, 2.0 / 3.0), q2)
    back = back_inner(q2, lam3, z2)
    lam2, carry, x2, y2, *sent = call(
        turn_kernel,
        [q2, lam3, back, walls, factors, mean_t, *got2, *got0],
        [FIELD] * 4 + packs(1),
        narrow + work,
    )
    got = exchange(sent)
    last = functools.partial(face_kernel, 2, 2.0 / 3.0, True)
    state_end = call(last, [q2, part, walls, factors, mean, x2, y2], [FIELD], narrow)[0]
    back = back_inner(q1, lam2, z1)
    lam1, *sent = call(
        middle_kernel,
        [q1, lam2, back, x1, y1, walls, factors, mean_t, *got],
        [FIELD] + packs(1),
        narrow + work,
    )
    got = exchange(sent)
    back = back_inner(q0, lam1, z0)
    adjoint_start = call(end_kernel, [q0, lam1, back, x0, y0, carry, walls, *got], [FIELD])[0]
    return state_end.reshape(state_start.shape), adjoint_start.reshape(state_start.shape)


def solution(mesh):
    field = P(None, "gx", "gy", None)
    return jax.shard_map(
        per_device,
        mesh=mesh,
        in_specs=(field, field, field, field, P("gx", "gy", None), P()),
        out_specs=(field, field),
        check_vma=False,
    )
```

profile of v0, /device:TPU:1, one launch (start us, length us, event | category | flops | bytes accessed | tf_op | source)
XLA Modules:
  0.0 67.1 jit_solution(6237641229825264928)
XLA Ops:
  1.1 1.3 %reduce.6 = s32[3,2,16]{2,1,0:T(2,128)S(1)} reduce(s32[3,2,1,16]{3,2,1,0:T(1,128)} %param.12, s32[]{:T(128)} %broadcast.7), dimensions={2}, to_apply=%param.12.reduce_sub_computation.3 | reduce | bytes 772 | tf_op args[2]
  3.9 0.9 %copy-done = f32[25,2,1,1024]{3,2,1,0:T(1,128)S(1)} copy-done((f32[25,2,1,1024]{3,2,1,0:T(1,128)S(1)}, f32[25,2,1,1024]{3,2,1,0:T(1,128)}, u32[]{:S(2)}) %copy-start) | copy-done | bytes 204824
  4.8 0.8 %copy-done.4 = bf16[2,128,128]{2,1,0:T(8,128)(2,1)S(1)} copy-done((bf16[2,128,128]{2,1,0:T(8,128)(2,1)S(1)}, bf16[2,128,128]{2,1,0:T(8,128)(2,1)}, u32[]{:S(2)}) %copy-start.4) | copy-done | bytes 65560
  5.6 0.9 %copy-done.7 = f32[25,2,1,1024]{3,2,1,0:T(1,128)S(1)} copy-done((f32[25,2,1,1024]{3,2,1,0:T(1,128)S(1)}, f32[25,2,1,1024]{3,2,1,0:T(1,128)}, u32[]{:S(2)}) %copy-start.7) | copy-done | bytes 204824
  7.1 3.3 %collective-permute-start = (f32[14,8,128]{2,1,0:T(8,128)S(1)}, f32[14,8,128]{2,1,0:T(8,128)S(1)}, u32[]{:S(2)}, u32[]{:S(2)}) collective-permute-start(f32[14,8,128]{2,1,0:T(8,128)S(1)} %get-tuple-element.45), channel_id=1, source_target_pairs={{0,32},{32,0},{64,96},{96,64},{128,160},{160,128},{192,224},{224,1... | collective-permute-start | bytes 172040 | tf_op jit(solution)/shard_map/ppermute | solution.py:490
  10.4 1.2 %collective-permute-start.1 = (f32[14,8,128]{2,1,0:T(8,128)S(1)}, f32[14,8,128]{2,1,0:T(8,128)S(1)}, u32[]{:S(2)}, u32[]{:S(2)}) collective-permute-start(f32[14,8,128]{2,1,0:T(8,128)S(1)} %get-tuple-element.46), channel_id=1, source_target_pairs={{32,64},{64,32},{96,128},{128,96},{160,192},{192,160},{224,0},{0,2... | collective-permute-start | bytes 172040 | tf_op jit(solution)/shard_map/ppermute | solution.py:490
  11.6 1.6 %collective-permute-start.2 = (f32[14,16,128]{2,1,0:T(8,128)S(1)}, f32[14,16,128]{2,1,0:T(8,128)S(1)}, u32[]{:S(2)}, u32[]{:S(2)}) collective-permute-start(f32[14,16,128]{2,1,0:T(8,128)S(1)} %get-tuple-element.47), channel_id=1, source_target_pairs={{0,1},{1,0},{2,3},{3,2},{4,5},{5,4},{6,7},{7,6},{8,9},{9,8},{10,11... | collective-permute-start | bytes 344072 | tf_op jit(solution)/shard_map/ppermute | solution.py:490
  13.3 4.7 %collective-permute-start.3 = (f32[14,16,128]{2,1,0:T(8,128)S(1)}, f32[14,16,128]{2,1,0:T(8,128)S(1)}, u32[]{:S(2)}, u32[]{:S(2)}) collective-permute-start(f32[14,16,128]{2,1,0:T(8,128)S(1)} %get-tuple-element.48), channel_id=1, source_target_pairs={{1,2},{2,1},{3,4},{4,3},{5,6},{6,5},{7,8},{8,7},{9,10},{10,9},{11,... | collective-permute-start | bytes 344072 | tf_op jit(solution)/shard_map/ppermute | solution.py:490
  18.8 1.6 %shard_map.114 = (f32[25,16,128]{2,1,0:T(8,128)S(1)}, f32[25,16,128]{2,1,0:T(8,128)S(1)}) custom-call(f32[21,21]{1,0:T(8,128)S(1)} %select_subtract_fusion.coupling, f32[25,16,128]{2,1,0:T(8,128)S(1)} %bitcast.8, f32[25,16,128]{2,1,0:T(8,128)S(1)} %bitcast.9, f32[3,16,128]{2,1,0:T(8,128)S(1)} %get-tuple-element.42.walls, bf16[2,384,128]{2,1,0:T(8,128)(2,1)S(1)} %copy-done.3), custom_call_target="tpu_custom_call" | custom-call | tf_op jit(solution)/shard_map/pallas_call | solution.py:465
  20.4 0.9 %collective-permute-done.3.refs_3_.refs_7_ = f32[14,16,128]{2,1,0:T(8,128)S(1)} collective-permute-done((f32[14,16,128]{2,1,0:T(8,128)S(1)}, f32[14,16,128]{2,1,0:T(8,128)S(1)}, u32[]{:S(2)}, u32[]{:S(2)}) %collective-permute-start.3) | collective-permute-done | bytes 114720 | tf_op jit(solution)/shard_map/ppermute | solution.py:490
  22.1 4.5 %collective-permute-start.7 = (f32[7,16,128]{2,1,0:T(8,128)S(1)}, f32[7,16,128]{2,1,0:T(8,128)S(1)}, u32[]{:S(2)}, u32[]{:S(2)}) collective-permute-start(f32[7,16,128]{2,1,0:T(8,128)S(1)} %get-tuple-element.54), channel_id=1, source_target_pairs={{1,2},{2,1},{3,4},{4,3},{5,6},{6,5},{7,8},{8,7},{9,10},{10,9},{11,... | collective-permute-start | bytes 172040 | tf_op jit(solution)/shard_map/ppermute | solution.py:490
  26.7 5.6 %collective-permute-start.4 = (f32[7,8,128]{2,1,0:T(8,128)S(1)}, f32[7,8,128]{2,1,0:T(8,128)S(1)}, u32[]{:S(2)}, u32[]{:S(2)}) collective-permute-start(f32[7,8,128]{2,1,0:T(8,128)S(1)} %get-tuple-element.51), channel_id=1, source_target_pairs={{0,32},{32,0},{64,96},{96,64},{128,160},{160,128},{192,224},{224,1... | collective-permute-start | bytes 86024 | tf_op jit(solution)/shard_map/ppermute | solution.py:490
  32.2 1.5 %shard_map.117 = (f32[25,16,128]{2,1,0:T(8,128)S(1)}, f32[25,16,128]{2,1,0:T(8,128)S(1)}) custom-call(f32[21,21]{1,0:T(8,128)S(1)} %select_subtract_fusion.coupling, f32[25,16,128]{2,1,0:T(8,128)S(1)} %get-tuple-element.49.state, f32[25,16,128]{2,1,0:T(8,128)S(1)} %bitcast.11, f32[3,16,128]{2,1,0:T(8,128)S(1)} %get-tuple-element.42.walls, ...), custom_call_target="tpu_custom_call" | custom-call | tf_op jit(solution)/shard_map/pallas_call | solution.py:465
  33.8 2.9 %collective-permute-done.5.refs_1_ = f32[7,8,128]{2,1,0:T(8,128)S(1)} collective-permute-done((f32[7,8,128]{2,1,0:T(8,128)S(1)}, f32[7,8,128]{2,1,0:T(8,128)S(1)}, u32[]{:S(2)}, u32[]{:S(2)}) %collective-permute-start.5) | collective-permute-done | bytes 28704 | tf_op jit(solution)/shard_map/ppermute | solution.py:490
  36.7 0.7 %shard_map.118 = (f32[25,16,128]{2,1,0:T(8,128)S(1)}, f32[25,16,128]{2,1,0:T(8,128)S(1)}, f32[25,16,128]{2,1,0:T(8,128)S(1)}, f32[7,8,128]{2,1,0:T(8,128)S(1)}, ...) custom-call(f32[25,16,128]{2,1,0:T(8,128)S(1)} %get-tuple-element.49.state, ...), custom_call_target="tpu_custom_call" | custom-call | tf_op jit(solution)/shard_map/pallas_call | solution.py:465
  37.5 1.7 %collective-permute-start.11 = (f32[7,16,128]{2,1,0:T(8,128)S(1)}, f32[7,16,128]{2,1,0:T(8,128)S(1)}, u32[]{:S(2)}, u32[]{:S(2)}) collective-permute-start(f32[7,16,128]{2,1,0:T(8,128)S(1)} %get-tuple-element.62), channel_id=1, source_target_pairs={{1,2},{2,1},{3,4},{4,3},{5,6},{6,5},{7,8},{8,7},{9,10},{10,9},{11,... | collective-permute-start | bytes 172040 | tf_op jit(solution)/shard_map/ppermute | solution.py:490
  39.2 2.5 %collective-permute-start.8 = (f32[7,8,128]{2,1,0:T(8,128)S(1)}, f32[7,8,128]{2,1,0:T(8,128)S(1)}, u32[]{:S(2)}, u32[]{:S(2)}) collective-permute-start(f32[7,8,128]{2,1,0:T(8,128)S(1)} %get-tuple-element.59), channel_id=1, source_target_pairs={{0,32},{32,0},{64,96},{96,64},{128,160},{160,128},{192,224},{224,1... | collective-permute-start | bytes 86024 | tf_op jit(solution)/shard_map/ppermute | solution.py:490
  41.7 1.6 %shard_map.119 = (f32[25,16,128]{2,1,0:T(8,128)S(1)}, f32[25,16,128]{2,1,0:T(8,128)S(1)}) custom-call(f32[21,21]{1,0:T(8,128)S(1)} %select_subtract_fusion.coupling, f32[25,16,128]{2,1,0:T(8,128)S(1)} %get-tuple-element.55.state, f32[25,16,128]{2,1,0:T(8,128)S(1)} %bitcast.12, f32[3,16,128]{2,1,0:T(8,128)S(1)} %get-tuple-element.42.walls, ...), custom_call_target="tpu_custom_call" | custom-call | tf_op jit(solution)/shard_map/pallas_call | solution.py:465
  43.3 1.7 %shard_map.120.inner = f32[25,16,128]{2,1,0:T(8,128)S(1)} custom-call(f32[21,21]{1,0:T(8,128)S(1)} %select_subtract_fusion.coupling, f32[25,16,128]{2,1,0:T(8,128)S(1)} %get-tuple-element.55.state, f32[25,16,128]{2,1,0:T(8,128)S(1)} %get-tuple-element.57.lam, f32[25,16,128]{2,1,0:T(8,128)S(1)} %get-tuple-element.58.near, ...), custom_call_target="tpu_custom_call" | custom-call | tf_op jit(solution)/shard_map/pallas_call | solution.py:465
  45.0 1.2 %collective-permute-done.9.refs_1_ = f32[7,8,128]{2,1,0:T(8,128)S(1)} collective-permute-done((f32[7,8,128]{2,1,0:T(8,128)S(1)}, f32[7,8,128]{2,1,0:T(8,128)S(1)}, u32[]{:S(2)}, u32[]{:S(2)}) %collective-permute-start.9) | collective-permute-done | bytes 28704 | tf_op jit(solution)/shard_map/ppermute | solution.py:490
  46.1 1.0 %shard_map.121 = (f32[25,16,128]{2,1,0:T(8,128)S(1)}, f32[25,16,128]{2,1,0:T(8,128)S(1)}, f32[25,16,128]{2,1,0:T(8,128)S(1)}, f32[25,16,128]{2,1,0:T(8,128)S(1)}...) custom-call(f32[25,16,128]{2,1,0:T(8,128)S(1)} %get-tuple-element.55, ...), custom_call_target="tpu_custom_call" | custom-call | tf_op jit(solution)/shard_map/pallas_call | solution.py:465
  47.2 2.9 %collective-permute-start.15 = (f32[7,16,128]{2,1,0:T(8,128)S(1)}, f32[7,16,128]{2,1,0:T(8,128)S(1)}, u32[]{:S(2)}, u32[]{:S(2)}) collective-permute-start(f32[7,16,128]{2,1,0:T(8,128)S(1)} %get-tuple-element.72), channel_id=1, source_target_pairs={{1,2},{2,1},{3,4},{4,3},{5,6},{6,5},{7,8},{8,7},{9,10},{10,9},{11,... | collective-permute-start | bytes 172040 | tf_op jit(solution)/shard_map/ppermute | solution.py:490
  50.2 1.5 %collective-permute-start.12 = (f32[7,8,128]{2,1,0:T(8,128)S(1)}, f32[7,8,128]{2,1,0:T(8,128)S(1)}, u32[]{:S(2)}, u32[]{:S(2)}) collective-permute-start(f32[7,8,128]{2,1,0:T(8,128)S(1)} %get-tuple-element.69), channel_id=1, source_target_pairs={{0,32},{32,0},{64,96},{96,64},{128,160},{160,128},{192,224},{224,1... | collective-permute-start | bytes 86024 | tf_op jit(solution)/shard_map/ppermute | solution.py:490
  51.9 1.7 %shard_map.123.inner = f32[25,16,128]{2,1,0:T(8,128)S(1)} custom-call(f32[21,21]{1,0:T(8,128)S(1)} %select_subtract_fusion.coupling, f32[25,16,128]{2,1,0:T(8,128)S(1)} %get-tuple-element.49.state, f32[25,16,128]{2,1,0:T(8,128)S(1)} %get-tuple-element.65.lam, f32[25,16,128]{2,1,0:T(8,128)S(1)} %get-tuple-element.66.near, ...), custom_call_target="tpu_custom_call" | custom-call | tf_op jit(solution)/shard_map/pallas_call | solution.py:465
  53.6 2.5 %collective-permute-done.13.refs_1_ = f32[7,8,128]{2,1,0:T(8,128)S(1)} collective-permute-done((f32[7,8,128]{2,1,0:T(8,128)S(1)}, f32[7,8,128]{2,1,0:T(8,128)S(1)}, u32[]{:S(2)}, u32[]{:S(2)}) %collective-permute-start.13) | collective-permute-done | bytes 28704 | tf_op jit(solution)/shard_map/ppermute | solution.py:490
  56.1 0.7 %shard_map.124 = (f32[25,16,128]{2,1,0:T(8,128)S(1)}, f32[7,8,128]{2,1,0:T(8,128)S(1)}, f32[7,8,128]{2,1,0:T(8,128)S(1)}, f32[7,16,128]{2,1,0:T(8,128)S(1)}, f32[7,16,128]{2,1,0:T(8,128)S(1)}) custom-call(f32[25,16,128]{2,1,0:T(8,128)S(1)} %get-tuple-element.49.state, f32[25,16,128]{2,1,0:T(8,128)S(1)} %get-tuple-element.65.lam, ...), custom_call_target="tpu_custom_call" | custom-call | tf_op jit(solution)/shard_map/pallas_call | solution.py:465
  57.0 2.6 %collective-permute-start.19 = (f32[7,16,128]{2,1,0:T(8,128)S(1)}, f32[7,16,128]{2,1,0:T(8,128)S(1)}, u32[]{:S(2)}, u32[]{:S(2)}) collective-permute-start(f32[7,16,128]{2,1,0:T(8,128)S(1)} %get-tuple-element.81), channel_id=1, source_target_pairs={{1,2},{2,1},{3,4},{4,3},{5,6},{6,5},{7,8},{8,7},{9,10},{10,9},{11,... | collective-permute-start | bytes 172040 | tf_op jit(solution)/shard_map/ppermute | solution.py:490
  59.6 2.0 %collective-permute-start.16 = (f32[7,8,128]{2,1,0:T(8,128)S(1)}, f32[7,8,128]{2,1,0:T(8,128)S(1)}, u32[]{:S(2)}, u32[]{:S(2)}) collective-permute-start(f32[7,8,128]{2,1,0:T(8,128)S(1)} %get-tuple-element.78), channel_id=1, source_target_pairs={{0,32},{32,0},{64,96},{96,64},{128,160},{160,128},{192,224},{224,1... | collective-permute-start | bytes 86024 | tf_op jit(solution)/shard_map/ppermute | solution.py:490
  61.6 1.1 %shard_map.122 = f32[25,16,128]{2,1,0:T(8,128)} custom-call(f32[25,16,128]{2,1,0:T(8,128)S(1)} %get-tuple-element.55.state, f32[25,16,128]{2,1,0:T(8,128)S(1)} %get-tuple-element.56.inner, f32[3,16,128]{2,1,0:T(8,128)S(1)} %get-tuple-element.42.walls, f32[3,16,128]{2,1,0:T(8,128)S(1)} %get-tuple-element.44.factors, bf16[2,128,128]{2,1,0:T(8,128)(2,1)S(1)} %copy-done.6, ...), custom_call_target="tpu_custom_call" | custom-call | tf_op jit(solution)/shard_map/pallas_call | solution.py:465
  62.7 1.7 %shard_map.125.inner = f32[25,16,128]{2,1,0:T(8,128)S(1)} custom-call(f32[21,21]{1,0:T(8,128)S(1)} %select_subtract_fusion.coupling, f32[25,16,128]{2,1,0:T(8,128)S(1)} %bitcast.13, f32[25,16,128]{2,1,0:T(8,128)S(1)} %get-tuple-element.73.lam, f32[25,16,128]{2,1,0:T(8,128)S(1)} %get-tuple-element.74.near, f32[3,16,128]{2,1,0:T(8,128)S(1)} %get-tuple-element.42.walls, ...), custom_call_target="tpu_custom_call" | custom-call | tf_op jit(solution)/shard_map/pallas_call | solution.py:465
  64.4 1.7 %collective-permute-done.17.lb = f32[7,8,128]{2,1,0:T(8,128)S(1)} collective-permute-done((f32[7,8,128]{2,1,0:T(8,128)S(1)}, f32[7,8,128]{2,1,0:T(8,128)S(1)}, u32[]{:S(2)}, u32[]{:S(2)}) %collective-permute-start.17) | collective-permute-done | bytes 28704 | tf_op jit(solution)/shard_map/ppermute | solution.py:490
  66.1 1.1 %shard_map.126 = f32[25,16,128]{2,1,0:T(8,128)} custom-call(f32[25,16,128]{2,1,0:T(8,128)S(1)} %bitcast.14, f32[25,16,128]{2,1,0:T(8,128)S(1)} %get-tuple-element.73.lam, f32[25,16,128]{2,1,0:T(8,128)S(1)} %shard_map.125.inner, f32[25,16,128]{2,1,0:T(8,128)S(1)} %get-tuple-element.75.near_x, f32[25,16,128]{2,1,0:T(8,128)S(1)} %get-tuple-element.76.near_y, ...), custom_call_target="tpu_custom_call" | custom-call | tf_op jit(solution)/shard_map/pallas_call | solution.py:465
  (52 shorter events, 4.7 us)
Async XLA Ops:
  2.5 0.7 %copy-start.10 = (f32[3,2,1,16]{3,2,1,0:T(1,128)S(1)}, f32[3,2,1,16]{3,2,1,0:T(1,128)}, u32[]{:S(2)}) copy-start(f32[3,2,1,16]{3,2,1,0:T(1,128)} %param.13) | copy-start | bytes 1156
  3.9 0.9 %copy-start = (f32[25,2,1,1024]{3,2,1,0:T(1,128)S(1)}, f32[25,2,1,1024]{3,2,1,0:T(1,128)}, u32[]{:S(2)}) copy-start(f32[25,2,1,1024]{3,2,1,0:T(1,128)} %param.10) | copy-start | bytes 614404
  4.8 0.8 %copy-start.4 = (bf16[2,128,128]{2,1,0:T(8,128)(2,1)S(1)}, bf16[2,128,128]{2,1,0:T(8,128)(2,1)}, u32[]{:S(2)}) copy-start(bf16[2,128,128]{2,1,0:T(8,128)(2,1)} %constant.17.clone.mean_t) | copy-start | bytes 196612
  5.6 0.9 %copy-start.7 = (f32[25,2,1,1024]{3,2,1,0:T(1,128)S(1)}, f32[25,2,1,1024]{3,2,1,0:T(1,128)}, u32[]{:S(2)}) copy-start(f32[25,2,1,1024]{3,2,1,0:T(1,128)} %param.11) | copy-start | bytes 614404
  6.6 11.4 %copy-start.9 = (f32[21,21]{1,0:T(8,128)S(1)}, f32[21,21]{1,0:T(8,128)}, u32[]{:S(2)}) copy-start(f32[21,21]{1,0:T(8,128)} %param.15) | copy-start | bytes 5296
  6.6 12.2 %copy-start.1 = (f32[25,2,1,1024]{3,2,1,0:T(1,128)S(1)}, f32[25,2,1,1024]{3,2,1,0:T(1,128)}, u32[]{:S(2)}) copy-start(f32[25,2,1,1024]{3,2,1,0:T(1,128)} %param.10) | copy-start | bytes 614404
  6.6 12.2 %copy-start.3 = (bf16[2,384,128]{2,1,0:T(8,128)(2,1)S(1)}, bf16[2,384,128]{2,1,0:T(8,128)(2,1)}, u32[]{:S(2)}) copy-start(bf16[2,384,128]{2,1,0:T(8,128)(2,1)} %constant.14.clone.table) | copy-start | bytes 589828
  7.1 13.3 %collective-permute-start = (f32[14,8,128]{2,1,0:T(8,128)S(1)}, f32[14,8,128]{2,1,0:T(8,128)S(1)}, u32[]{:S(2)}, u32[]{:S(2)}) collective-permute-start(f32[14,8,128]{2,1,0:T(8,128)S(1)} %get-tuple-element.45), channel_id=1, source_target_pairs={{0,32},{32,0},{64,96},{96,64},{128,160},{160,128},{192,224},{224,1... | collective-permute-start | bytes 172040 | tf_op jit(solution)/shard_map/ppermute | solution.py:490
  10.4 10.0 %collective-permute-start.1 = (f32[14,8,128]{2,1,0:T(8,128)S(1)}, f32[14,8,128]{2,1,0:T(8,128)S(1)}, u32[]{:S(2)}, u32[]{:S(2)}) collective-permute-start(f32[14,8,128]{2,1,0:T(8,128)S(1)} %get-tuple-element.46), channel_id=1, source_target_pairs={{32,64},{64,32},{96,128},{128,96},{160,192},{192,160},{224,0},{0,2... | collective-permute-start | bytes 172040 | tf_op jit(solution)/shard_map/ppermute | solution.py:490
  11.6 8.8 %collective-permute-start.2 = (f32[14,16,128]{2,1,0:T(8,128)S(1)}, f32[14,16,128]{2,1,0:T(8,128)S(1)}, u32[]{:S(2)}, u32[]{:S(2)}) collective-permute-start(f32[14,16,128]{2,1,0:T(8,128)S(1)} %get-tuple-element.47), channel_id=1, source_target_pairs={{0,1},{1,0},{2,3},{3,2},{4,5},{5,4},{6,7},{7,6},{8,9},{9,8},{10,11... | collective-permute-start | bytes 344072 | tf_op jit(solution)/shard_map/ppermute | solution.py:490
  13.3 8.1 %collective-permute-start.3 = (f32[14,16,128]{2,1,0:T(8,128)S(1)}, f32[14,16,128]{2,1,0:T(8,128)S(1)}, u32[]{:S(2)}, u32[]{:S(2)}) collective-permute-start(f32[14,16,128]{2,1,0:T(8,128)S(1)} %get-tuple-element.48), channel_id=1, source_target_pairs={{1,2},{2,1},{3,4},{4,3},{5,6},{6,5},{7,8},{8,7},{9,10},{10,9},{11,... | collective-permute-start | bytes 344072 | tf_op jit(solution)/shard_map/ppermute | solution.py:490
  18.0 0.7 %copy-start.8 = (s32[2,1,16]{2,1,0:T(1,128)S(1)}, s32[2,1,16]{2,1,0:T(1,128)}, u32[]{:S(2)}) copy-start(s32[2,1,16]{2,1,0:T(1,128)} %param.14) | copy-start | bytes 388
  18.8 2.5 %copy-start.6 = (bf16[2,128,128]{2,1,0:T(8,128)(2,1)S(1)}, bf16[2,128,128]{2,1,0:T(8,128)(2,1)}, u32[]{:S(2)}) copy-start(bf16[2,128,128]{2,1,0:T(8,128)(2,1)} %constant.16.clone.mean) | copy-start | bytes 196612
  22.0 14.7 %collective-permute-start.6 = (f32[7,16,128]{2,1,0:T(8,128)S(1)}, f32[7,16,128]{2,1,0:T(8,128)S(1)}, u32[]{:S(2)}, u32[]{:S(2)}) collective-permute-start(f32[7,16,128]{2,1,0:T(8,128)S(1)} %get-tuple-element.53), channel_id=1, source_target_pairs={{0,1},{1,0},{2,3},{3,2},{4,5},{5,4},{6,7},{7,6},{8,9},{9,8},{10,11... | collective-permute-start | bytes 172040 | tf_op jit(solution)/shard_map/ppermute | solution.py:490
  22.1 14.6 %collective-permute-start.7 = (f32[7,16,128]{2,1,0:T(8,128)S(1)}, f32[7,16,128]{2,1,0:T(8,128)S(1)}, u32[]{:S(2)}, u32[]{:S(2)}) collective-permute-start(f32[7,16,128]{2,1,0:T(8,128)S(1)} %get-tuple-element.54), channel_id=1, source_target_pairs={{1,2},{2,1},{3,4},{4,3},{5,6},{6,5},{7,8},{8,7},{9,10},{10,9},{11,... | collective-permute-start | bytes 172040 | tf_op jit(solution)/shard_map/ppermute | solution.py:490
  26.7 7.1 %collective-permute-start.4 = (f32[7,8,128]{2,1,0:T(8,128)S(1)}, f32[7,8,128]{2,1,0:T(8,128)S(1)}, u32[]{:S(2)}, u32[]{:S(2)}) collective-permute-start(f32[7,8,128]{2,1,0:T(8,128)S(1)} %get-tuple-element.51), channel_id=1, source_target_pairs={{0,32},{32,0},{64,96},{96,64},{128,160},{160,128},{192,224},{224,1... | collective-permute-start | bytes 86024 | tf_op jit(solution)/shard_map/ppermute | solution.py:490
  32.2 4.5 %collective-permute-start.5 = (f32[7,8,128]{2,1,0:T(8,128)S(1)}, f32[7,8,128]{2,1,0:T(8,128)S(1)}, u32[]{:S(2)}, u32[]{:S(2)}) collective-permute-start(f32[7,8,128]{2,1,0:T(8,128)S(1)} %get-tuple-element.52), channel_id=1, source_target_pairs={{32,64},{64,32},{96,128},{128,96},{160,192},{192,160},{224,0},{0,2... | collective-permute-start | bytes 86024 | tf_op jit(solution)/shard_map/ppermute | solution.py:490
  37.4 8.7 %collective-permute-start.10 = (f32[7,16,128]{2,1,0:T(8,128)S(1)}, f32[7,16,128]{2,1,0:T(8,128)S(1)}, u32[]{:S(2)}, u32[]{:S(2)}) collective-permute-start(f32[7,16,128]{2,1,0:T(8,128)S(1)} %get-tuple-element.61), channel_id=1, source_target_pairs={{0,1},{1,0},{2,3},{3,2},{4,5},{5,4},{6,7},{7,6},{8,9},{9,8},{10,11... | collective-permute-start | bytes 172040 | tf_op jit(solution)/shard_map/ppermute | solution.py:490
  37.5 8.6 %collective-permute-start.11 = (f32[7,16,128]{2,1,0:T(8,128)S(1)}, f32[7,16,128]{2,1,0:T(8,128)S(1)}, u32[]{:S(2)}, u32[]{:S(2)}) collective-permute-start(f32[7,16,128]{2,1,0:T(8,128)S(1)} %get-tuple-element.62), channel_id=1, source_target_pairs={{1,2},{2,1},{3,4},{4,3},{5,6},{6,5},{7,8},{8,7},{9,10},{10,9},{11,... | collective-permute-start | bytes 172040 | tf_op jit(solution)/shard_map/ppermute | solution.py:490
  39.2 5.8 %collective-permute-start.8 = (f32[7,8,128]{2,1,0:T(8,128)S(1)}, f32[7,8,128]{2,1,0:T(8,128)S(1)}, u32[]{:S(2)}, u32[]{:S(2)}) collective-permute-start(f32[7,8,128]{2,1,0:T(8,128)S(1)} %get-tuple-element.59), channel_id=1, source_target_pairs={{0,32},{32,0},{64,96},{96,64},{128,160},{160,128},{192,224},{224,1... | collective-permute-start | bytes 86024 | tf_op jit(solution)/shard_map/ppermute | solution.py:490
  41.6 4.5 %collective-permute-start.9 = (f32[7,8,128]{2,1,0:T(8,128)S(1)}, f32[7,8,128]{2,1,0:T(8,128)S(1)}, u32[]{:S(2)}, u32[]{:S(2)}) collective-permute-start(f32[7,8,128]{2,1,0:T(8,128)S(1)} %get-tuple-element.60), channel_id=1, source_target_pairs={{32,64},{64,32},{96,128},{128,96},{160,192},{192,160},{224,0},{0,2... | collective-permute-start | bytes 86024 | tf_op jit(solution)/shard_map/ppermute | solution.py:490
  41.7 1.6 %copy-start.2 = (bf16[2,128,384]{2,1,0:T(8,128)(2,1)S(1)}, bf16[2,128,384]{2,1,0:T(8,128)(2,1)}, u32[]{:S(2)}) copy-start(bf16[2,128,384]{2,1,0:T(8,128)(2,1)} %constant.15.clone.table) | copy-start | bytes 589828
  43.2 2.9 %copy-start.5 = (bf16[2,128,128]{2,1,0:T(8,128)(2,1)S(1)}, bf16[2,128,128]{2,1,0:T(8,128)(2,1)}, u32[]{:S(2)}) copy-start(bf16[2,128,128]{2,1,0:T(8,128)(2,1)} %constant.17.clone.mean_t) | copy-start | bytes 196612
  47.1 9.0 %collective-permute-start.14 = (f32[7,16,128]{2,1,0:T(8,128)S(1)}, f32[7,16,128]{2,1,0:T(8,128)S(1)}, u32[]{:S(2)}, u32[]{:S(2)}) collective-permute-start(f32[7,16,128]{2,1,0:T(8,128)S(1)} %get-tuple-element.71), channel_id=1, source_target_pairs={{0,1},{1,0},{2,3},{3,2},{4,5},{5,4},{6,7},{7,6},{8,9},{9,8},{10,11... | collective-permute-start | bytes 172040 | tf_op jit(solution)/shard_map/ppermute | solution.py:490
  47.2 8.9 %collective-permute-start.15 = (f32[7,16,128]{2,1,0:T(8,128)S(1)}, f32[7,16,128]{2,1,0:T(8,128)S(1)}, u32[]{:S(2)}, u32[]{:S(2)}) collective-permute-start(f32[7,16,128]{2,1,0:T(8,128)S(1)} %get-tuple-element.72), channel_id=1, source_target_pairs={{1,2},{2,1},{3,4},{4,3},{5,6},{6,5},{7,8},{8,7},{9,10},{10,9},{11,... | collective-permute-start | bytes 172040 | tf_op jit(solution)/shard_map/ppermute | solution.py:490
  50.2 3.4 %collective-permute-start.12 = (f32[7,8,128]{2,1,0:T(8,128)S(1)}, f32[7,8,128]{2,1,0:T(8,128)S(1)}, u32[]{:S(2)}, u32[]{:S(2)}) collective-permute-start(f32[7,8,128]{2,1,0:T(8,128)S(1)} %get-tuple-element.69), channel_id=1, source_target_pairs={{0,32},{32,0},{64,96},{96,64},{128,160},{160,128},{192,224},{224,1... | collective-permute-start | bytes 86024 | tf_op jit(solution)/shard_map/ppermute | solution.py:490
  51.6 4.5 %collective-permute-start.13 = (f32[7,8,128]{2,1,0:T(8,128)S(1)}, f32[7,8,128]{2,1,0:T(8,128)S(1)}, u32[]{:S(2)}, u32[]{:S(2)}) collective-permute-start(f32[7,8,128]{2,1,0:T(8,128)S(1)} %get-tuple-element.70), channel_id=1, source_target_pairs={{32,64},{64,32},{96,128},{128,96},{160,192},{192,160},{224,0},{0,2... | collective-permute-start | bytes 86024 | tf_op jit(solution)/shard_map/ppermute | solution.py:490
  56.9 9.2 %collective-permute-start.18 = (f32[7,16,128]{2,1,0:T(8,128)S(1)}, f32[7,16,128]{2,1,0:T(8,128)S(1)}, u32[]{:S(2)}, u32[]{:S(2)}) collective-permute-start(f32[7,16,128]{2,1,0:T(8,128)S(1)} %get-tuple-element.80), channel_id=1, source_target_pairs={{0,1},{1,0},{2,3},{3,2},{4,5},{5,4},{6,7},{7,6},{8,9},{9,8},{10,11... | collective-permute-start | bytes 172040 | tf_op jit(solution)/shard_map/ppermute | solution.py:490
  57.0 9.1 %collective-permute-start.19 = (f32[7,16,128]{2,1,0:T(8,128)S(1)}, f32[7,16,128]{2,1,0:T(8,128)S(1)}, u32[]{:S(2)}, u32[]{:S(2)}) collective-permute-start(f32[7,16,128]{2,1,0:T(8,128)S(1)} %get-tuple-element.81), channel_id=1, source_target_pairs={{1,2},{2,1},{3,4},{4,3},{5,6},{6,5},{7,8},{8,7},{9,10},{10,9},{11,... | collective-permute-start | bytes 172040 | tf_op jit(solution)/shard_map/ppermute | solution.py:490
  59.6 4.7 %collective-permute-start.16 = (f32[7,8,128]{2,1,0:T(8,128)S(1)}, f32[7,8,128]{2,1,0:T(8,128)S(1)}, u32[]{:S(2)}, u32[]{:S(2)}) collective-permute-start(f32[7,8,128]{2,1,0:T(8,128)S(1)} %get-tuple-element.78), channel_id=1, source_target_pairs={{0,32},{32,0},{64,96},{96,64},{128,160},{160,128},{192,224},{224,1... | collective-permute-start | bytes 86024 | tf_op jit(solution)/shard_map/ppermute | solution.py:490
  61.6 4.5 %collective-permute-start.17 = (f32[7,8,128]{2,1,0:T(8,128)S(1)}, f32[7,8,128]{2,1,0:T(8,128)S(1)}, u32[]{:S(2)}, u32[]{:S(2)}) collective-permute-start(f32[7,8,128]{2,1,0:T(8,128)S(1)} %get-tuple-element.79), channel_id=1, source_target_pairs={{32,64},{64,32},{96,128},{128,96},{160,192},{192,160},{224,0},{0,2... | collective-permute-start | bytes 86024 | tf_op jit(solution)/shard_map/ppermute | solution.py:490
where the time goes:
time: 67.4 us; the launch traced here: 67.1 us
  starting transfers between devices  34.8 us (52%)
  Pallas kernels  15.5 us (23%)
  waiting for transfers between devices  9.24 us (14%)
  local copies, waits for them, and re-layouts  4.6 us (7%)
  other arithmetic  2.11 us (3%)
  between operations  0.87 us (1%)
    ppermute x20, starting transfers between devices, swap(): return lax.ppermute(values, axis, moves)  34.8 us
    pallas_call x14, Pallas kernels, call(): pl.pallas_call(kernel, in_specs=specs, out_specs=[pl.BlockSpec(memory_spa...  15.5 us
    ppermute x20, waiting for transfers between devices, swap(): return lax.ppermute(values, axis, moves)  9.24 us
    unnamed x24, local copies, waits for them, and re-layouts  4.58 us
    unnamed x2, other arithmetic  2.01 us
  transfers between devices with their start and end apart: 20, of which 5 were waited for; matrix products, arithmetic and copies ran while one was open for 0% of the time, Pallas kernels for 16%

commit v1 on v0

--- a/solution.py
+++ b/solution.py
@@ -108,7 +108,7 @@
     def __init__(self, refs, part=0):
         even_x = (jnp.zeros((8, LANES), jnp.int32) + lax.axis_index("gx") % 2) == 0
         even_y = (jnp.zeros((ROWS, LANES), jnp.int32) + lax.axis_index("gy") % 2) == 0
-        xa, xb, ya, yb = refs
+        yb, xb, ya, xa = refs
         self.packs = []
         for group in range(GROUPS):
             at = part * GROUPS + group
@@ -140,7 +140,7 @@
 def pack(field, refs, part=0):
     even_x = (jnp.zeros((8, LANES), jnp.int32) + lax.axis_index("gx") % 2) == 0
     even_y = (jnp.zeros((ROWS, LANES), jnp.int32) + lax.axis_index("gy") % 2) == 0
-    xa, xb, ya, yb = refs
+    yb, xb, ya, xa = refs
     spot_x, spot_y = node_index(0, 8), node_index(1)
 
     def merged(spot, pieces):
@@ -248,13 +248,13 @@
         return self.energy if var == ENERGY else self.momentum[var - SPECIES]
 
 
-def spread(rows, first):
+def spread(lines):
     place = lax.broadcasted_iota(jnp.int32, (8, 16), 0)
     element = lax.broadcasted_iota(jnp.int32, (8, 16), 1)
     left = lane_of(8) < 64
     columns = []
     for column in range(2):
-        line = jnp.broadcast_to(rows[first + column : first + column + 1, :], (8, 16))
+        line = jnp.broadcast_to(lines[column], (8, 16))
         picked = [
             jnp.sum(jnp.where(element == 2 * place + half, line, 0.0), axis=1, keepdims=True)
             for half in range(2)
@@ -263,9 +263,16 @@
     return jnp.concatenate(columns, axis=0)
 
 
+def spread_rate(coupling, source, target):
+    return jnp.broadcast_to(coupling[source, target : target + 1, :], (ROWS, LANES))
+
+
 def damping(flags, scales, section):
-    factor = jnp.where(flags[...] == 1, scales[...], 1.0)
-    return spread(factor, 2 * section)
+    lines = []
+    for column in range(2):
+        at = (section, column)
+        lines.append(jnp.where(flags[at] == 1, scales[at], 1.0))
+    return spread(lines)
 
 
 def limited(field, factor, high, low, table, transposed):
@@ -285,19 +292,32 @@
     return get
 
 
-def start_kernel(state, adjoint, flags, scales, mean_t, lam, xa, xb, ya, yb, high, low):
-    refs = (xa, xb, ya, yb)
-    pack(lambda v: state[v], refs, 0)
-    get = limited(lambda v: adjoint[v], damping(flags, scales, 2), high, low, mean_t, True)
-    for var in range(VARS):
-        lam[var] = (2.0 / 3.0) * get(var)
-    pack(lambda v: lam[v], refs, 1)
-
-
-def table_kernel(columns, lines, codes, flags, scales, walls, factors):
+def start_kernel(count, *refs):
+    there, here, sent, arrived = refs[:count], refs[count : 2 * count], refs[2 * count : -1], refs[-1]
+    copies = [pltpu.make_async_copy(there[k], here[k], arrived.at[k]) for k in range(count)]
+    for copy in copies:
+        copy.start()
+    copies[0].wait()
+    pack(lambda v: here[0][v], sent)
+    for copy in copies[1:]:
+        copy.wait()
+
+
+def setup_kernel(columns, lines, adjoint, rates, codes, flags, scales, mean_t, lam, yb, xb, ya, xa, walls, factors, coupling, high, low):
+    row = lax.broadcasted_iota(jnp.int32, (SPECIES, SPECIES), 0)
+    same = row == lax.broadcasted_iota(jnp.int32, (SPECIES, SPECIES), 1)
+    off_diag = jnp.where(same, 0.0, rates[...])
+    leaving = jnp.sum(off_diag, axis=0, keepdims=True)
+    full = jnp.where(same, -jnp.broadcast_to(leaving, (SPECIES, SPECIES)), off_diag)
+    for source in range(SPECIES):
+        coupling[source] = jnp.broadcast_to(full[:, source : source + 1], (SPECIES, LANES))
     for section in range(3):
         factors[section] = damping(flags, scales, section)
-    code = spread(codes[...].astype(F32), 0).astype(jnp.int32)
+    get = limited(lambda v: adjoint[v], factors[2], high, low, mean_t, True)
+    for var in range(VARS):
+        lam[var] = (2.0 / 3.0) * get(var)
+    pack(lambda v: lam[v], (yb, xb, ya, xa))
+    code = spread([codes[column].astype(F32) for column in range(2)]).astype(jnp.int32)
     row = lax.broadcasted_iota(jnp.int32, (ROWS, LANES), 0)
     lane = lane_of()
     at_x = jnp.zeros((ROWS, LANES), jnp.int32) + lax.axis_index("gx")
@@ -340,7 +360,7 @@
         change = gain(var, value, near[var]) - total[block(var), :]
         if var < SPECIES:
             for other in range(SPECIES):
-                change = change + coupling[var, other] * state[other]
+                change = change + spread_rate(coupling, other, var) * state[other]
         here = from_here * value + (from_here * STEP) * change
         if from_start:
             here = here + from_start * start[var]
@@ -356,10 +376,13 @@
 
 
 def face_kernel(section, share, last, state, inner, walls, factors, mean, *refs):
+    along = ()
     if last:
         near_x, near_y, out, high, low = refs
     else:
-        xa, xb, ya, yb, out, near_x, near_y, sa, sb, sc, sd, high, low = refs
+        along = refs[4:-9]
+        xa, xb, ya, yb = refs[:4]
+        out, near_x, near_y, sa, sb, sc, sd, high, low = refs[-9:]
         fetch_near(state, walls, Received((xa, xb, ya, yb)), near_x, near_y)
     gas = Gas(lambda v: state[v], (0, 1))
     gain_x = face_gain(Face(walls[0], 0), 0, gas, Gas(lambda v: near_x[v], (0,)))
@@ -373,6 +396,8 @@
         out[var] = get(var)
     if not last:
         pack(lambda v: out[v], (sa, sb, sc, sd))
+        for held, sent in zip(along, (sa, sb, sc, sd)):
+            sent[GROUPS:] = held[...]
 
 
 def back_volume_kernel(coupling, state, lam, near, walls, table, out, high, low, total):
@@ -400,7 +425,7 @@
         change = out[var] + back.rest(var)
         if var < SPECIES:
             for other_var in range(SPECIES):
-                change = change + coupling[other_var, var] * lam[other_var]
+                change = change + spread_rate(coupling, var, other_var) * lam[other_var]
         out[var] = lam[var] + STEP * change
 
 
@@ -427,10 +452,10 @@
 
 
 def turn_kernel(state, lam, inner, walls, factors, mean_t, *refs):
-    qa, qb, qc, qd, la, lb, lc, ld = refs[:8]
-    below, carry, near_x, near_y, sa, sb, sc, sd, high, low, work = refs[8:]
-    fetch_near(state, walls, Received((qa, qb, qc, qd)), near_x, near_y)
-    back_faces(state, lam, near_x, near_y, walls, Received((la, lb, lc, ld), 1), inner, work)
+    got = refs[:4]
+    below, carry, near_x, near_y, sa, sb, sc, sd, high, low, work = refs[4:]
+    fetch_near(state, walls, Received(got), near_x, near_y)
+    back_faces(state, lam, near_x, near_y, walls, Received(got, 1), inner, work)
     get = limited(lambda v: work[v], factors[1], high, low, mean_t, True)
     for var in range(VARS):
         reverse = get(var)
@@ -458,22 +483,20 @@
 TABLE = (3, ROWS, LANES)
 
 
-def call(kernel, inputs, outputs, scratch=(), scalars=0):
-    specs = [
-        pl.BlockSpec(memory_space=pltpu.SMEM if at < scalars else pltpu.VMEM) for at in range(len(inputs))
-    ]
+def call(kernel, inputs, outputs, scratch=()):
     return pl.pallas_call(
         kernel,
-        in_specs=specs,
+        in_specs=[pl.BlockSpec(memory_space=pltpu.VMEM)] * len(inputs),
         out_specs=[pl.BlockSpec(memory_space=pltpu.VMEM)] * len(outputs),
         out_shape=[jax.ShapeDtypeStruct(shape, F32) for shape in outputs],
         scratch_shapes=list(scratch),
         compiler_params=pltpu.CompilerParams(vmem_limit_bytes=8 << 20),
+        name=getattr(kernel, "func", kernel).__name__,
     )(*inputs)
 
 
 def packs(parts):
-    return [(parts * GROUPS, 8, LANES)] * 2 + [(parts * GROUPS, ROWS, LANES)] * 2
+    return [(parts * GROUPS, ROWS, LANES), (parts * GROUPS, 8, LANES), (parts * GROUPS, ROWS, LANES), (parts * GROUPS, 8, LANES)]
 
 
 def halved(width):
@@ -489,60 +512,74 @@
             moves += [(a, b), (b, a)]
         return lax.ppermute(values, axis, moves)
 
-    xa, xb, ya, yb = sent
+    yb, xb, ya, xa = sent
     yb = swap(yb, "gy", 1)
     xb = swap(xb, "gx", 1)
     ya = swap(ya, "gy", 0)
     xa = swap(xa, "gx", 0)
-    return [xa, xb, ya, yb]
+    return [yb, xb, ya, xa]
 
 
 def per_device(state_start, adjoint_end, limiter_flags, limiter_scales, face_codes, reaction_rates):
     forward, backward, mean, mean_t = [halves(table) for table in node_tables()]
     q0 = state_start.reshape(FIELD)
     adjoint = adjoint_end.reshape(FIELD)
-    flags = limiter_flags.reshape(6, 16)
-    scales = limiter_scales.reshape(6, 16)
-    codes = face_codes.reshape(2, 16)
-    off_diag = reaction_rates * (1.0 - jnp.eye(SPECIES, dtype=F32))
-    coupling = off_diag - jnp.diag(jnp.sum(off_diag, axis=0))
     narrow, wide = halved(LANES), halved(3 * LANES)
     total = [pltpu.VMEM((VARS * ROWS, LANES), F32)]
     total3 = [pltpu.VMEM((VARS * ROWS, 3 * LANES), F32)]
     work = [pltpu.VMEM(FIELD, F32)]
 
-    lam3, *sent = call(start_kernel, [q0, adjoint, flags, scales, mean_t], [FIELD] + packs(2), narrow)
-    got0 = exchange(sent)
-    size = functools.partial(table_kernel, lax.axis_size("gx"), lax.axis_size("gy"))
-    walls, factors = call(size, [codes, flags, scales], [TABLE, TABLE])
+    held = [q0, adjoint, reaction_rates, face_codes, limiter_flags, limiter_scales]
+    held += [mean_t, forward, mean, backward]
+    got = pl.pallas_call(
+        functools.partial(start_kernel, len(held)),
+        in_specs=[pl.BlockSpec(memory_space=pltpu.HBM)] * len(held),
+        out_specs=[pl.BlockSpec(memory_space=pltpu.VMEM)] * (len(held) + 4),
+        out_shape=[jax.ShapeDtypeStruct(v.shape, v.dtype) for v in held]
+        + [jax.ShapeDtypeStruct(shape, F32) for shape in packs(1)],
+        scratch_shapes=[pltpu.SemaphoreType.DMA((len(held),))],
+        compiler_params=pltpu.CompilerParams(vmem_limit_bytes=8 << 20),
+        name="start_kernel",
+    )(*[pltpu.with_memory_space_constraint(v, pltpu.HBM) for v in held])
+    q0, adjoint, rates, codes, flags, scales, mean_t, forward, mean, backward = got[: len(held)]
+    got = exchange(got[len(held) :])
+    size = functools.partial(setup_kernel, lax.axis_size("gx"), lax.axis_size("gy"))
+    lam3, *along, walls, factors, coupling = call(
+        size,
+        [adjoint, rates, codes, flags, scales, mean_t],
+        [FIELD] + packs(1) + [TABLE, TABLE, (SPECIES, SPECIES, LANES)],
+        narrow,
+    )
 
     def inner(mix, state):
         kernel = functools.partial(volume_kernel, mix)
-        return call(kernel, [coupling, state, q0, walls, forward], [FIELD, FIELD], wide + total, 1)
+        return call(kernel, [coupling, state, q0, walls, forward], [FIELD, FIELD], wide + total)
 
     def back_inner(state, lam, near):
         return call(
-            back_volume_kernel, [coupling, state, lam, near, walls, backward], [FIELD], narrow + total3, 1
+            back_volume_kernel, [coupling, state, lam, near, walls, backward], [FIELD], narrow + total3
         )[0]
 
-    def outer(section, share, state, part, got):
+    def outer(section, share, state, part, got, along=()):
         kernel = functools.partial(face_kernel, section, share, False)
         out, near_x, near_y, *sent = call(
-            kernel, [state, part, walls, factors, mean, *got], [FIELD] * 3 + packs(1), narrow
+            kernel, [state, part, walls, factors, mean, *got, *along],
+            [FIELD] * 3 + packs(2 if along else 1),
+            narrow,
         )
         return out, near_x, near_y, sent
 
     part, z0 = inner((0.0, 1.0), q0)
-    q1, x0, y0, sent = outer(0, 1.0, q0, part, got0)
-    got1 = exchange(sent)
+    q1, x0, y0, sent = outer(0, 1.0, q0, part, got)
+    got = exchange(sent)
     part, z1 = inner((0.75, 0.25), q1)
-    q2, x1, y1, sent = outer(1, 0.25, q1, part, got1)
-    got2 = exchange(sent)
+    q2, x1, y1, sent = outer(1, 0.25, q1, part, got, along)
+    got = exchange(sent)
     part, z2 = inner((1.0 / 3.0, 2.0 / 3.0), q2)
     back = back_inner(q2, lam3, z2)
     lam2, carry, x2, y2, *sent = call(
         turn_kernel,
-        [q2, lam3, back, walls, factors, mean_t, *got2, *got0],
+        [q2, lam3, back, walls, factors, mean_t, *got],
         [FIELD] * 4 + packs(1),
         narrow + work,
     )

time: 67.4 us -> 58.4 us (0.87)
  the two profiles are of different devices: /device:TPU:1 before, /device:TPU:32 now
where the time goes in v1:
time: 58.4 us; the launch traced here: 58.3 us
  starting transfers between devices  36 us (62%)
  Pallas kernels  12.4 us (21%)
  waiting for transfers between devices  9.1 us (16%)
  between operations  0.76 us (1%)
    ppermute x20, starting transfers between devices, swap(): return lax.ppermute(values, axis, moves)  36 us
    pallas_call x13, Pallas kernels, call(): pl.pallas_call(kernel, in_specs=[pl.BlockSpec(memory_space=pltpu.VMEM)] *...  11 us
    ppermute x20, waiting for transfers between devices, swap(): return lax.ppermute(values, axis, moves)  9.1 us
    pallas_call x1, Pallas kernels, per_device(): pl.pallas_call(functools.partial(start_kernel, len(held)), in_specs=[pl.B...  1.44 us
  transfers between devices with their start and end apart: 20, of which 5 were waited for; matrix products, arithmetic and copies ran while one was open for 0% of the time, Pallas kernels for 12%

profile of v1, /device:TPU:32, one launch (start us, length us, event | category | flops | bytes accessed | tf_op | source)
XLA Modules:
  0.0 58.3 jit_solution(14755168106611108438)
XLA Ops:
  0.6 1.4 %start_kernel.1 = (f32[25,16,128]{2,1,0:T(8,128)S(1)}, f32[25,16,128]{2,1,0:T(8,128)S(1)}, f32[21,21]{1,0:T(8,128)S(1)}, s32[2,1,16]{2,1,0:T(1,128)S(1)}, s32[3,...) custom-call(f32[25,16,128]{2,1,0:T(8,128)} %bitcast.5, ...), custom_call_target="tpu_custom_call" | custom-call | tf_op jit(solution)/shard_map/start_kernel/pallas_call | solution.py:534
  2.1 1.1 %collective-permute-start = (f32[7,16,128]{2,1,0:T(8,128)S(1)}, f32[7,16,128]{2,1,0:T(8,128)S(1)}, u32[]{:S(2)}, u32[]{:S(2)}) collective-permute-start(f32[7,16,128]{2,1,0:T(8,128)S(1)} %get-tuple-element.70), channel_id=1, source_target_pairs={{1,2},{2,1},{3,4},{4,3},{5,6},{6,5},{7,8},{8,7},{9,10},{10,9},{11,... | collective-permute-start | bytes 172040 | tf_op jit(solution)/shard_map/ppermute | solution.py:513
  3.2 5.6 %collective-permute-start.2 = (f32[7,16,128]{2,1,0:T(8,128)S(1)}, f32[7,16,128]{2,1,0:T(8,128)S(1)}, u32[]{:S(2)}, u32[]{:S(2)}) collective-permute-start(f32[7,16,128]{2,1,0:T(8,128)S(1)} %get-tuple-element.72), channel_id=1, source_target_pairs={{0,1},{1,0},{2,3},{3,2},{4,5},{5,4},{6,7},{7,6},{8,9},{9,8},{10,11... | collective-permute-start | bytes 172040 | tf_op jit(solution)/shard_map/ppermute | solution.py:513
  8.8 4.3 %collective-permute-start.1 = (f32[7,8,128]{2,1,0:T(8,128)S(1)}, f32[7,8,128]{2,1,0:T(8,128)S(1)}, u32[]{:S(2)}, u32[]{:S(2)}) collective-permute-start(f32[7,8,128]{2,1,0:T(8,128)S(1)} %get-tuple-element.71), channel_id=1, source_target_pairs={{32,64},{64,32},{96,128},{128,96},{160,192},{192,160},{224,0},{0,2... | collective-permute-start | bytes 86024 | tf_op jit(solution)/shard_map/ppermute | solution.py:513
  13.1 0.5 setup_kernel.1
  13.6 0.9 %volume_kernel.3 = (f32[25,16,128]{2,1,0:T(8,128)S(1)}, f32[25,16,128]{2,1,0:T(8,128)S(1)}) custom-call(f32[21,21,128]{2,1,0:T(8,128)S(1)} %get-tuple-element.64.coupling, f32[25,16,128]{2,1,0:T(8,128)S(1)} %get-tuple-element.57.state.start, f32[25,16,128]{2,1,0:T(8,128)S(1)} %get-tuple-element.57.state.start, f32[3,16,128]{2,1,0:T(8,128)S(1)} %get-tuple-element.65.walls, ...), custom_call_target="tpu_custom_call" | custom-call | tf_op jit(solution)/shard_map/volume_kernel/pallas_call | solution.py:487
  14.7 0.7 %face_kernel.3 = (f32[25,16,128]{2,1,0:T(8,128)S(1)}, f32[25,16,128]{2,1,0:T(8,128)S(1)}, f32[25,16,128]{2,1,0:T(8,128)S(1)}, f32[7,16,128]{2,1,0:T(8,128)S(1)},...) custom-call(f32[25,16,128]{2,1,0:T(8,128)S(1)} %get-tuple-element.57.state.start, ...), custom_call_target="tpu_custom_call" | custom-call | tf_op jit(solution)/shard_map/face_kernel/pallas_call | solution.py:487
  15.5 2.6 %collective-permute-start.6 = (f32[7,16,128]{2,1,0:T(8,128)S(1)}, f32[7,16,128]{2,1,0:T(8,128)S(1)}, u32[]{:S(2)}, u32[]{:S(2)}) collective-permute-start(f32[7,16,128]{2,1,0:T(8,128)S(1)} %get-tuple-element.78), channel_id=1, source_target_pairs={{0,1},{1,0},{2,3},{3,2},{4,5},{5,4},{6,7},{7,6},{8,9},{9,8},{10,11... | collective-permute-start | bytes 172040 | tf_op jit(solution)/shard_map/ppermute | solution.py:513
  18.1 3.0 %collective-permute-start.5 = (f32[7,8,128]{2,1,0:T(8,128)S(1)}, f32[7,8,128]{2,1,0:T(8,128)S(1)}, u32[]{:S(2)}, u32[]{:S(2)}) collective-permute-start(f32[7,8,128]{2,1,0:T(8,128)S(1)} %get-tuple-element.77), channel_id=1, source_target_pairs={{32,64},{64,32},{96,128},{128,96},{160,192},{192,160},{224,0},{0,2... | collective-permute-start | bytes 86024 | tf_op jit(solution)/shard_map/ppermute | solution.py:513
  21.1 0.3 collective-permute-start.7
  21.5 0.9 %volume_kernel.4 = (f32[25,16,128]{2,1,0:T(8,128)S(1)}, f32[25,16,128]{2,1,0:T(8,128)S(1)}) custom-call(f32[21,21,128]{2,1,0:T(8,128)S(1)} %get-tuple-element.64.coupling, f32[25,16,128]{2,1,0:T(8,128)S(1)} %get-tuple-element.74.state, f32[25,16,128]{2,1,0:T(8,128)S(1)} %get-tuple-element.57.state.start, f32[3,16,128]{2,1,0:T(8,128)S(1)} %get-tuple-element.65.walls, ...), custom_call_target="tpu_custom_call" | custom-call | tf_op jit(solution)/shard_map/volume_kernel/pallas_call | solution.py:487
  22.4 1.4 %collective-permute-done.5.refs_1_ = f32[7,8,128]{2,1,0:T(8,128)S(1)} collective-permute-done((f32[7,8,128]{2,1,0:T(8,128)S(1)}, f32[7,8,128]{2,1,0:T(8,128)S(1)}, u32[]{:S(2)}, u32[]{:S(2)}) %collective-permute-start.5) | collective-permute-done | bytes 28704 | tf_op jit(solution)/shard_map/ppermute | solution.py:513
  23.8 0.7 %face_kernel.4 = (f32[25,16,128]{2,1,0:T(8,128)S(1)}, f32[25,16,128]{2,1,0:T(8,128)S(1)}, f32[25,16,128]{2,1,0:T(8,128)S(1)}, f32[14,16,128]{2,1,0:T(8,128)S(1)}...) custom-call(f32[25,16,128]{2,1,0:T(8,128)S(1)} %get-tuple-element.74.state, ...), custom_call_target="tpu_custom_call" | custom-call | tf_op jit(solution)/shard_map/face_kernel/pallas_call | solution.py:487
  24.5 2.1 %collective-permute-start.8 = (f32[14,16,128]{2,1,0:T(8,128)S(1)}, f32[14,16,128]{2,1,0:T(8,128)S(1)}, u32[]{:S(2)}, u32[]{:S(2)}) collective-permute-start(f32[14,16,128]{2,1,0:T(8,128)S(1)} %get-tuple-element.89), channel_id=1, source_target_pairs={{1,2},{2,1},{3,4},{4,3},{5,6},{6,5},{7,8},{8,7},{9,10},{10,9},{11,... | collective-permute-start | bytes 344072 | tf_op jit(solution)/shard_map/ppermute | solution.py:513
  26.6 3.2 %collective-permute-start.10 = (f32[14,16,128]{2,1,0:T(8,128)S(1)}, f32[14,16,128]{2,1,0:T(8,128)S(1)}, u32[]{:S(2)}, u32[]{:S(2)}) collective-permute-start(f32[14,16,128]{2,1,0:T(8,128)S(1)} %get-tuple-element.91), channel_id=1, source_target_pairs={{0,1},{1,0},{2,3},{3,2},{4,5},{5,4},{6,7},{7,6},{8,9},{9,8},{10,11... | collective-permute-start | bytes 344072 | tf_op jit(solution)/shard_map/ppermute | solution.py:513
  29.8 1.7 %collective-permute-start.9 = (f32[14,8,128]{2,1,0:T(8,128)S(1)}, f32[14,8,128]{2,1,0:T(8,128)S(1)}, u32[]{:S(2)}, u32[]{:S(2)}) collective-permute-start(f32[14,8,128]{2,1,0:T(8,128)S(1)} %get-tuple-element.90), channel_id=1, source_target_pairs={{32,64},{64,32},{96,128},{128,96},{160,192},{192,160},{224,0},{0,2... | collective-permute-start | bytes 172040 | tf_op jit(solution)/shard_map/ppermute | solution.py:513
  31.5 0.9 %volume_kernel.5 = (f32[25,16,128]{2,1,0:T(8,128)S(1)}, f32[25,16,128]{2,1,0:T(8,128)S(1)}) custom-call(f32[21,21,128]{2,1,0:T(8,128)S(1)} %get-tuple-element.64.coupling, f32[25,16,128]{2,1,0:T(8,128)S(1)} %get-tuple-element.84.state, f32[25,16,128]{2,1,0:T(8,128)S(1)} %get-tuple-element.57.state.start, f32[3,16,128]{2,1,0:T(8,128)S(1)} %get-tuple-element.65.walls, ...), custom_call_target="tpu_custom_call" | custom-call | tf_op jit(solution)/shard_map/volume_kernel/pallas_call | solution.py:487
  32.4 0.8 %back_volume_kernel.3.inner = f32[25,16,128]{2,1,0:T(8,128)S(1)} custom-call(f32[21,21,128]{2,1,0:T(8,128)S(1)} %get-tuple-element.64.coupling, f32[25,16,128]{2,1,0:T(8,128)S(1)} %get-tuple-element.84.state, f32[25,16,128]{2,1,0:T(8,128)S(1)} %get-tuple-element.86.lam, f32[25,16,128]{2,1,0:T(8,128)S(1)} %get-tuple-element.87.near, ...), custom_call_target="tpu_custom_call" | custom-call | tf_op jit(solution)/shard_map/back_volume_kernel/pallas_call | solution.py:487
  33.3 2.2 %collective-permute-done.9.refs_1_ = f32[14,8,128]{2,1,0:T(8,128)S(1)} collective-permute-done((f32[14,8,128]{2,1,0:T(8,128)S(1)}, f32[14,8,128]{2,1,0:T(8,128)S(1)}, u32[]{:S(2)}, u32[]{:S(2)}) %collective-permute-start.9) | collective-permute-done | bytes 57376 | tf_op jit(solution)/shard_map/ppermute | solution.py:513
  35.5 1.0 %turn_kernel.1 = (f32[25,16,128]{2,1,0:T(8,128)S(1)}, f32[25,16,128]{2,1,0:T(8,128)S(1)}, f32[25,16,128]{2,1,0:T(8,128)S(1)}, f32[25,16,128]{2,1,0:T(8,128)S(1)}...) custom-call(f32[25,16,128]{2,1,0:T(8,128)S(1)} %get-tuple-element.84, ...), custom_call_target="tpu_custom_call" | custom-call | tf_op jit(solution)/shard_map/turn_kernel/pallas_call | solution.py:487
  36.6 3.9 %collective-permute-start.14 = (f32[7,16,128]{2,1,0:T(8,128)S(1)}, f32[7,16,128]{2,1,0:T(8,128)S(1)}, u32[]{:S(2)}, u32[]{:S(2)}) collective-permute-start(f32[7,16,128]{2,1,0:T(8,128)S(1)} %get-tuple-element.101), channel_id=1, source_target_pairs={{0,1},{1,0},{2,3},{3,2},{4,5},{5,4},{6,7},{7,6},{8,9},{9,8},{10,11... | collective-permute-start | bytes 172040 | tf_op jit(solution)/shard_map/ppermute | solution.py:513
  40.5 1.9 %collective-permute-start.13 = (f32[7,8,128]{2,1,0:T(8,128)S(1)}, f32[7,8,128]{2,1,0:T(8,128)S(1)}, u32[]{:S(2)}, u32[]{:S(2)}) collective-permute-start(f32[7,8,128]{2,1,0:T(8,128)S(1)} %get-tuple-element.100), channel_id=1, source_target_pairs={{32,64},{64,32},{96,128},{128,96},{160,192},{192,160},{224,0},{0,2... | collective-permute-start | bytes 86024 | tf_op jit(solution)/shard_map/ppermute | solution.py:513
  42.4 0.8 %back_volume_kernel.4.inner = f32[25,16,128]{2,1,0:T(8,128)S(1)} custom-call(f32[21,21,128]{2,1,0:T(8,128)S(1)} %get-tuple-element.64.coupling, f32[25,16,128]{2,1,0:T(8,128)S(1)} %get-tuple-element.74.state, f32[25,16,128]{2,1,0:T(8,128)S(1)} %get-tuple-element.95.lam, f32[25,16,128]{2,1,0:T(8,128)S(1)} %get-tuple-element.96.near, ...), custom_call_target="tpu_custom_call" | custom-call | tf_op jit(solution)/shard_map/back_volume_kernel/pallas_call | solution.py:487
  43.2 2.7 %collective-permute-done.13.refs_1_ = f32[7,8,128]{2,1,0:T(8,128)S(1)} collective-permute-done((f32[7,8,128]{2,1,0:T(8,128)S(1)}, f32[7,8,128]{2,1,0:T(8,128)S(1)}, u32[]{:S(2)}, u32[]{:S(2)}) %collective-permute-start.13) | collective-permute-done | bytes 28704 | tf_op jit(solution)/shard_map/ppermute | solution.py:513
  45.9 0.8 %middle_kernel.1 = (f32[25,16,128]{2,1,0:T(8,128)S(1)}, f32[7,16,128]{2,1,0:T(8,128)S(1)}, f32[7,8,128]{2,1,0:T(8,128)S(1)}, f32[7,16,128]{2,1,0:T(8,128)S(1)}, f32[7,8,128]{2,1,0:T(8,128)S(1)}) custom-call(f32[25,16,128]{2,1,0:T(8,128)S(1)} %get-tuple-element.74.state, f32[25,16,128]{2,1,0:T(8,128)S(1)} %get-tuple-element.95.lam, ...), custom_call_target="tpu_custom_call" | custom-call | tf_op jit(solution)/shard_map/middle_kernel/pallas_call | solution.py:487
  46.7 0.4 collective-permute-start.16
  47.1 4.7 %collective-permute-start.18 = (f32[7,16,128]{2,1,0:T(8,128)S(1)}, f32[7,16,128]{2,1,0:T(8,128)S(1)}, u32[]{:S(2)}, u32[]{:S(2)}) collective-permute-start(f32[7,16,128]{2,1,0:T(8,128)S(1)} %get-tuple-element.110), channel_id=1, source_target_pairs={{0,1},{1,0},{2,3},{3,2},{4,5},{5,4},{6,7},{7,6},{8,9},{9,8},{10,11... | collective-permute-start | bytes 172040 | tf_op jit(solution)/shard_map/ppermute | solution.py:513
  51.8 0.9 %collective-permute-start.17 = (f32[7,8,128]{2,1,0:T(8,128)S(1)}, f32[7,8,128]{2,1,0:T(8,128)S(1)}, u32[]{:S(2)}, u32[]{:S(2)}) collective-permute-start(f32[7,8,128]{2,1,0:T(8,128)S(1)} %get-tuple-element.109), channel_id=1, source_target_pairs={{32,64},{64,32},{96,128},{128,96},{160,192},{192,160},{224,0},{0,2... | collective-permute-start | bytes 86024 | tf_op jit(solution)/shard_map/ppermute | solution.py:513
  52.8 1.1 %face_kernel.5 = f32[25,16,128]{2,1,0:T(8,128)} custom-call(f32[25,16,128]{2,1,0:T(8,128)S(1)} %get-tuple-element.84.state, f32[25,16,128]{2,1,0:T(8,128)S(1)} %get-tuple-element.85.inner, f32[3,16,128]{2,1,0:T(8,128)S(1)} %get-tuple-element.65.walls, f32[3,16,128]{2,1,0:T(8,128)S(1)} %get-tuple-element.68.factors, ...), custom_call_target="tpu_custom_call" | custom-call | tf_op jit(solution)/shard_map/face_kernel/pallas_call | solution.py:487
  53.8 0.8 %back_volume_kernel.5.inner = f32[25,16,128]{2,1,0:T(8,128)S(1)} custom-call(f32[21,21,128]{2,1,0:T(8,128)S(1)} %get-tuple-element.64.coupling, f32[25,16,128]{2,1,0:T(8,128)S(1)} %get-tuple-element.57.state.start, f32[25,16,128]{2,1,0:T(8,128)S(1)} %get-tuple-element.103.lam, f32[25,16,128]{2,1,0:T(8,128)S(1)} %get-tuple-element.104.near, ...), custom_call_target="tpu_custom_call" | custom-call | tf_op jit(solution)/shard_map/back_volume_kernel/pallas_call | solution.py:487
  54.7 2.6 %collective-permute-done.17.lb = f32[7,8,128]{2,1,0:T(8,128)S(1)} collective-permute-done((f32[7,8,128]{2,1,0:T(8,128)S(1)}, f32[7,8,128]{2,1,0:T(8,128)S(1)}, u32[]{:S(2)}, u32[]{:S(2)}) %collective-permute-start.17) | collective-permute-done | bytes 28704 | tf_op jit(solution)/shard_map/ppermute | solution.py:513
  57.2 1.1 %end_kernel.1 = f32[25,16,128]{2,1,0:T(8,128)} custom-call(f32[25,16,128]{2,1,0:T(8,128)S(1)} %get-tuple-element.57.state.start, f32[25,16,128]{2,1,0:T(8,128)S(1)} %get-tuple-element.103.lam, f32[25,16,128]{2,1,0:T(8,128)S(1)} %back_volume_kernel.5.inner, f32[25,16,128]{2,1,0:T(8,128)S(1)} %get-tuple-element.105.near_x, ...), custom_call_target="tpu_custom_call" | custom-call | tf_op jit(solution)/shard_map/end_kernel/pallas_call | solution.py:487
  (22 shorter events, 0.4 us)
Async XLA Ops:
  2.1 12.6 %collective-permute-start = (f32[7,16,128]{2,1,0:T(8,128)S(1)}, f32[7,16,128]{2,1,0:T(8,128)S(1)}, u32[]{:S(2)}, u32[]{:S(2)}) collective-permute-start(f32[7,16,128]{2,1,0:T(8,128)S(1)} %get-tuple-element.70), channel_id=1, source_target_pairs={{1,2},{2,1},{3,4},{4,3},{5,6},{6,5},{7,8},{8,7},{9,10},{10,9},{11,... | collective-permute-start | bytes 172040 | tf_op jit(solution)/shard_map/ppermute | solution.py:513
  3.2 11.5 %collective-permute-start.2 = (f32[7,16,128]{2,1,0:T(8,128)S(1)}, f32[7,16,128]{2,1,0:T(8,128)S(1)}, u32[]{:S(2)}, u32[]{:S(2)}) collective-permute-start(f32[7,16,128]{2,1,0:T(8,128)S(1)} %get-tuple-element.72), channel_id=1, source_target_pairs={{0,1},{1,0},{2,3},{3,2},{4,5},{5,4},{6,7},{7,6},{8,9},{9,8},{10,11... | collective-permute-start | bytes 172040 | tf_op jit(solution)/shard_map/ppermute | solution.py:513
  8.8 5.8 %collective-permute-start.1 = (f32[7,8,128]{2,1,0:T(8,128)S(1)}, f32[7,8,128]{2,1,0:T(8,128)S(1)}, u32[]{:S(2)}, u32[]{:S(2)}) collective-permute-start(f32[7,8,128]{2,1,0:T(8,128)S(1)} %get-tuple-element.71), channel_id=1, source_target_pairs={{32,64},{64,32},{96,128},{128,96},{160,192},{192,160},{224,0},{0,2... | collective-permute-start | bytes 86024 | tf_op jit(solution)/shard_map/ppermute | solution.py:513
  13.1 1.6 %collective-permute-start.3 = (f32[7,8,128]{2,1,0:T(8,128)S(1)}, f32[7,8,128]{2,1,0:T(8,128)S(1)}, u32[]{:S(2)}, u32[]{:S(2)}) collective-permute-start(f32[7,8,128]{2,1,0:T(8,128)S(1)} %get-tuple-element.73), channel_id=1, source_target_pairs={{0,32},{32,0},{64,96},{96,64},{128,160},{160,128},{192,224},{224,1... | collective-permute-start | bytes 86024 | tf_op jit(solution)/shard_map/ppermute | solution.py:513
  15.4 8.4 %collective-permute-start.4 = (f32[7,16,128]{2,1,0:T(8,128)S(1)}, f32[7,16,128]{2,1,0:T(8,128)S(1)}, u32[]{:S(2)}, u32[]{:S(2)}) collective-permute-start(f32[7,16,128]{2,1,0:T(8,128)S(1)} %get-tuple-element.76), channel_id=1, source_target_pairs={{1,2},{2,1},{3,4},{4,3},{5,6},{6,5},{7,8},{8,7},{9,10},{10,9},{11,... | collective-permute-start | bytes 172040 | tf_op jit(solution)/shard_map/ppermute | solution.py:513
  15.5 8.3 %collective-permute-start.6 = (f32[7,16,128]{2,1,0:T(8,128)S(1)}, f32[7,16,128]{2,1,0:T(8,128)S(1)}, u32[]{:S(2)}, u32[]{:S(2)}) collective-permute-start(f32[7,16,128]{2,1,0:T(8,128)S(1)} %get-tuple-element.78), channel_id=1, source_target_pairs={{0,1},{1,0},{2,3},{3,2},{4,5},{5,4},{6,7},{7,6},{8,9},{9,8},{10,11... | collective-permute-start | bytes 172040 | tf_op jit(solution)/shard_map/ppermute | solution.py:513
  18.1 5.7 %collective-permute-start.5 = (f32[7,8,128]{2,1,0:T(8,128)S(1)}, f32[7,8,128]{2,1,0:T(8,128)S(1)}, u32[]{:S(2)}, u32[]{:S(2)}) collective-permute-start(f32[7,8,128]{2,1,0:T(8,128)S(1)} %get-tuple-element.77), channel_id=1, source_target_pairs={{32,64},{64,32},{96,128},{128,96},{160,192},{192,160},{224,0},{0,2... | collective-permute-start | bytes 86024 | tf_op jit(solution)/shard_map/ppermute | solution.py:513
  21.1 2.7 %collective-permute-start.7 = (f32[7,8,128]{2,1,0:T(8,128)S(1)}, f32[7,8,128]{2,1,0:T(8,128)S(1)}, u32[]{:S(2)}, u32[]{:S(2)}) collective-permute-start(f32[7,8,128]{2,1,0:T(8,128)S(1)} %get-tuple-element.79), channel_id=1, source_target_pairs={{0,32},{32,0},{64,96},{96,64},{128,160},{160,128},{192,224},{224,1... | collective-permute-start | bytes 86024 | tf_op jit(solution)/shard_map/ppermute | solution.py:513
  24.5 11.0 %collective-permute-start.8 = (f32[14,16,128]{2,1,0:T(8,128)S(1)}, f32[14,16,128]{2,1,0:T(8,128)S(1)}, u32[]{:S(2)}, u32[]{:S(2)}) collective-permute-start(f32[14,16,128]{2,1,0:T(8,128)S(1)} %get-tuple-element.89), channel_id=1, source_target_pairs={{1,2},{2,1},{3,4},{4,3},{5,6},{6,5},{7,8},{8,7},{9,10},{10,9},{11,... | collective-permute-start | bytes 344072 | tf_op jit(solution)/shard_map/ppermute | solution.py:513
  26.6 8.9 %collective-permute-start.10 = (f32[14,16,128]{2,1,0:T(8,128)S(1)}, f32[14,16,128]{2,1,0:T(8,128)S(1)}, u32[]{:S(2)}, u32[]{:S(2)}) collective-permute-start(f32[14,16,128]{2,1,0:T(8,128)S(1)} %get-tuple-element.91), channel_id=1, source_target_pairs={{0,1},{1,0},{2,3},{3,2},{4,5},{5,4},{6,7},{7,6},{8,9},{9,8},{10,11... | collective-permute-start | bytes 344072 | tf_op jit(solution)/shard_map/ppermute | solution.py:513
  29.8 5.7 %collective-permute-start.9 = (f32[14,8,128]{2,1,0:T(8,128)S(1)}, f32[14,8,128]{2,1,0:T(8,128)S(1)}, u32[]{:S(2)}, u32[]{:S(2)}) collective-permute-start(f32[14,8,128]{2,1,0:T(8,128)S(1)} %get-tuple-element.90), channel_id=1, source_target_pairs={{32,64},{64,32},{96,128},{128,96},{160,192},{192,160},{224,0},{0,2... | collective-permute-start | bytes 172040 | tf_op jit(solution)/shard_map/ppermute | solution.py:513
  31.5 4.0 %collective-permute-start.11 = (f32[14,8,128]{2,1,0:T(8,128)S(1)}, f32[14,8,128]{2,1,0:T(8,128)S(1)}, u32[]{:S(2)}, u32[]{:S(2)}) collective-permute-start(f32[14,8,128]{2,1,0:T(8,128)S(1)} %get-tuple-element.92), channel_id=1, source_target_pairs={{0,32},{32,0},{64,96},{96,64},{128,160},{160,128},{192,224},{224,1... | collective-permute-start | bytes 172040 | tf_op jit(solution)/shard_map/ppermute | solution.py:513
  36.5 9.4 %collective-permute-start.12 = (f32[7,16,128]{2,1,0:T(8,128)S(1)}, f32[7,16,128]{2,1,0:T(8,128)S(1)}, u32[]{:S(2)}, u32[]{:S(2)}) collective-permute-start(f32[7,16,128]{2,1,0:T(8,128)S(1)} %get-tuple-element.99), channel_id=1, source_target_pairs={{1,2},{2,1},{3,4},{4,3},{5,6},{6,5},{7,8},{8,7},{9,10},{10,9},{11,... | collective-permute-start | bytes 172040 | tf_op jit(solution)/shard_map/ppermute | solution.py:513
  36.6 9.3 %collective-permute-start.14 = (f32[7,16,128]{2,1,0:T(8,128)S(1)}, f32[7,16,128]{2,1,0:T(8,128)S(1)}, u32[]{:S(2)}, u32[]{:S(2)}) collective-permute-start(f32[7,16,128]{2,1,0:T(8,128)S(1)} %get-tuple-element.101), channel_id=1, source_target_pairs={{0,1},{1,0},{2,3},{3,2},{4,5},{5,4},{6,7},{7,6},{8,9},{9,8},{10,11... | collective-permute-start | bytes 172040 | tf_op jit(solution)/shard_map/ppermute | solution.py:513
  40.5 5.4 %collective-permute-start.13 = (f32[7,8,128]{2,1,0:T(8,128)S(1)}, f32[7,8,128]{2,1,0:T(8,128)S(1)}, u32[]{:S(2)}, u32[]{:S(2)}) collective-permute-start(f32[7,8,128]{2,1,0:T(8,128)S(1)} %get-tuple-element.100), channel_id=1, source_target_pairs={{32,64},{64,32},{96,128},{128,96},{160,192},{192,160},{224,0},{0,2... | collective-permute-start | bytes 86024 | tf_op jit(solution)/shard_map/ppermute | solution.py:513
  42.4 3.6 %collective-permute-start.15 = (f32[7,8,128]{2,1,0:T(8,128)S(1)}, f32[7,8,128]{2,1,0:T(8,128)S(1)}, u32[]{:S(2)}, u32[]{:S(2)}) collective-permute-start(f32[7,8,128]{2,1,0:T(8,128)S(1)} %get-tuple-element.102), channel_id=1, source_target_pairs={{0,32},{32,0},{64,96},{96,64},{128,160},{160,128},{192,224},{224,1... | collective-permute-start | bytes 86024 | tf_op jit(solution)/shard_map/ppermute | solution.py:513
  46.7 10.5 %collective-permute-start.16 = (f32[7,16,128]{2,1,0:T(8,128)S(1)}, f32[7,16,128]{2,1,0:T(8,128)S(1)}, u32[]{:S(2)}, u32[]{:S(2)}) collective-permute-start(f32[7,16,128]{2,1,0:T(8,128)S(1)} %get-tuple-element.108), channel_id=1, source_target_pairs={{1,2},{2,1},{3,4},{4,3},{5,6},{6,5},{7,8},{8,7},{9,10},{10,9},{11,... | collective-permute-start | bytes 172040 | tf_op jit(solution)/shard_map/ppermute | solution.py:513
  47.1 10.1 %collective-permute-start.18 = (f32[7,16,128]{2,1,0:T(8,128)S(1)}, f32[7,16,128]{2,1,0:T(8,128)S(1)}, u32[]{:S(2)}, u32[]{:S(2)}) collective-permute-start(f32[7,16,128]{2,1,0:T(8,128)S(1)} %get-tuple-element.110), channel_id=1, source_target_pairs={{0,1},{1,0},{2,3},{3,2},{4,5},{5,4},{6,7},{7,6},{8,9},{9,8},{10,11... | collective-permute-start | bytes 172040 | tf_op jit(solution)/shard_map/ppermute | solution.py:513
  51.8 5.4 %collective-permute-start.17 = (f32[7,8,128]{2,1,0:T(8,128)S(1)}, f32[7,8,128]{2,1,0:T(8,128)S(1)}, u32[]{:S(2)}, u32[]{:S(2)}) collective-permute-start(f32[7,8,128]{2,1,0:T(8,128)S(1)} %get-tuple-element.109), channel_id=1, source_target_pairs={{32,64},{64,32},{96,128},{128,96},{160,192},{192,160},{224,0},{0,2... | collective-permute-start | bytes 86024 | tf_op jit(solution)/shard_map/ppermute | solution.py:513
  52.8 4.5 %collective-permute-start.19 = (f32[7,8,128]{2,1,0:T(8,128)S(1)}, f32[7,8,128]{2,1,0:T(8,128)S(1)}, u32[]{:S(2)}, u32[]{:S(2)}) collective-permute-start(f32[7,8,128]{2,1,0:T(8,128)S(1)} %get-tuple-element.111), channel_id=1, source_target_pairs={{0,32},{32,0},{64,96},{96,64},{128,160},{160,128},{192,224},{224,1... | collective-permute-start | bytes 86024 | tf_op jit(solution)/shard_map/ppermute | solution.py:513

commit v2 on v1

--- a/solution.py
+++ b/solution.py
@@ -504,19 +504,28 @@
 
 
 def exchange(sent):
-    def swap(values, axis, first):
-        count = lax.axis_size(axis)
+    columns, lines = lax.axis_size("gx"), lax.axis_size("gy")
+
+    def swap(values, along_x, first):
         moves = []
-        for low in range(first, count + first, 2):
-            a, b = low % count, (low + 1) % count
-            moves += [(a, b), (b, a)]
-        return lax.ppermute(values, axis, moves)
+        for x in range(columns):
+            for y in range(lines):
+                at, count, other = (x, columns, y) if along_x else (y, lines, x)
+                if at % 2 == first:
+                    mate, across = at + 1, other
+                else:
+                    mate, across = at - 1, other
+                if mate < 0 or mate >= count:
+                    mate, across = at, other ^ 1
+                to = (mate, across) if along_x else (across, mate)
+                moves.append((x * lines + y, to[0] * lines + to[1]))
+        return lax.ppermute(values, ("gx", "gy"), moves)
 
     yb, xb, ya, xa = sent
-    yb = swap(yb, "gy", 1)
-    xb = swap(xb, "gx", 1)
-    ya = swap(ya, "gy", 0)
-    xa = swap(xa, "gx", 0)
+    yb = swap(yb, False, 1)
+    xb = swap(xb, True, 1)
+    ya = swap(ya, False, 0)
+    xa = swap(xa, True, 0)
     return [yb, xb, ya, xa]
 
 

time: 58.4 us -> 51.4 us (0.88)
  the two profiles are of different devices: /device:TPU:32 before, /device:TPU:89 now
where the time goes in v2:
time: 51.4 us; the launch traced here: 51.3 us
  starting transfers between devices  33.2 us (65%)
  Pallas kernels  12.4 us (24%)
  waiting for transfers between devices  4.93 us (10%)
  between operations  0.74 us (1%)
    ppermute x20, starting transfers between devices, swap(): return lax.ppermute(values, ('gx', 'gy'), moves)  33.2 us
    pallas_call x13, Pallas kernels, call(): pl.pallas_call(kernel, in_specs=[pl.BlockSpec(memory_space=pltpu.VMEM)] *...  11 us
    ppermute x20, waiting for transfers between devices, swap(): return lax.ppermute(values, ('gx', 'gy'), moves)  4.93 us
    pallas_call x1, Pallas kernels, per_device(): pl.pallas_call(functools.partial(start_kernel, len(held)), in_specs=[pl.B...  1.44 us
  transfers between devices with their start and end apart: 20, of which 5 were waited for; matrix products, arithmetic and copies ran while one was open for 0% of the time, Pallas kernels for 13%

profile of v2, /device:TPU:89, one launch (start us, length us, event | category | flops | bytes accessed | tf_op | source)
XLA Modules:
  0.0 51.3 jit_solution(2992128978036680513)
XLA Ops:
  0.6 1.4 %start_kernel.1 = (f32[25,16,128]{2,1,0:T(8,128)S(1)}, f32[25,16,128]{2,1,0:T(8,128)S(1)}, f32[21,21]{1,0:T(8,128)S(1)}, s32[2,1,16]{2,1,0:T(1,128)S(1)}, s32[3,...) custom-call(f32[25,16,128]{2,1,0:T(8,128)} %bitcast.5, ...), custom_call_target="tpu_custom_call" | custom-call | tf_op jit(solution)/shard_map/start_kernel/pallas_call | solution.py:543
  2.1 4.1 %collective-permute-start = (f32[7,16,128]{2,1,0:T(8,128)S(1)}, f32[7,16,128]{2,1,0:T(8,128)S(1)}, u32[]{:S(2)}, u32[]{:S(2)}) collective-permute-start(f32[7,16,128]{2,1,0:T(8,128)S(1)} %get-tuple-element.70), channel_id=1, source_target_pairs={{0,32},{1,2},{2,1},{3,4},{4,3},{5,6},{6,5},{7,8},{8,7},{9,10},{10,... | collective-permute-start | bytes 172040 | tf_op jit(solution)/shard_map/ppermute | solution.py:522
  6.2 4.1 %collective-permute-start.1 = (f32[7,8,128]{2,1,0:T(8,128)S(1)}, f32[7,8,128]{2,1,0:T(8,128)S(1)}, u32[]{:S(2)}, u32[]{:S(2)}) collective-permute-start(f32[7,8,128]{2,1,0:T(8,128)S(1)} %get-tuple-element.71), channel_id=1, source_target_pairs={{0,1},{1,0},{2,3},{3,2},{4,5},{5,4},{6,7},{7,6},{8,9},{9,8},{10,11... | collective-permute-start | bytes 86024 | tf_op jit(solution)/shard_map/ppermute | solution.py:522
  10.3 0.0 collective-permute-start.3
  10.3 0.5 setup_kernel.1
  10.8 0.9 %volume_kernel.3 = (f32[25,16,128]{2,1,0:T(8,128)S(1)}, f32[25,16,128]{2,1,0:T(8,128)S(1)}) custom-call(f32[21,21,128]{2,1,0:T(8,128)S(1)} %get-tuple-element.64.coupling, f32[25,16,128]{2,1,0:T(8,128)S(1)} %get-tuple-element.57.state.start, f32[25,16,128]{2,1,0:T(8,128)S(1)} %get-tuple-element.57.state.start, f32[3,16,128]{2,1,0:T(8,128)S(1)} %get-tuple-element.65.walls, ...), custom_call_target="tpu_custom_call" | custom-call | tf_op jit(solution)/shard_map/volume_kernel/pallas_call | solution.py:487
  11.7 0.2 collective-permute-done.1.refs_1_
  11.9 0.7 %face_kernel.3 = (f32[25,16,128]{2,1,0:T(8,128)S(1)}, f32[25,16,128]{2,1,0:T(8,128)S(1)}, f32[25,16,128]{2,1,0:T(8,128)S(1)}, f32[7,16,128]{2,1,0:T(8,128)S(1)},...) custom-call(f32[25,16,128]{2,1,0:T(8,128)S(1)} %get-tuple-element.57.state.start, ...), custom_call_target="tpu_custom_call" | custom-call | tf_op jit(solution)/shard_map/face_kernel/pallas_call | solution.py:487
  12.6 2.8 %collective-permute-start.4 = (f32[7,16,128]{2,1,0:T(8,128)S(1)}, f32[7,16,128]{2,1,0:T(8,128)S(1)}, u32[]{:S(2)}, u32[]{:S(2)}) collective-permute-start(f32[7,16,128]{2,1,0:T(8,128)S(1)} %get-tuple-element.76), channel_id=1, source_target_pairs={{0,32},{1,2},{2,1},{3,4},{4,3},{5,6},{6,5},{7,8},{8,7},{9,10},{10,... | collective-permute-start | bytes 172040 | tf_op jit(solution)/shard_map/ppermute | solution.py:522
  15.4 0.1 collective-permute-start.6
  15.4 3.6 %collective-permute-start.5 = (f32[7,8,128]{2,1,0:T(8,128)S(1)}, f32[7,8,128]{2,1,0:T(8,128)S(1)}, u32[]{:S(2)}, u32[]{:S(2)}) collective-permute-start(f32[7,8,128]{2,1,0:T(8,128)S(1)} %get-tuple-element.77), channel_id=1, source_target_pairs={{0,1},{1,0},{2,3},{3,2},{4,5},{5,4},{6,7},{7,6},{8,9},{9,8},{10,11... | collective-permute-start | bytes 86024 | tf_op jit(solution)/shard_map/ppermute | solution.py:522
  19.0 0.9 %volume_kernel.4 = (f32[25,16,128]{2,1,0:T(8,128)S(1)}, f32[25,16,128]{2,1,0:T(8,128)S(1)}) custom-call(f32[21,21,128]{2,1,0:T(8,128)S(1)} %get-tuple-element.64.coupling, f32[25,16,128]{2,1,0:T(8,128)S(1)} %get-tuple-element.74.state, f32[25,16,128]{2,1,0:T(8,128)S(1)} %get-tuple-element.57.state.start, f32[3,16,128]{2,1,0:T(8,128)S(1)} %get-tuple-element.65.walls, ...), custom_call_target="tpu_custom_call" | custom-call | tf_op jit(solution)/shard_map/volume_kernel/pallas_call | solution.py:487
  20.0 0.9 %collective-permute-done.5.refs_1_ = f32[7,8,128]{2,1,0:T(8,128)S(1)} collective-permute-done((f32[7,8,128]{2,1,0:T(8,128)S(1)}, f32[7,8,128]{2,1,0:T(8,128)S(1)}, u32[]{:S(2)}, u32[]{:S(2)}) %collective-permute-start.5) | collective-permute-done | bytes 28704 | tf_op jit(solution)/shard_map/ppermute | solution.py:522
  20.9 0.7 %face_kernel.4 = (f32[25,16,128]{2,1,0:T(8,128)S(1)}, f32[25,16,128]{2,1,0:T(8,128)S(1)}, f32[25,16,128]{2,1,0:T(8,128)S(1)}, f32[14,16,128]{2,1,0:T(8,128)S(1)}...) custom-call(f32[25,16,128]{2,1,0:T(8,128)S(1)} %get-tuple-element.74.state, ...), custom_call_target="tpu_custom_call" | custom-call | tf_op jit(solution)/shard_map/face_kernel/pallas_call | solution.py:487
  21.5 3.6 %collective-permute-start.8 = (f32[14,16,128]{2,1,0:T(8,128)S(1)}, f32[14,16,128]{2,1,0:T(8,128)S(1)}, u32[]{:S(2)}, u32[]{:S(2)}) collective-permute-start(f32[14,16,128]{2,1,0:T(8,128)S(1)} %get-tuple-element.89), channel_id=1, source_target_pairs={{0,32},{1,2},{2,1},{3,4},{4,3},{5,6},{6,5},{7,8},{8,7},{9,10},{10,... | collective-permute-start | bytes 344072 | tf_op jit(solution)/shard_map/ppermute | solution.py:522
  25.2 2.7 %collective-permute-start.9 = (f32[14,8,128]{2,1,0:T(8,128)S(1)}, f32[14,8,128]{2,1,0:T(8,128)S(1)}, u32[]{:S(2)}, u32[]{:S(2)}) collective-permute-start(f32[14,8,128]{2,1,0:T(8,128)S(1)} %get-tuple-element.90), channel_id=1, source_target_pairs={{0,1},{1,0},{2,3},{3,2},{4,5},{5,4},{6,7},{7,6},{8,9},{9,8},{10,11... | collective-permute-start | bytes 172040 | tf_op jit(solution)/shard_map/ppermute | solution.py:522
  27.9 0.0 collective-permute-start.11
  27.9 0.9 %volume_kernel.5 = (f32[25,16,128]{2,1,0:T(8,128)S(1)}, f32[25,16,128]{2,1,0:T(8,128)S(1)}) custom-call(f32[21,21,128]{2,1,0:T(8,128)S(1)} %get-tuple-element.64.coupling, f32[25,16,128]{2,1,0:T(8,128)S(1)} %get-tuple-element.84.state, f32[25,16,128]{2,1,0:T(8,128)S(1)} %get-tuple-element.57.state.start, f32[3,16,128]{2,1,0:T(8,128)S(1)} %get-tuple-element.65.walls, ...), custom_call_target="tpu_custom_call" | custom-call | tf_op jit(solution)/shard_map/volume_kernel/pallas_call | solution.py:487
  28.8 0.8 %back_volume_kernel.3.inner = f32[25,16,128]{2,1,0:T(8,128)S(1)} custom-call(f32[21,21,128]{2,1,0:T(8,128)S(1)} %get-tuple-element.64.coupling, f32[25,16,128]{2,1,0:T(8,128)S(1)} %get-tuple-element.84.state, f32[25,16,128]{2,1,0:T(8,128)S(1)} %get-tuple-element.86.lam, f32[25,16,128]{2,1,0:T(8,128)S(1)} %get-tuple-element.87.near, ...), custom_call_target="tpu_custom_call" | custom-call | tf_op jit(solution)/shard_map/back_volume_kernel/pallas_call | solution.py:487
  29.7 1.3 %collective-permute-done.9.refs_1_ = f32[14,8,128]{2,1,0:T(8,128)S(1)} collective-permute-done((f32[14,8,128]{2,1,0:T(8,128)S(1)}, f32[14,8,128]{2,1,0:T(8,128)S(1)}, u32[]{:S(2)}, u32[]{:S(2)}) %collective-permute-start.9) | collective-permute-done | bytes 57376 | tf_op jit(solution)/shard_map/ppermute | solution.py:522
  31.0 1.0 %turn_kernel.1 = (f32[25,16,128]{2,1,0:T(8,128)S(1)}, f32[25,16,128]{2,1,0:T(8,128)S(1)}, f32[25,16,128]{2,1,0:T(8,128)S(1)}, f32[25,16,128]{2,1,0:T(8,128)S(1)}...) custom-call(f32[25,16,128]{2,1,0:T(8,128)S(1)} %get-tuple-element.84, ...), custom_call_target="tpu_custom_call" | custom-call | tf_op jit(solution)/shard_map/turn_kernel/pallas_call | solution.py:487
  31.9 4.1 %collective-permute-start.12 = (f32[7,16,128]{2,1,0:T(8,128)S(1)}, f32[7,16,128]{2,1,0:T(8,128)S(1)}, u32[]{:S(2)}, u32[]{:S(2)}) collective-permute-start(f32[7,16,128]{2,1,0:T(8,128)S(1)} %get-tuple-element.99), channel_id=1, source_target_pairs={{0,32},{1,2},{2,1},{3,4},{4,3},{5,6},{6,5},{7,8},{8,7},{9,10},{10,... | collective-permute-start | bytes 172040 | tf_op jit(solution)/shard_map/ppermute | solution.py:522
  36.0 2.5 %collective-permute-start.13 = (f32[7,8,128]{2,1,0:T(8,128)S(1)}, f32[7,8,128]{2,1,0:T(8,128)S(1)}, u32[]{:S(2)}, u32[]{:S(2)}) collective-permute-start(f32[7,8,128]{2,1,0:T(8,128)S(1)} %get-tuple-element.100), channel_id=1, source_target_pairs={{0,1},{1,0},{2,3},{3,2},{4,5},{5,4},{6,7},{7,6},{8,9},{9,8},{10,11... | collective-permute-start | bytes 86024 | tf_op jit(solution)/shard_map/ppermute | solution.py:522
  38.5 0.8 %back_volume_kernel.4.inner = f32[25,16,128]{2,1,0:T(8,128)S(1)} custom-call(f32[21,21,128]{2,1,0:T(8,128)S(1)} %get-tuple-element.64.coupling, f32[25,16,128]{2,1,0:T(8,128)S(1)} %get-tuple-element.74.state, f32[25,16,128]{2,1,0:T(8,128)S(1)} %get-tuple-element.95.lam, f32[25,16,128]{2,1,0:T(8,128)S(1)} %get-tuple-element.96.near, ...), custom_call_target="tpu_custom_call" | custom-call | tf_op jit(solution)/shard_map/back_volume_kernel/pallas_call | solution.py:487
  39.4 2.0 %collective-permute-done.13.refs_1_ = f32[7,8,128]{2,1,0:T(8,128)S(1)} collective-permute-done((f32[7,8,128]{2,1,0:T(8,128)S(1)}, f32[7,8,128]{2,1,0:T(8,128)S(1)}, u32[]{:S(2)}, u32[]{:S(2)}) %collective-permute-start.13) | collective-permute-done | bytes 28704 | tf_op jit(solution)/shard_map/ppermute | solution.py:522
  41.4 0.8 %middle_kernel.1 = (f32[25,16,128]{2,1,0:T(8,128)S(1)}, f32[7,16,128]{2,1,0:T(8,128)S(1)}, f32[7,8,128]{2,1,0:T(8,128)S(1)}, f32[7,16,128]{2,1,0:T(8,128)S(1)}, f32[7,8,128]{2,1,0:T(8,128)S(1)}) custom-call(f32[25,16,128]{2,1,0:T(8,128)S(1)} %get-tuple-element.74.state, f32[25,16,128]{2,1,0:T(8,128)S(1)} %get-tuple-element.95.lam, ...), custom_call_target="tpu_custom_call" | custom-call | tf_op jit(solution)/shard_map/middle_kernel/pallas_call | solution.py:487
  42.2 2.6 %collective-permute-start.16 = (f32[7,16,128]{2,1,0:T(8,128)S(1)}, f32[7,16,128]{2,1,0:T(8,128)S(1)}, u32[]{:S(2)}, u32[]{:S(2)}) collective-permute-start(f32[7,16,128]{2,1,0:T(8,128)S(1)} %get-tuple-element.108), channel_id=1, source_target_pairs={{0,32},{1,2},{2,1},{3,4},{4,3},{5,6},{6,5},{7,8},{8,7},{9,10},{10,... | collective-permute-start | bytes 172040 | tf_op jit(solution)/shard_map/ppermute | solution.py:522
  44.8 2.9 %collective-permute-start.17 = (f32[7,8,128]{2,1,0:T(8,128)S(1)}, f32[7,8,128]{2,1,0:T(8,128)S(1)}, u32[]{:S(2)}, u32[]{:S(2)}) collective-permute-start(f32[7,8,128]{2,1,0:T(8,128)S(1)} %get-tuple-element.109), channel_id=1, source_target_pairs={{0,1},{1,0},{2,3},{3,2},{4,5},{5,4},{6,7},{7,6},{8,9},{9,8},{10,11... | collective-permute-start | bytes 86024 | tf_op jit(solution)/shard_map/ppermute | solution.py:522
  47.8 1.1 %face_kernel.5 = f32[25,16,128]{2,1,0:T(8,128)} custom-call(f32[25,16,128]{2,1,0:T(8,128)S(1)} %get-tuple-element.84.state, f32[25,16,128]{2,1,0:T(8,128)S(1)} %get-tuple-element.85.inner, f32[3,16,128]{2,1,0:T(8,128)S(1)} %get-tuple-element.65.walls, f32[3,16,128]{2,1,0:T(8,128)S(1)} %get-tuple-element.68.factors, ...), custom_call_target="tpu_custom_call" | custom-call | tf_op jit(solution)/shard_map/face_kernel/pallas_call | solution.py:487
  48.8 0.8 %back_volume_kernel.5.inner = f32[25,16,128]{2,1,0:T(8,128)S(1)} custom-call(f32[21,21,128]{2,1,0:T(8,128)S(1)} %get-tuple-element.64.coupling, f32[25,16,128]{2,1,0:T(8,128)S(1)} %get-tuple-element.57.state.start, f32[25,16,128]{2,1,0:T(8,128)S(1)} %get-tuple-element.103.lam, f32[25,16,128]{2,1,0:T(8,128)S(1)} %get-tuple-element.104.near, ...), custom_call_target="tpu_custom_call" | custom-call | tf_op jit(solution)/shard_map/back_volume_kernel/pallas_call | solution.py:487
  49.7 0.6 %collective-permute-done.17.lb = f32[7,8,128]{2,1,0:T(8,128)S(1)} collective-permute-done((f32[7,8,128]{2,1,0:T(8,128)S(1)}, f32[7,8,128]{2,1,0:T(8,128)S(1)}, u32[]{:S(2)}, u32[]{:S(2)}) %collective-permute-start.17) | collective-permute-done | bytes 28704 | tf_op jit(solution)/shard_map/ppermute | solution.py:522
  50.2 1.1 %end_kernel.1 = f32[25,16,128]{2,1,0:T(8,128)} custom-call(f32[25,16,128]{2,1,0:T(8,128)S(1)} %get-tuple-element.57.state.start, f32[25,16,128]{2,1,0:T(8,128)S(1)} %get-tuple-element.103.lam, f32[25,16,128]{2,1,0:T(8,128)S(1)} %back_volume_kernel.5.inner, f32[25,16,128]{2,1,0:T(8,128)S(1)} %get-tuple-element.105.near_x, ...), custom_call_target="tpu_custom_call" | custom-call | tf_op jit(solution)/shard_map/end_kernel/pallas_call | solution.py:487
  (22 shorter events, 0.1 us)
Async XLA Ops:
  2.1 9.8 %collective-permute-start = (f32[7,16,128]{2,1,0:T(8,128)S(1)}, f32[7,16,128]{2,1,0:T(8,128)S(1)}, u32[]{:S(2)}, u32[]{:S(2)}) collective-permute-start(f32[7,16,128]{2,1,0:T(8,128)S(1)} %get-tuple-element.70), channel_id=1, source_target_pairs={{0,32},{1,2},{2,1},{3,4},{4,3},{5,6},{6,5},{7,8},{8,7},{9,10},{10,... | collective-permute-start | bytes 172040 | tf_op jit(solution)/shard_map/ppermute | solution.py:522
  6.2 5.7 %collective-permute-start.2 = (f32[7,16,128]{2,1,0:T(8,128)S(1)}, f32[7,16,128]{2,1,0:T(8,128)S(1)}, u32[]{:S(2)}, u32[]{:S(2)}) collective-permute-start(f32[7,16,128]{2,1,0:T(8,128)S(1)} %get-tuple-element.72), channel_id=1, source_target_pairs={{0,1},{1,0},{2,3},{3,2},{4,5},{5,4},{6,7},{7,6},{8,9},{9,8},{10,11... | collective-permute-start | bytes 172040 | tf_op jit(solution)/shard_map/ppermute | solution.py:522
  6.2 5.7 %collective-permute-start.1 = (f32[7,8,128]{2,1,0:T(8,128)S(1)}, f32[7,8,128]{2,1,0:T(8,128)S(1)}, u32[]{:S(2)}, u32[]{:S(2)}) collective-permute-start(f32[7,8,128]{2,1,0:T(8,128)S(1)} %get-tuple-element.71), channel_id=1, source_target_pairs={{0,1},{1,0},{2,3},{3,2},{4,5},{5,4},{6,7},{7,6},{8,9},{9,8},{10,11... | collective-permute-start | bytes 86024 | tf_op jit(solution)/shard_map/ppermute | solution.py:522
  10.3 1.6 %collective-permute-start.3 = (f32[7,8,128]{2,1,0:T(8,128)S(1)}, f32[7,8,128]{2,1,0:T(8,128)S(1)}, u32[]{:S(2)}, u32[]{:S(2)}) collective-permute-start(f32[7,8,128]{2,1,0:T(8,128)S(1)} %get-tuple-element.73), channel_id=1, source_target_pairs={{0,32},{1,33},{2,34},{3,35},{4,36},{5,37},{6,38},{7,39},{8,40},{9,... | collective-permute-start | bytes 86024 | tf_op jit(solution)/shard_map/ppermute | solution.py:522
  12.6 8.3 %collective-permute-start.4 = (f32[7,16,128]{2,1,0:T(8,128)S(1)}, f32[7,16,128]{2,1,0:T(8,128)S(1)}, u32[]{:S(2)}, u32[]{:S(2)}) collective-permute-start(f32[7,16,128]{2,1,0:T(8,128)S(1)} %get-tuple-element.76), channel_id=1, source_target_pairs={{0,32},{1,2},{2,1},{3,4},{4,3},{5,6},{6,5},{7,8},{8,7},{9,10},{10,... | collective-permute-start | bytes 172040 | tf_op jit(solution)/shard_map/ppermute | solution.py:522
  15.4 5.5 %collective-permute-start.6 = (f32[7,16,128]{2,1,0:T(8,128)S(1)}, f32[7,16,128]{2,1,0:T(8,128)S(1)}, u32[]{:S(2)}, u32[]{:S(2)}) collective-permute-start(f32[7,16,128]{2,1,0:T(8,128)S(1)} %get-tuple-element.78), channel_id=1, source_target_pairs={{0,1},{1,0},{2,3},{3,2},{4,5},{5,4},{6,7},{7,6},{8,9},{9,8},{10,11... | collective-permute-start | bytes 172040 | tf_op jit(solution)/shard_map/ppermute | solution.py:522
  15.4 5.4 %collective-permute-start.5 = (f32[7,8,128]{2,1,0:T(8,128)S(1)}, f32[7,8,128]{2,1,0:T(8,128)S(1)}, u32[]{:S(2)}, u32[]{:S(2)}) collective-permute-start(f32[7,8,128]{2,1,0:T(8,128)S(1)} %get-tuple-element.77), channel_id=1, source_target_pairs={{0,1},{1,0},{2,3},{3,2},{4,5},{5,4},{6,7},{7,6},{8,9},{9,8},{10,11... | collective-permute-start | bytes 86024 | tf_op jit(solution)/shard_map/ppermute | solution.py:522
  19.0 1.8 %collective-permute-start.7 = (f32[7,8,128]{2,1,0:T(8,128)S(1)}, f32[7,8,128]{2,1,0:T(8,128)S(1)}, u32[]{:S(2)}, u32[]{:S(2)}) collective-permute-start(f32[7,8,128]{2,1,0:T(8,128)S(1)} %get-tuple-element.79), channel_id=1, source_target_pairs={{0,32},{1,33},{2,34},{3,35},{4,36},{5,37},{6,38},{7,39},{8,40},{9,... | collective-permute-start | bytes 86024 | tf_op jit(solution)/shard_map/ppermute | solution.py:522
  21.5 9.4 %collective-permute-start.8 = (f32[14,16,128]{2,1,0:T(8,128)S(1)}, f32[14,16,128]{2,1,0:T(8,128)S(1)}, u32[]{:S(2)}, u32[]{:S(2)}) collective-permute-start(f32[14,16,128]{2,1,0:T(8,128)S(1)} %get-tuple-element.89), channel_id=1, source_target_pairs={{0,32},{1,2},{2,1},{3,4},{4,3},{5,6},{6,5},{7,8},{8,7},{9,10},{10,... | collective-permute-start | bytes 344072 | tf_op jit(solution)/shard_map/ppermute | solution.py:522
  25.2 5.8 %collective-permute-start.10 = (f32[14,16,128]{2,1,0:T(8,128)S(1)}, f32[14,16,128]{2,1,0:T(8,128)S(1)}, u32[]{:S(2)}, u32[]{:S(2)}) collective-permute-start(f32[14,16,128]{2,1,0:T(8,128)S(1)} %get-tuple-element.91), channel_id=1, source_target_pairs={{0,1},{1,0},{2,3},{3,2},{4,5},{5,4},{6,7},{7,6},{8,9},{9,8},{10,11... | collective-permute-start | bytes 344072 | tf_op jit(solution)/shard_map/ppermute | solution.py:522
  25.2 5.8 %collective-permute-start.9 = (f32[14,8,128]{2,1,0:T(8,128)S(1)}, f32[14,8,128]{2,1,0:T(8,128)S(1)}, u32[]{:S(2)}, u32[]{:S(2)}) collective-permute-start(f32[14,8,128]{2,1,0:T(8,128)S(1)} %get-tuple-element.90), channel_id=1, source_target_pairs={{0,1},{1,0},{2,3},{3,2},{4,5},{5,4},{6,7},{7,6},{8,9},{9,8},{10,11... | collective-permute-start | bytes 172040 | tf_op jit(solution)/shard_map/ppermute | solution.py:522
  27.9 3.1 %collective-permute-start.11 = (f32[14,8,128]{2,1,0:T(8,128)S(1)}, f32[14,8,128]{2,1,0:T(8,128)S(1)}, u32[]{:S(2)}, u32[]{:S(2)}) collective-permute-start(f32[14,8,128]{2,1,0:T(8,128)S(1)} %get-tuple-element.92), channel_id=1, source_target_pairs={{0,32},{1,33},{2,34},{3,35},{4,36},{5,37},{6,38},{7,39},{8,40},{9,... | collective-permute-start | bytes 172040 | tf_op jit(solution)/shard_map/ppermute | solution.py:522
  31.9 9.5 %collective-permute-start.12 = (f32[7,16,128]{2,1,0:T(8,128)S(1)}, f32[7,16,128]{2,1,0:T(8,128)S(1)}, u32[]{:S(2)}, u32[]{:S(2)}) collective-permute-start(f32[7,16,128]{2,1,0:T(8,128)S(1)} %get-tuple-element.99), channel_id=1, source_target_pairs={{0,32},{1,2},{2,1},{3,4},{4,3},{5,6},{6,5},{7,8},{8,7},{9,10},{10,... | collective-permute-start | bytes 172040 | tf_op jit(solution)/shard_map/ppermute | solution.py:522
  36.0 5.4 %collective-permute-start.14 = (f32[7,16,128]{2,1,0:T(8,128)S(1)}, f32[7,16,128]{2,1,0:T(8,128)S(1)}, u32[]{:S(2)}, u32[]{:S(2)}) collective-permute-start(f32[7,16,128]{2,1,0:T(8,128)S(1)} %get-tuple-element.101), channel_id=1, source_target_pairs={{0,1},{1,0},{2,3},{3,2},{4,5},{5,4},{6,7},{7,6},{8,9},{9,8},{10,11... | collective-permute-start | bytes 172040 | tf_op jit(solution)/shard_map/ppermute | solution.py:522
  36.0 5.4 %collective-permute-start.13 = (f32[7,8,128]{2,1,0:T(8,128)S(1)}, f32[7,8,128]{2,1,0:T(8,128)S(1)}, u32[]{:S(2)}, u32[]{:S(2)}) collective-permute-start(f32[7,8,128]{2,1,0:T(8,128)S(1)} %get-tuple-element.100), channel_id=1, source_target_pairs={{0,1},{1,0},{2,3},{3,2},{4,5},{5,4},{6,7},{7,6},{8,9},{9,8},{10,11... | collective-permute-start | bytes 86024 | tf_op jit(solution)/shard_map/ppermute | solution.py:522
  38.5 2.9 %collective-permute-start.15 = (f32[7,8,128]{2,1,0:T(8,128)S(1)}, f32[7,8,128]{2,1,0:T(8,128)S(1)}, u32[]{:S(2)}, u32[]{:S(2)}) collective-permute-start(f32[7,8,128]{2,1,0:T(8,128)S(1)} %get-tuple-element.102), channel_id=1, source_target_pairs={{0,32},{1,33},{2,34},{3,35},{4,36},{5,37},{6,38},{7,39},{8,40},{9,... | collective-permute-start | bytes 86024 | tf_op jit(solution)/shard_map/ppermute | solution.py:522
  42.2 8.0 %collective-permute-start.16 = (f32[7,16,128]{2,1,0:T(8,128)S(1)}, f32[7,16,128]{2,1,0:T(8,128)S(1)}, u32[]{:S(2)}, u32[]{:S(2)}) collective-permute-start(f32[7,16,128]{2,1,0:T(8,128)S(1)} %get-tuple-element.108), channel_id=1, source_target_pairs={{0,32},{1,2},{2,1},{3,4},{4,3},{5,6},{6,5},{7,8},{8,7},{9,10},{10,... | collective-permute-start | bytes 172040 | tf_op jit(solution)/shard_map/ppermute | solution.py:522
  44.8 5.4 %collective-permute-start.18 = (f32[7,16,128]{2,1,0:T(8,128)S(1)}, f32[7,16,128]{2,1,0:T(8,128)S(1)}, u32[]{:S(2)}, u32[]{:S(2)}) collective-permute-start(f32[7,16,128]{2,1,0:T(8,128)S(1)} %get-tuple-element.110), channel_id=1, source_target_pairs={{0,1},{1,0},{2,3},{3,2},{4,5},{5,4},{6,7},{7,6},{8,9},{9,8},{10,11... | collective-permute-start | bytes 172040 | tf_op jit(solution)/shard_map/ppermute | solution.py:522
  44.8 5.4 %collective-permute-start.17 = (f32[7,8,128]{2,1,0:T(8,128)S(1)}, f32[7,8,128]{2,1,0:T(8,128)S(1)}, u32[]{:S(2)}, u32[]{:S(2)}) collective-permute-start(f32[7,8,128]{2,1,0:T(8,128)S(1)} %get-tuple-element.109), channel_id=1, source_target_pairs={{0,1},{1,0},{2,3},{3,2},{4,5},{5,4},{6,7},{7,6},{8,9},{9,8},{10,11... | collective-permute-start | bytes 86024 | tf_op jit(solution)/shard_map/ppermute | solution.py:522
  47.8 2.5 %collective-permute-start.19 = (f32[7,8,128]{2,1,0:T(8,128)S(1)}, f32[7,8,128]{2,1,0:T(8,128)S(1)}, u32[]{:S(2)}, u32[]{:S(2)}) collective-permute-start(f32[7,8,128]{2,1,0:T(8,128)S(1)} %get-tuple-element.111), channel_id=1, source_target_pairs={{0,32},{1,33},{2,34},{3,35},{4,36},{5,37},{6,38},{7,39},{8,40},{9,... | collective-permute-start | bytes 86024 | tf_op jit(solution)/shard_map/ppermute | solution.py:522

commit v3 on v2

--- a/solution.py
+++ b/solution.py
@@ -21,7 +21,6 @@
 
 def node_tables():
     points = np.array([-1.0, -1.0 / np.sqrt(5.0), 1.0 / np.sqrt(5.0), 1.0])
-    weights = np.array([1.0, 5.0, 5.0, 1.0]) / 6.0
     bary = np.array([1.0 / np.prod([points[a] - points[b] for b in range(4) if b != a]) for a in range(4)])
     deriv = np.zeros((4, 4))
     for a in range(4):
@@ -37,11 +36,16 @@
         np.kron(np.kron(eye, eye), deriv.T),
     ]
     grads = [np.kron(pair, op) for op in ops]
-    cube = np.kron(np.kron(weights, weights), weights) / 8.0
+    whole = np.array([1.0, 5.0, 5.0, 1.0])
+    cube = np.kron(np.kron(whole, whole), whole) / 2048.0
     mean = np.kron(pair, np.repeat(cube[:, None], 64, axis=1))
     forward = np.concatenate(grads, axis=0)
     backward = np.concatenate([g.T for g in grads], axis=1)
     return forward, backward, mean, mean.T
+
+
+def stacked(table):
+    return jnp.asarray(np.concatenate([table, table], axis=0).astype(jnp.bfloat16))
 
 
 def halves(table):
@@ -275,13 +279,13 @@
     return spread(lines)
 
 
-def limited(field, factor, high, low, table, transposed):
+def limited(field, factor, both, table, transposed):
     for var in range(VARS):
         value = field(var)
         if transposed:
             value = (1.0 - factor) * value
-        high[block(var), :], low[block(var), :] = split(value)
-    means = product(high[...], low[...], table)
+        both[block(var), pl.ds(0, LANES)], both[block(var), pl.ds(LANES, LANES)] = split(value)
+    means = jnp.dot(both[...], table[...], preferred_element_type=F32) * (2048.0 / 1728.0)
 
     def get(var):
         mean = means[ROWS * var : ROWS * (var + 1)]
@@ -303,7 +307,7 @@
         copy.wait()
 
 
-def setup_kernel(columns, lines, adjoint, rates, codes, flags, scales, mean_t, lam, yb, xb, ya, xa, walls, factors, coupling, high, low):
+def setup_kernel(columns, lines, adjoint, rates, codes, flags, scales, mean_t, lam, yb, xb, ya, xa, walls, factors, coupling, both):
     row = lax.broadcasted_iota(jnp.int32, (SPECIES, SPECIES), 0)
     same = row == lax.broadcasted_iota(jnp.int32, (SPECIES, SPECIES), 1)
     off_diag = jnp.where(same, 0.0, rates[...])
@@ -313,7 +317,7 @@
         coupling[source] = jnp.broadcast_to(full[:, source : source + 1], (SPECIES, LANES))
     for section in range(3):
         factors[section] = damping(flags, scales, section)
-    get = limited(lambda v: adjoint[v], factors[2], high, low, mean_t, True)
+    get = limited(lambda v: adjoint[v], factors[2], both, mean_t, True)
     for var in range(VARS):
         lam[var] = (2.0 / 3.0) * get(var)
     pack(lambda v: lam[v], (yb, xb, ya, xa))
@@ -378,11 +382,11 @@
 def face_kernel(section, share, last, state, inner, walls, factors, mean, *refs):
     along = ()
     if last:
-        near_x, near_y, out, high, low = refs
+        near_x, near_y, out, both = refs
     else:
-        along = refs[4:-9]
+        along = refs[4:-8]
         xa, xb, ya, yb = refs[:4]
-        out, near_x, near_y, sa, sb, sc, sd, high, low = refs[-9:]
+        out, near_x, near_y, sa, sb, sc, sd, both = refs[-8:]
         fetch_near(state, walls, Received((xa, xb, ya, yb)), near_x, near_y)
     gas = Gas(lambda v: state[v], (0, 1))
     gain_x = face_gain(Face(walls[0], 0), 0, gas, Gas(lambda v: near_x[v], (0,)))
@@ -391,7 +395,7 @@
         value = state[var]
         change = gain_x(var, value, near_x[var]) + gain_y(var, value, near_y[var])
         out[var] = inner[var] + (share * STEP) * change
-    get = limited(lambda v: out[v], factors[section], high, low, mean, False)
+    get = limited(lambda v: out[v], factors[section], both, mean, False)
     for var in range(VARS):
         out[var] = get(var)
     if not last:
@@ -453,10 +457,10 @@
 
 def turn_kernel(state, lam, inner, walls, factors, mean_t, *refs):
     got = refs[:4]
-    below, carry, near_x, near_y, sa, sb, sc, sd, high, low, work = refs[4:]
+    below, carry, near_x, near_y, sa, sb, sc, sd, both, work = refs[4:]
     fetch_near(state, walls, Received(got), near_x, near_y)
     back_faces(state, lam, near_x, near_y, walls, Received(got, 1), inner, work)
-    get = limited(lambda v: work[v], factors[1], high, low, mean_t, True)
+    get = limited(lambda v: work[v], factors[1], both, mean_t, True)
     for var in range(VARS):
         reverse = get(var)
         carry[var] = 0.5 * lam[var] + 0.75 * reverse
@@ -465,9 +469,9 @@
 
 
 def middle_kernel(state, lam, inner, near_x, near_y, walls, factors, mean_t, *refs):
-    la, lb, lc, ld, below, sa, sb, sc, sd, high, low, work = refs
+    la, lb, lc, ld, below, sa, sb, sc, sd, both, work = refs
     back_faces(state, lam, near_x, near_y, walls, Received((la, lb, lc, ld)), inner, work)
-    get = limited(lambda v: work[v], factors[0], high, low, mean_t, True)
+    get = limited(lambda v: work[v], factors[0], both, mean_t, True)
     for var in range(VARS):
         below[var] = get(var)
     pack(lambda v: below[v], (sa, sb, sc, sd))
@@ -530,16 +534,18 @@
 
 
 def per_device(state_start, adjoint_end, limiter_flags, limiter_scales, face_codes, reaction_rates):
-    forward, backward, mean, mean_t = [halves(table) for table in node_tables()]
+    forward, backward, mean, mean_t = node_tables()
+    forward, backward, mean, mean_t = halves(forward), halves(backward), stacked(mean), stacked(mean_t)
     q0 = state_start.reshape(FIELD)
     adjoint = adjoint_end.reshape(FIELD)
     narrow, wide = halved(LANES), halved(3 * LANES)
+    both = [pltpu.VMEM((VARS * ROWS, 2 * LANES), BF16)]
     total = [pltpu.VMEM((VARS * ROWS, LANES), F32)]
     total3 = [pltpu.VMEM((VARS * ROWS, 3 * LANES), F32)]
     work = [pltpu.VMEM(FIELD, F32)]
 
     held = [q0, adjoint, reaction_rates, face_codes, limiter_flags, limiter_scales]
-    held += [mean_t, forward, mean, backward]
+    held += [mean_t, forward]
     got = pl.pallas_call(
         functools.partial(start_kernel, len(held)),
         in_specs=[pl.BlockSpec(memory_space=pltpu.HBM)] * len(held),
@@ -550,14 +556,14 @@
         compiler_params=pltpu.CompilerParams(vmem_limit_bytes=8 << 20),
         name="start_kernel",
     )(*[pltpu.with_memory_space_constraint(v, pltpu.HBM) for v in held])
-    q0, adjoint, rates, codes, flags, scales, mean_t, forward, mean, backward = got[: len(held)]
+    q0, adjoint, rates, codes, flags, scales, mean_t, forward = got[: len(held)]
     got = exchange(got[len(held) :])
     size = functools.partial(setup_kernel, lax.axis_size("gx"), lax.axis_size("gy"))
     lam3, *along, walls, factors, coupling = call(
         size,
         [adjoint, rates, codes, flags, scales, mean_t],
         [FIELD] + packs(1) + [TABLE, TABLE, (SPECIES, SPECIES, LANES)],
-        narrow,
+        both,
     )
 
     def inner(mix, state):
@@ -574,7 +580,7 @@
         out, near_x, near_y, *sent = call(
             kernel, [state, part, walls, factors, mean, *got, *along],
             [FIELD] * 3 + packs(2 if along else 1),
-            narrow,
+            both,
         )
         return out, near_x, near_y, sent
 
@@ -590,17 +596,17 @@
         turn_kernel,
         [q2, lam3, back, walls, factors, mean_t, *got],
         [FIELD] * 4 + packs(1),
-        narrow + work,
+        both + work,
     )
     got = exchange(sent)
     last = functools.partial(face_kernel, 2, 2.0 / 3.0, True)
-    state_end = call(last, [q2, part, walls, factors, mean, x2, y2], [FIELD], narrow)[0]
+    state_end = call(last, [q2, part, walls, factors, mean, x2, y2], [FIELD], both)[0]
     back = back_inner(q1, lam2, z1)
     lam1, *sent = call(
         middle_kernel,
         [q1, lam2, back, x1, y1, walls, factors, mean_t, *got],
         [FIELD] + packs(1),
-        narrow + work,
+        both + work,
     )
     got = exchange(sent)
     back = back_inner(q0, lam1, z0)

time: 51.4 us -> 51.2 us (level)
  no operation moved by 1% of the time
where the time goes in v3:
time: 51.2 us; the launch traced here: 51 us
  starting transfers between devices  33.4 us (65%)
  Pallas kernels  11.9 us (23%)
  waiting for transfers between devices  4.95 us (10%)
  between operations  0.77 us (2%)
    ppermute x20, starting transfers between devices, swap(): return lax.ppermute(values, ('gx', 'gy'), moves)  33.4 us
    pallas_call x13, Pallas kernels, call(): pl.pallas_call(kernel, in_specs=[pl.BlockSpec(memory_space=pltpu.VMEM)] *...  10.6 us
    ppermute x20, waiting for transfers between devices, swap(): return lax.ppermute(values, ('gx', 'gy'), moves)  4.95 us
    pallas_call x1, Pallas kernels, per_device(): pl.pallas_call(functools.partial(start_kernel, len(held)), in_specs=[pl.B...  1.3 us
  transfers between devices with their start and end apart: 20, of which 5 were waited for; matrix products, arithmetic and copies ran while one was open for 0% of the time, Pallas kernels for 13%

profile of v3, /device:TPU:89, one launch (start us, length us, event | category | flops | bytes accessed | tf_op | source)
XLA Modules:
  0.0 51.0 jit_solution(3910432481142119031)
XLA Ops:
  0.6 1.3 %start_kernel.1 = (f32[25,16,128]{2,1,0:T(8,128)S(1)}, f32[25,16,128]{2,1,0:T(8,128)S(1)}, f32[21,21]{1,0:T(8,128)S(1)}, s32[2,1,16]{2,1,0:T(1,128)S(1)}, s32[3,...) custom-call(f32[25,16,128]{2,1,0:T(8,128)} %bitcast.5, ...), custom_call_target="tpu_custom_call" | custom-call | tf_op jit(solution)/shard_map/start_kernel/pallas_call | solution.py:549
  1.9 4.1 %collective-permute-start = (f32[7,16,128]{2,1,0:T(8,128)S(1)}, f32[7,16,128]{2,1,0:T(8,128)S(1)}, u32[]{:S(2)}, u32[]{:S(2)}) collective-permute-start(f32[7,16,128]{2,1,0:T(8,128)S(1)} %get-tuple-element.67), channel_id=1, source_target_pairs={{0,32},{1,2},{2,1},{3,4},{4,3},{5,6},{6,5},{7,8},{8,7},{9,10},{10,... | collective-permute-start | bytes 172040 | tf_op jit(solution)/shard_map/ppermute | solution.py:526
  6.0 4.1 %collective-permute-start.1 = (f32[7,8,128]{2,1,0:T(8,128)S(1)}, f32[7,8,128]{2,1,0:T(8,128)S(1)}, u32[]{:S(2)}, u32[]{:S(2)}) collective-permute-start(f32[7,8,128]{2,1,0:T(8,128)S(1)} %get-tuple-element.68), channel_id=1, source_target_pairs={{0,1},{1,0},{2,3},{3,2},{4,5},{5,4},{6,7},{7,6},{8,9},{9,8},{10,11... | collective-permute-start | bytes 86024 | tf_op jit(solution)/shard_map/ppermute | solution.py:526
  10.2 0.0 collective-permute-start.3
  10.2 0.5 setup_kernel.1
  10.7 0.0 copy-start.1
  10.7 0.9 %volume_kernel.3 = (f32[25,16,128]{2,1,0:T(8,128)S(1)}, f32[25,16,128]{2,1,0:T(8,128)S(1)}) custom-call(f32[21,21,128]{2,1,0:T(8,128)S(1)} %get-tuple-element.62.coupling, f32[25,16,128]{2,1,0:T(8,128)S(1)} %get-tuple-element.55.state.start, f32[25,16,128]{2,1,0:T(8,128)S(1)} %get-tuple-element.55.state.start, f32[3,16,128]{2,1,0:T(8,128)S(1)} %get-tuple-element.63.walls, ...), custom_call_target="tpu_custom_call" | custom-call | tf_op jit(solution)/shard_map/volume_kernel/pallas_call | solution.py:491
  11.6 0.2 collective-permute-done.1.refs_1_
  11.8 0.6 %face_kernel.3 = (f32[25,16,128]{2,1,0:T(8,128)S(1)}, f32[25,16,128]{2,1,0:T(8,128)S(1)}, f32[25,16,128]{2,1,0:T(8,128)S(1)}, f32[7,16,128]{2,1,0:T(8,128)S(1)},...) custom-call(f32[25,16,128]{2,1,0:T(8,128)S(1)} %get-tuple-element.55.state.start, ...), custom_call_target="tpu_custom_call" | custom-call | tf_op jit(solution)/shard_map/face_kernel/pallas_call | solution.py:491
  12.4 2.8 %collective-permute-start.4 = (f32[7,16,128]{2,1,0:T(8,128)S(1)}, f32[7,16,128]{2,1,0:T(8,128)S(1)}, u32[]{:S(2)}, u32[]{:S(2)}) collective-permute-start(f32[7,16,128]{2,1,0:T(8,128)S(1)} %get-tuple-element.73), channel_id=1, source_target_pairs={{0,32},{1,2},{2,1},{3,4},{4,3},{5,6},{6,5},{7,8},{8,7},{9,10},{10,... | collective-permute-start | bytes 172040 | tf_op jit(solution)/shard_map/ppermute | solution.py:526
  15.1 0.1 collective-permute-start.6
  15.2 3.6 %collective-permute-start.5 = (f32[7,8,128]{2,1,0:T(8,128)S(1)}, f32[7,8,128]{2,1,0:T(8,128)S(1)}, u32[]{:S(2)}, u32[]{:S(2)}) collective-permute-start(f32[7,8,128]{2,1,0:T(8,128)S(1)} %get-tuple-element.74), channel_id=1, source_target_pairs={{0,1},{1,0},{2,3},{3,2},{4,5},{5,4},{6,7},{7,6},{8,9},{9,8},{10,11... | collective-permute-start | bytes 86024 | tf_op jit(solution)/shard_map/ppermute | solution.py:526
  18.8 0.9 %volume_kernel.4 = (f32[25,16,128]{2,1,0:T(8,128)S(1)}, f32[25,16,128]{2,1,0:T(8,128)S(1)}) custom-call(f32[21,21,128]{2,1,0:T(8,128)S(1)} %get-tuple-element.62.coupling, f32[25,16,128]{2,1,0:T(8,128)S(1)} %get-tuple-element.71.state, f32[25,16,128]{2,1,0:T(8,128)S(1)} %get-tuple-element.55.state.start, f32[3,16,128]{2,1,0:T(8,128)S(1)} %get-tuple-element.63.walls, ...), custom_call_target="tpu_custom_call" | custom-call | tf_op jit(solution)/shard_map/volume_kernel/pallas_call | solution.py:491
  19.8 0.9 %collective-permute-done.5.refs_1_ = f32[7,8,128]{2,1,0:T(8,128)S(1)} collective-permute-done((f32[7,8,128]{2,1,0:T(8,128)S(1)}, f32[7,8,128]{2,1,0:T(8,128)S(1)}, u32[]{:S(2)}, u32[]{:S(2)}) %collective-permute-start.5) | collective-permute-done | bytes 28704 | tf_op jit(solution)/shard_map/ppermute | solution.py:526
  20.6 0.6 %face_kernel.4 = (f32[25,16,128]{2,1,0:T(8,128)S(1)}, f32[25,16,128]{2,1,0:T(8,128)S(1)}, f32[25,16,128]{2,1,0:T(8,128)S(1)}, f32[14,16,128]{2,1,0:T(8,128)S(1)}...) custom-call(f32[25,16,128]{2,1,0:T(8,128)S(1)} %get-tuple-element.71.state, ...), custom_call_target="tpu_custom_call" | custom-call | tf_op jit(solution)/shard_map/face_kernel/pallas_call | solution.py:491
  21.3 3.6 %collective-permute-start.8 = (f32[14,16,128]{2,1,0:T(8,128)S(1)}, f32[14,16,128]{2,1,0:T(8,128)S(1)}, u32[]{:S(2)}, u32[]{:S(2)}) collective-permute-start(f32[14,16,128]{2,1,0:T(8,128)S(1)} %get-tuple-element.85), channel_id=1, source_target_pairs={{0,32},{1,2},{2,1},{3,4},{4,3},{5,6},{6,5},{7,8},{8,7},{9,10},{10,... | collective-permute-start | bytes 344072 | tf_op jit(solution)/shard_map/ppermute | solution.py:526
  24.9 2.7 %collective-permute-start.9 = (f32[14,8,128]{2,1,0:T(8,128)S(1)}, f32[14,8,128]{2,1,0:T(8,128)S(1)}, u32[]{:S(2)}, u32[]{:S(2)}) collective-permute-start(f32[14,8,128]{2,1,0:T(8,128)S(1)} %get-tuple-element.86), channel_id=1, source_target_pairs={{0,1},{1,0},{2,3},{3,2},{4,5},{5,4},{6,7},{7,6},{8,9},{9,8},{10,11... | collective-permute-start | bytes 172040 | tf_op jit(solution)/shard_map/ppermute | solution.py:526
  27.6 0.9 %volume_kernel.5 = (f32[25,16,128]{2,1,0:T(8,128)S(1)}, f32[25,16,128]{2,1,0:T(8,128)S(1)}) custom-call(f32[21,21,128]{2,1,0:T(8,128)S(1)} %get-tuple-element.62.coupling, f32[25,16,128]{2,1,0:T(8,128)S(1)} %get-tuple-element.81.state, f32[25,16,128]{2,1,0:T(8,128)S(1)} %get-tuple-element.55.state.start, f32[3,16,128]{2,1,0:T(8,128)S(1)} %get-tuple-element.63.walls, ...), custom_call_target="tpu_custom_call" | custom-call | tf_op jit(solution)/shard_map/volume_kernel/pallas_call | solution.py:491
  28.6 0.8 %back_volume_kernel.3.inner = f32[25,16,128]{2,1,0:T(8,128)S(1)} custom-call(f32[21,21,128]{2,1,0:T(8,128)S(1)} %get-tuple-element.62.coupling, f32[25,16,128]{2,1,0:T(8,128)S(1)} %get-tuple-element.81.state, f32[25,16,128]{2,1,0:T(8,128)S(1)} %get-tuple-element.83.lam, f32[25,16,128]{2,1,0:T(8,128)S(1)} %get-tuple-element.84.near, ...), custom_call_target="tpu_custom_call" | custom-call | tf_op jit(solution)/shard_map/back_volume_kernel/pallas_call | solution.py:491
  29.4 1.3 %collective-permute-done.9.refs_1_ = f32[14,8,128]{2,1,0:T(8,128)S(1)} collective-permute-done((f32[14,8,128]{2,1,0:T(8,128)S(1)}, f32[14,8,128]{2,1,0:T(8,128)S(1)}, u32[]{:S(2)}, u32[]{:S(2)}) %collective-permute-start.9) | collective-permute-done | bytes 57376 | tf_op jit(solution)/shard_map/ppermute | solution.py:526
  30.7 0.9 %turn_kernel.1 = (f32[25,16,128]{2,1,0:T(8,128)S(1)}, f32[25,16,128]{2,1,0:T(8,128)S(1)}, f32[25,16,128]{2,1,0:T(8,128)S(1)}, f32[25,16,128]{2,1,0:T(8,128)S(1)}...) custom-call(f32[25,16,128]{2,1,0:T(8,128)S(1)} %get-tuple-element.81, ...), custom_call_target="tpu_custom_call" | custom-call | tf_op jit(solution)/shard_map/turn_kernel/pallas_call | solution.py:491
  31.6 4.2 %collective-permute-start.12 = (f32[7,16,128]{2,1,0:T(8,128)S(1)}, f32[7,16,128]{2,1,0:T(8,128)S(1)}, u32[]{:S(2)}, u32[]{:S(2)}) collective-permute-start(f32[7,16,128]{2,1,0:T(8,128)S(1)} %get-tuple-element.95), channel_id=1, source_target_pairs={{0,32},{1,2},{2,1},{3,4},{4,3},{5,6},{6,5},{7,8},{8,7},{9,10},{10,... | collective-permute-start | bytes 172040 | tf_op jit(solution)/shard_map/ppermute | solution.py:526
  35.8 2.5 %collective-permute-start.13 = (f32[7,8,128]{2,1,0:T(8,128)S(1)}, f32[7,8,128]{2,1,0:T(8,128)S(1)}, u32[]{:S(2)}, u32[]{:S(2)}) collective-permute-start(f32[7,8,128]{2,1,0:T(8,128)S(1)} %get-tuple-element.96), channel_id=1, source_target_pairs={{0,1},{1,0},{2,3},{3,2},{4,5},{5,4},{6,7},{7,6},{8,9},{9,8},{10,11... | collective-permute-start | bytes 86024 | tf_op jit(solution)/shard_map/ppermute | solution.py:526
  38.4 0.8 %back_volume_kernel.4.inner = f32[25,16,128]{2,1,0:T(8,128)S(1)} custom-call(f32[21,21,128]{2,1,0:T(8,128)S(1)} %get-tuple-element.62.coupling, f32[25,16,128]{2,1,0:T(8,128)S(1)} %get-tuple-element.71.state, f32[25,16,128]{2,1,0:T(8,128)S(1)} %get-tuple-element.91.lam, f32[25,16,128]{2,1,0:T(8,128)S(1)} %get-tuple-element.92.near, ...), custom_call_target="tpu_custom_call" | custom-call | tf_op jit(solution)/shard_map/back_volume_kernel/pallas_call | solution.py:491
  39.2 2.0 %collective-permute-done.13.refs_1_ = f32[7,8,128]{2,1,0:T(8,128)S(1)} collective-permute-done((f32[7,8,128]{2,1,0:T(8,128)S(1)}, f32[7,8,128]{2,1,0:T(8,128)S(1)}, u32[]{:S(2)}, u32[]{:S(2)}) %collective-permute-start.13) | collective-permute-done | bytes 28704 | tf_op jit(solution)/shard_map/ppermute | solution.py:526
  41.2 0.7 %middle_kernel.1 = (f32[25,16,128]{2,1,0:T(8,128)S(1)}, f32[7,16,128]{2,1,0:T(8,128)S(1)}, f32[7,8,128]{2,1,0:T(8,128)S(1)}, f32[7,16,128]{2,1,0:T(8,128)S(1)}, f32[7,8,128]{2,1,0:T(8,128)S(1)}) custom-call(f32[25,16,128]{2,1,0:T(8,128)S(1)} %get-tuple-element.71.state, f32[25,16,128]{2,1,0:T(8,128)S(1)} %get-tuple-element.91.lam, ...), custom_call_target="tpu_custom_call" | custom-call | tf_op jit(solution)/shard_map/middle_kernel/pallas_call | solution.py:491
  41.9 2.6 %collective-permute-start.16 = (f32[7,16,128]{2,1,0:T(8,128)S(1)}, f32[7,16,128]{2,1,0:T(8,128)S(1)}, u32[]{:S(2)}, u32[]{:S(2)}) collective-permute-start(f32[7,16,128]{2,1,0:T(8,128)S(1)} %get-tuple-element.104), channel_id=1, source_target_pairs={{0,32},{1,2},{2,1},{3,4},{4,3},{5,6},{6,5},{7,8},{8,7},{9,10},{10,... | collective-permute-start | bytes 172040 | tf_op jit(solution)/shard_map/ppermute | solution.py:526
  44.5 3.0 %collective-permute-start.17 = (f32[7,8,128]{2,1,0:T(8,128)S(1)}, f32[7,8,128]{2,1,0:T(8,128)S(1)}, u32[]{:S(2)}, u32[]{:S(2)}) collective-permute-start(f32[7,8,128]{2,1,0:T(8,128)S(1)} %get-tuple-element.105), channel_id=1, source_target_pairs={{0,1},{1,0},{2,3},{3,2},{4,5},{5,4},{6,7},{7,6},{8,9},{9,8},{10,11... | collective-permute-start | bytes 86024 | tf_op jit(solution)/shard_map/ppermute | solution.py:526
  47.6 1.0 %face_kernel.5 = f32[25,16,128]{2,1,0:T(8,128)} custom-call(f32[25,16,128]{2,1,0:T(8,128)S(1)} %get-tuple-element.81.state, f32[25,16,128]{2,1,0:T(8,128)S(1)} %get-tuple-element.82.inner, f32[3,16,128]{2,1,0:T(8,128)S(1)} %get-tuple-element.63.walls, f32[3,16,128]{2,1,0:T(8,128)S(1)} %get-tuple-element.66.factors, bf16[256,128]{1,0:T(8,128)(2,1)S(1)} %copy-done.1, ...), custom_call_target="tpu_custom_call" | custom-call | tf_op jit(solution)/shard_map/face_kernel/pallas_call | solution.py:491
  48.5 0.8 %back_volume_kernel.5.inner = f32[25,16,128]{2,1,0:T(8,128)S(1)} custom-call(f32[21,21,128]{2,1,0:T(8,128)S(1)} %get-tuple-element.62.coupling, f32[25,16,128]{2,1,0:T(8,128)S(1)} %get-tuple-element.55.state.start, f32[25,16,128]{2,1,0:T(8,128)S(1)} %get-tuple-element.99.lam, f32[25,16,128]{2,1,0:T(8,128)S(1)} %get-tuple-element.100.near, ...), custom_call_target="tpu_custom_call" | custom-call | tf_op jit(solution)/shard_map/back_volume_kernel/pallas_call | solution.py:491
  49.4 0.6 %collective-permute-done.17.lb = f32[7,8,128]{2,1,0:T(8,128)S(1)} collective-permute-done((f32[7,8,128]{2,1,0:T(8,128)S(1)}, f32[7,8,128]{2,1,0:T(8,128)S(1)}, u32[]{:S(2)}, u32[]{:S(2)}) %collective-permute-start.17) | collective-permute-done | bytes 28704 | tf_op jit(solution)/shard_map/ppermute | solution.py:526
  50.0 1.1 %end_kernel.1 = f32[25,16,128]{2,1,0:T(8,128)} custom-call(f32[25,16,128]{2,1,0:T(8,128)S(1)} %get-tuple-element.55.state.start, f32[25,16,128]{2,1,0:T(8,128)S(1)} %get-tuple-element.99.lam, f32[25,16,128]{2,1,0:T(8,128)S(1)} %back_volume_kernel.5.inner, f32[25,16,128]{2,1,0:T(8,128)S(1)} %get-tuple-element.101.near_x, ...), custom_call_target="tpu_custom_call" | custom-call | tf_op jit(solution)/shard_map/end_kernel/pallas_call | solution.py:491
  (26 shorter events, 0.1 us)
Async XLA Ops:
  1.9 9.8 %collective-permute-start = (f32[7,16,128]{2,1,0:T(8,128)S(1)}, f32[7,16,128]{2,1,0:T(8,128)S(1)}, u32[]{:S(2)}, u32[]{:S(2)}) collective-permute-start(f32[7,16,128]{2,1,0:T(8,128)S(1)} %get-tuple-element.67), channel_id=1, source_target_pairs={{0,32},{1,2},{2,1},{3,4},{4,3},{5,6},{6,5},{7,8},{8,7},{9,10},{10,... | collective-permute-start | bytes 172040 | tf_op jit(solution)/shard_map/ppermute | solution.py:526
  6.0 5.7 %collective-permute-start.2 = (f32[7,16,128]{2,1,0:T(8,128)S(1)}, f32[7,16,128]{2,1,0:T(8,128)S(1)}, u32[]{:S(2)}, u32[]{:S(2)}) collective-permute-start(f32[7,16,128]{2,1,0:T(8,128)S(1)} %get-tuple-element.69), channel_id=1, source_target_pairs={{0,1},{1,0},{2,3},{3,2},{4,5},{5,4},{6,7},{7,6},{8,9},{9,8},{10,11... | collective-permute-start | bytes 172040 | tf_op jit(solution)/shard_map/ppermute | solution.py:526
  6.0 5.7 %collective-permute-start.1 = (f32[7,8,128]{2,1,0:T(8,128)S(1)}, f32[7,8,128]{2,1,0:T(8,128)S(1)}, u32[]{:S(2)}, u32[]{:S(2)}) collective-permute-start(f32[7,8,128]{2,1,0:T(8,128)S(1)} %get-tuple-element.68), channel_id=1, source_target_pairs={{0,1},{1,0},{2,3},{3,2},{4,5},{5,4},{6,7},{7,6},{8,9},{9,8},{10,11... | collective-permute-start | bytes 86024 | tf_op jit(solution)/shard_map/ppermute | solution.py:526
  10.2 1.6 %collective-permute-start.3 = (f32[7,8,128]{2,1,0:T(8,128)S(1)}, f32[7,8,128]{2,1,0:T(8,128)S(1)}, u32[]{:S(2)}, u32[]{:S(2)}) collective-permute-start(f32[7,8,128]{2,1,0:T(8,128)S(1)} %get-tuple-element.70), channel_id=1, source_target_pairs={{0,32},{1,33},{2,34},{3,35},{4,36},{5,37},{6,38},{7,39},{8,40},{9,... | collective-permute-start | bytes 86024 | tf_op jit(solution)/shard_map/ppermute | solution.py:526
  10.7 1.1 %copy-start.1 = (bf16[256,128]{1,0:T(8,128)(2,1)S(1)}, bf16[256,128]{1,0:T(8,128)(2,1)}, u32[]{:S(2)}) copy-start(bf16[256,128]{1,0:T(8,128)(2,1)} %constant.10.clone.mean) | copy-start | bytes 196612
  12.4 8.3 %collective-permute-start.4 = (f32[7,16,128]{2,1,0:T(8,128)S(1)}, f32[7,16,128]{2,1,0:T(8,128)S(1)}, u32[]{:S(2)}, u32[]{:S(2)}) collective-permute-start(f32[7,16,128]{2,1,0:T(8,128)S(1)} %get-tuple-element.73), channel_id=1, source_target_pairs={{0,32},{1,2},{2,1},{3,4},{4,3},{5,6},{6,5},{7,8},{8,7},{9,10},{10,... | collective-permute-start | bytes 172040 | tf_op jit(solution)/shard_map/ppermute | solution.py:526
  15.1 5.5 %collective-permute-start.6 = (f32[7,16,128]{2,1,0:T(8,128)S(1)}, f32[7,16,128]{2,1,0:T(8,128)S(1)}, u32[]{:S(2)}, u32[]{:S(2)}) collective-permute-start(f32[7,16,128]{2,1,0:T(8,128)S(1)} %get-tuple-element.75), channel_id=1, source_target_pairs={{0,1},{1,0},{2,3},{3,2},{4,5},{5,4},{6,7},{7,6},{8,9},{9,8},{10,11... | collective-permute-start | bytes 172040 | tf_op jit(solution)/shard_map/ppermute | solution.py:526
  15.2 5.4 %collective-permute-start.5 = (f32[7,8,128]{2,1,0:T(8,128)S(1)}, f32[7,8,128]{2,1,0:T(8,128)S(1)}, u32[]{:S(2)}, u32[]{:S(2)}) collective-permute-start(f32[7,8,128]{2,1,0:T(8,128)S(1)} %get-tuple-element.74), channel_id=1, source_target_pairs={{0,1},{1,0},{2,3},{3,2},{4,5},{5,4},{6,7},{7,6},{8,9},{9,8},{10,11... | collective-permute-start | bytes 86024 | tf_op jit(solution)/shard_map/ppermute | solution.py:526
  18.8 1.8 %collective-permute-start.7 = (f32[7,8,128]{2,1,0:T(8,128)S(1)}, f32[7,8,128]{2,1,0:T(8,128)S(1)}, u32[]{:S(2)}, u32[]{:S(2)}) collective-permute-start(f32[7,8,128]{2,1,0:T(8,128)S(1)} %get-tuple-element.76), channel_id=1, source_target_pairs={{0,32},{1,33},{2,34},{3,35},{4,36},{5,37},{6,38},{7,39},{8,40},{9,... | collective-permute-start | bytes 86024 | tf_op jit(solution)/shard_map/ppermute | solution.py:526
  21.3 9.4 %collective-permute-start.8 = (f32[14,16,128]{2,1,0:T(8,128)S(1)}, f32[14,16,128]{2,1,0:T(8,128)S(1)}, u32[]{:S(2)}, u32[]{:S(2)}) collective-permute-start(f32[14,16,128]{2,1,0:T(8,128)S(1)} %get-tuple-element.85), channel_id=1, source_target_pairs={{0,32},{1,2},{2,1},{3,4},{4,3},{5,6},{6,5},{7,8},{8,7},{9,10},{10,... | collective-permute-start | bytes 344072 | tf_op jit(solution)/shard_map/ppermute | solution.py:526
  24.9 5.8 %collective-permute-start.10 = (f32[14,16,128]{2,1,0:T(8,128)S(1)}, f32[14,16,128]{2,1,0:T(8,128)S(1)}, u32[]{:S(2)}, u32[]{:S(2)}) collective-permute-start(f32[14,16,128]{2,1,0:T(8,128)S(1)} %get-tuple-element.87), channel_id=1, source_target_pairs={{0,1},{1,0},{2,3},{3,2},{4,5},{5,4},{6,7},{7,6},{8,9},{9,8},{10,11... | collective-permute-start | bytes 344072 | tf_op jit(solution)/shard_map/ppermute | solution.py:526
  24.9 5.8 %collective-permute-start.9 = (f32[14,8,128]{2,1,0:T(8,128)S(1)}, f32[14,8,128]{2,1,0:T(8,128)S(1)}, u32[]{:S(2)}, u32[]{:S(2)}) collective-permute-start(f32[14,8,128]{2,1,0:T(8,128)S(1)} %get-tuple-element.86), channel_id=1, source_target_pairs={{0,1},{1,0},{2,3},{3,2},{4,5},{5,4},{6,7},{7,6},{8,9},{9,8},{10,11... | collective-permute-start | bytes 172040 | tf_op jit(solution)/shard_map/ppermute | solution.py:526
  27.6 3.1 %collective-permute-start.11 = (f32[14,8,128]{2,1,0:T(8,128)S(1)}, f32[14,8,128]{2,1,0:T(8,128)S(1)}, u32[]{:S(2)}, u32[]{:S(2)}) collective-permute-start(f32[14,8,128]{2,1,0:T(8,128)S(1)} %get-tuple-element.88), channel_id=1, source_target_pairs={{0,32},{1,33},{2,34},{3,35},{4,36},{5,37},{6,38},{7,39},{8,40},{9,... | collective-permute-start | bytes 172040 | tf_op jit(solution)/shard_map/ppermute | solution.py:526
  27.6 0.9 %copy-start = (bf16[2,128,384]{2,1,0:T(8,128)(2,1)S(1)}, bf16[2,128,384]{2,1,0:T(8,128)(2,1)}, u32[]{:S(2)}) copy-start(bf16[2,128,384]{2,1,0:T(8,128)(2,1)} %constant.9.clone.table) | copy-start | bytes 589828
  31.6 9.7 %collective-permute-start.12 = (f32[7,16,128]{2,1,0:T(8,128)S(1)}, f32[7,16,128]{2,1,0:T(8,128)S(1)}, u32[]{:S(2)}, u32[]{:S(2)}) collective-permute-start(f32[7,16,128]{2,1,0:T(8,128)S(1)} %get-tuple-element.95), channel_id=1, source_target_pairs={{0,32},{1,2},{2,1},{3,4},{4,3},{5,6},{6,5},{7,8},{8,7},{9,10},{10,... | collective-permute-start | bytes 172040 | tf_op jit(solution)/shard_map/ppermute | solution.py:526
  35.8 5.4 %collective-permute-start.14 = (f32[7,16,128]{2,1,0:T(8,128)S(1)}, f32[7,16,128]{2,1,0:T(8,128)S(1)}, u32[]{:S(2)}, u32[]{:S(2)}) collective-permute-start(f32[7,16,128]{2,1,0:T(8,128)S(1)} %get-tuple-element.97), channel_id=1, source_target_pairs={{0,1},{1,0},{2,3},{3,2},{4,5},{5,4},{6,7},{7,6},{8,9},{9,8},{10,11... | collective-permute-start | bytes 172040 | tf_op jit(solution)/shard_map/ppermute | solution.py:526
  35.8 5.4 %collective-permute-start.13 = (f32[7,8,128]{2,1,0:T(8,128)S(1)}, f32[7,8,128]{2,1,0:T(8,128)S(1)}, u32[]{:S(2)}, u32[]{:S(2)}) collective-permute-start(f32[7,8,128]{2,1,0:T(8,128)S(1)} %get-tuple-element.96), channel_id=1, source_target_pairs={{0,1},{1,0},{2,3},{3,2},{4,5},{5,4},{6,7},{7,6},{8,9},{9,8},{10,11... | collective-permute-start | bytes 86024 | tf_op jit(solution)/shard_map/ppermute | solution.py:526
  38.4 2.9 %collective-permute-start.15 = (f32[7,8,128]{2,1,0:T(8,128)S(1)}, f32[7,8,128]{2,1,0:T(8,128)S(1)}, u32[]{:S(2)}, u32[]{:S(2)}) collective-permute-start(f32[7,8,128]{2,1,0:T(8,128)S(1)} %get-tuple-element.98), channel_id=1, source_target_pairs={{0,32},{1,33},{2,34},{3,35},{4,36},{5,37},{6,38},{7,39},{8,40},{9,... | collective-permute-start | bytes 86024 | tf_op jit(solution)/shard_map/ppermute | solution.py:526
  41.9 8.0 %collective-permute-start.16 = (f32[7,16,128]{2,1,0:T(8,128)S(1)}, f32[7,16,128]{2,1,0:T(8,128)S(1)}, u32[]{:S(2)}, u32[]{:S(2)}) collective-permute-start(f32[7,16,128]{2,1,0:T(8,128)S(1)} %get-tuple-element.104), channel_id=1, source_target_pairs={{0,32},{1,2},{2,1},{3,4},{4,3},{5,6},{6,5},{7,8},{8,7},{9,10},{10,... | collective-permute-start | bytes 172040 | tf_op jit(solution)/shard_map/ppermute | solution.py:526
  44.5 5.4 %collective-permute-start.18 = (f32[7,16,128]{2,1,0:T(8,128)S(1)}, f32[7,16,128]{2,1,0:T(8,128)S(1)}, u32[]{:S(2)}, u32[]{:S(2)}) collective-permute-start(f32[7,16,128]{2,1,0:T(8,128)S(1)} %get-tuple-element.106), channel_id=1, source_target_pairs={{0,1},{1,0},{2,3},{3,2},{4,5},{5,4},{6,7},{7,6},{8,9},{9,8},{10,11... | collective-permute-start | bytes 172040 | tf_op jit(solution)/shard_map/ppermute | solution.py:526
  44.5 5.4 %collective-permute-start.17 = (f32[7,8,128]{2,1,0:T(8,128)S(1)}, f32[7,8,128]{2,1,0:T(8,128)S(1)}, u32[]{:S(2)}, u32[]{:S(2)}) collective-permute-start(f32[7,8,128]{2,1,0:T(8,128)S(1)} %get-tuple-element.105), channel_id=1, source_target_pairs={{0,1},{1,0},{2,3},{3,2},{4,5},{5,4},{6,7},{7,6},{8,9},{9,8},{10,11... | collective-permute-start | bytes 86024 | tf_op jit(solution)/shard_map/ppermute | solution.py:526
  47.6 2.4 %collective-permute-start.19 = (f32[7,8,128]{2,1,0:T(8,128)S(1)}, f32[7,8,128]{2,1,0:T(8,128)S(1)}, u32[]{:S(2)}, u32[]{:S(2)}) collective-permute-start(f32[7,8,128]{2,1,0:T(8,128)S(1)} %get-tuple-element.107), channel_id=1, source_target_pairs={{0,32},{1,33},{2,34},{3,35},{4,36},{5,37},{6,38},{7,39},{8,40},{9,... | collective-permute-start | bytes 86024 | tf_op jit(solution)/shard_map/ppermute | solution.py:526

commit v4 on v3

--- a/solution.py
+++ b/solution.py
@@ -108,6 +108,13 @@
     return low, high
 
 
+def rows_of(ref, group, part):
+    if group < GROUPS - 1:
+        return pl.ds(ROWS * (part * (GROUPS - 1) + group), ROWS)
+    parts = ref.shape[0] // 100
+    return pl.ds(96 * parts + 4 * part, 4)
+
+
 class Received:
     def __init__(self, refs, part=0):
         even_x = (jnp.zeros((8, LANES), jnp.int32) + lax.axis_index("gx") % 2) == 0
@@ -116,13 +123,16 @@
         self.packs = []
         for group in range(GROUPS):
             at = part * GROUPS + group
-            a, b, c, d = xa[at], xb[at], ya[at], yb[at]
+            a, b = xa[at], xb[at]
+            c, d, even = *(ref[rows_of(ref, group, part), :] for ref in (ya, yb)), even_y
+            if group == GROUPS - 1:
+                even = even_y[:4]
             self.packs.append(
                 (
                     jnp.where(even_x, b, a),
                     jnp.where(even_x, a, b),
-                    jnp.where(even_y, d, c),
-                    jnp.where(even_y, c, d),
+                    jnp.where(even, d, c),
+                    jnp.where(even, c, d),
                 )
             )
 
@@ -138,6 +148,11 @@
     def along_y(self, var):
         group, slot = divmod(var, 4)
         low, high = self.packs[group][2:]
+        if group == GROUPS - 1:
+            return (
+                jnp.concatenate([roll(low, -4 * k, 1) for k in range(4)], axis=0),
+                jnp.concatenate([roll(high, 4 * (3 - k), 1) for k in range(4)], axis=0),
+            )
         return roll(low, -4 * slot, 1), roll(high, 4 * (3 - slot), 1)
 
 
@@ -158,7 +173,9 @@
         own = [field(min(4 * group + slot, ENERGY)) for slot in range(4)]
         if group == GROUPS - 1:
             x_low, x_high = own[0][:8], roll(own[0][8:], -48, 1)
-            y_low, y_high = own[0], roll(own[0], -12, 1)
+            quarters = [own[0][4 * k : 4 * k + 4] for k in range(4)]
+            y_low = merged(spot_y[:4], [roll(quarters[k], 4 * k, 1) for k in range(4)])
+            y_high = merged(spot_y[:4], [roll(quarters[k], 4 * (k - 3), 1) for k in range(4)])
         else:
             x_low = merged(spot_x, [roll(own[s][:8], 16 * s, 1) for s in range(4)])
             x_high = merged(spot_x, [roll(own[s][8:], 16 * (s - 3), 1) for s in range(4)])
@@ -166,8 +183,9 @@
             y_high = merged(spot_y, [roll(own[s], 4 * (s - 3), 1) for s in range(4)])
         xa[at] = jnp.where(even_x, x_high, x_low)
         xb[at] = jnp.where(even_x, x_low, x_high)
-        ya[at] = jnp.where(even_y, y_high, y_low)
-        yb[at] = jnp.where(even_y, y_low, y_high)
+        even = even_y[:4] if group == GROUPS - 1 else even_y
+        ya[rows_of(ya, group, part), :] = jnp.where(even, y_high, y_low)
+        yb[rows_of(yb, group, part), :] = jnp.where(even, y_low, y_high)
 
 
 class Gas:
@@ -401,7 +419,11 @@
     if not last:
         pack(lambda v: out[v], (sa, sb, sc, sd))
         for held, sent in zip(along, (sa, sb, sc, sd)):
-            sent[GROUPS:] = held[...]
+            if len(held.shape) == 3:
+                sent[GROUPS:] = held[...]
+            else:
+                sent[96:192, :] = held[:96, :]
+                sent[196:200, :] = held[96:100, :]
 
 
 def back_volume_kernel(coupling, state, lam, near, walls, table, out, high, low, total):
@@ -500,7 +522,7 @@
 
 
 def packs(parts):
-    return [(parts * GROUPS, ROWS, LANES), (parts * GROUPS, 8, LANES), (parts * GROUPS, ROWS, LANES), (parts * GROUPS, 8, LANES)]
+    return [(parts * 100, LANES), (parts * GROUPS, 8, LANES), (parts * 100, LANES), (parts * GROUPS, 8, LANES)]
 
 
 def halved(width):

time: 51.2 us -> 50.4 us (0.984)
  starting transfers between devices: 33.4 us -> 32.6 us
    ppermute x20, starting transfers between devices: 33.4 us -> 32.6 us  [swap(): return lax.ppermute(values, ('gx', 'gy'), moves)]
where the time goes in v4:
time: 50.4 us; the launch traced here: 50.2 us
  starting transfers between devices  32.6 us (65%)
  Pallas kernels  11.9 us (24%)
  waiting for transfers between devices  4.89 us (10%)
  between operations  0.77 us (2%)
    ppermute x20, starting transfers between devices, swap(): return lax.ppermute(values, ('gx', 'gy'), moves)  32.6 us
    pallas_call x13, Pallas kernels, call(): pl.pallas_call(kernel, in_specs=[pl.BlockSpec(memory_space=pltpu.VMEM)] *...  10.6 us
    ppermute x20, waiting for transfers between devices, swap(): return lax.ppermute(values, ('gx', 'gy'), moves)  4.89 us
    pallas_call x1, Pallas kernels, per_device(): pl.pallas_call(functools.partial(start_kernel, len(held)), in_specs=[pl.B...  1.3 us
  transfers between devices with their start and end apart: 20, of which 5 were waited for; matrix products, arithmetic and copies ran while one was open for 0% of the time, Pallas kernels for 13%

profile of v4, /device:TPU:89, one launch (start us, length us, event | category | flops | bytes accessed | tf_op | source)
XLA Modules:
  0.0 50.2 jit_solution(16984390587055001990)
XLA Ops:
  0.6 1.3 %start_kernel.1 = (f32[25,16,128]{2,1,0:T(8,128)S(1)}, f32[25,16,128]{2,1,0:T(8,128)S(1)}, f32[21,21]{1,0:T(8,128)S(1)}, s32[2,1,16]{2,1,0:T(1,128)S(1)}, s32[3,...) custom-call(f32[25,16,128]{2,1,0:T(8,128)} %bitcast.5, ...), custom_call_target="tpu_custom_call" | custom-call | tf_op jit(solution)/shard_map/start_kernel/pallas_call | solution.py:571
  1.9 4.1 %collective-permute-start = (f32[100,128]{1,0:T(8,128)S(1)}, f32[100,128]{1,0:T(8,128)S(1)}, u32[]{:S(2)}, u32[]{:S(2)}) collective-permute-start(f32[100,128]{1,0:T(8,128)S(1)} %get-tuple-element.67), channel_id=1, source_target_pairs={{0,32},{1,2},{2,1},{3,4},{4,3},{5,6},{6,5},{7,8},{8,7},{9,10},{10,... | collective-permute-start | bytes 153608 | tf_op jit(solution)/shard_map/ppermute | solution.py:548
  6.0 4.1 %collective-permute-start.1 = (f32[7,8,128]{2,1,0:T(8,128)S(1)}, f32[7,8,128]{2,1,0:T(8,128)S(1)}, u32[]{:S(2)}, u32[]{:S(2)}) collective-permute-start(f32[7,8,128]{2,1,0:T(8,128)S(1)} %get-tuple-element.68), channel_id=1, source_target_pairs={{0,1},{1,0},{2,3},{3,2},{4,5},{5,4},{6,7},{7,6},{8,9},{9,8},{10,11... | collective-permute-start | bytes 86024 | tf_op jit(solution)/shard_map/ppermute | solution.py:548
  10.2 0.5 setup_kernel.1
  10.7 0.0 copy-start.1
  10.7 0.9 %volume_kernel.3 = (f32[25,16,128]{2,1,0:T(8,128)S(1)}, f32[25,16,128]{2,1,0:T(8,128)S(1)}) custom-call(f32[21,21,128]{2,1,0:T(8,128)S(1)} %get-tuple-element.62.coupling, f32[25,16,128]{2,1,0:T(8,128)S(1)} %get-tuple-element.55.state.start, f32[25,16,128]{2,1,0:T(8,128)S(1)} %get-tuple-element.55.state.start, f32[3,16,128]{2,1,0:T(8,128)S(1)} %get-tuple-element.63.walls, ...), custom_call_target="tpu_custom_call" | custom-call | tf_op jit(solution)/shard_map/volume_kernel/pallas_call | solution.py:513
  11.6 0.2 collective-permute-done.1.refs_1_
  11.8 0.6 %face_kernel.3 = (f32[25,16,128]{2,1,0:T(8,128)S(1)}, f32[25,16,128]{2,1,0:T(8,128)S(1)}, f32[25,16,128]{2,1,0:T(8,128)S(1)}, f32[100,128]{1,0:T(8,128)S(1)}, f3...) custom-call(f32[25,16,128]{2,1,0:T(8,128)S(1)} %get-tuple-element.55.state.start, ...), custom_call_target="tpu_custom_call" | custom-call | tf_op jit(solution)/shard_map/face_kernel/pallas_call | solution.py:513
  12.4 2.7 %collective-permute-start.4 = (f32[100,128]{1,0:T(8,128)S(1)}, f32[100,128]{1,0:T(8,128)S(1)}, u32[]{:S(2)}, u32[]{:S(2)}) collective-permute-start(f32[100,128]{1,0:T(8,128)S(1)} %get-tuple-element.73), channel_id=1, source_target_pairs={{0,32},{1,2},{2,1},{3,4},{4,3},{5,6},{6,5},{7,8},{8,7},{9,10},{10,... | collective-permute-start | bytes 153608 | tf_op jit(solution)/shard_map/ppermute | solution.py:548
  15.0 0.1 collective-permute-start.6
  15.2 3.6 %collective-permute-start.5 = (f32[7,8,128]{2,1,0:T(8,128)S(1)}, f32[7,8,128]{2,1,0:T(8,128)S(1)}, u32[]{:S(2)}, u32[]{:S(2)}) collective-permute-start(f32[7,8,128]{2,1,0:T(8,128)S(1)} %get-tuple-element.74), channel_id=1, source_target_pairs={{0,1},{1,0},{2,3},{3,2},{4,5},{5,4},{6,7},{7,6},{8,9},{9,8},{10,11... | collective-permute-start | bytes 86024 | tf_op jit(solution)/shard_map/ppermute | solution.py:548
  18.8 0.9 %volume_kernel.4 = (f32[25,16,128]{2,1,0:T(8,128)S(1)}, f32[25,16,128]{2,1,0:T(8,128)S(1)}) custom-call(f32[21,21,128]{2,1,0:T(8,128)S(1)} %get-tuple-element.62.coupling, f32[25,16,128]{2,1,0:T(8,128)S(1)} %get-tuple-element.71.state, f32[25,16,128]{2,1,0:T(8,128)S(1)} %get-tuple-element.55.state.start, f32[3,16,128]{2,1,0:T(8,128)S(1)} %get-tuple-element.63.walls, ...), custom_call_target="tpu_custom_call" | custom-call | tf_op jit(solution)/shard_map/volume_kernel/pallas_call | solution.py:513
  19.8 0.8 %collective-permute-done.5.refs_1_ = f32[7,8,128]{2,1,0:T(8,128)S(1)} collective-permute-done((f32[7,8,128]{2,1,0:T(8,128)S(1)}, f32[7,8,128]{2,1,0:T(8,128)S(1)}, u32[]{:S(2)}, u32[]{:S(2)}) %collective-permute-start.5) | collective-permute-done | bytes 28704 | tf_op jit(solution)/shard_map/ppermute | solution.py:548
  20.6 0.6 %face_kernel.4 = (f32[25,16,128]{2,1,0:T(8,128)S(1)}, f32[25,16,128]{2,1,0:T(8,128)S(1)}, f32[25,16,128]{2,1,0:T(8,128)S(1)}, f32[200,128]{1,0:T(8,128)S(1)}, f3...) custom-call(f32[25,16,128]{2,1,0:T(8,128)S(1)} %get-tuple-element.71.state, ...), custom_call_target="tpu_custom_call" | custom-call | tf_op jit(solution)/shard_map/face_kernel/pallas_call | solution.py:513
  21.2 3.6 %collective-permute-start.8 = (f32[200,128]{1,0:T(8,128)S(1)}, f32[200,128]{1,0:T(8,128)S(1)}, u32[]{:S(2)}, u32[]{:S(2)}) collective-permute-start(f32[200,128]{1,0:T(8,128)S(1)} %get-tuple-element.85), channel_id=1, source_target_pairs={{0,32},{1,2},{2,1},{3,4},{4,3},{5,6},{6,5},{7,8},{8,7},{9,10},{10,... | collective-permute-start | bytes 307208 | tf_op jit(solution)/shard_map/ppermute | solution.py:548
  24.8 2.8 %collective-permute-start.9 = (f32[14,8,128]{2,1,0:T(8,128)S(1)}, f32[14,8,128]{2,1,0:T(8,128)S(1)}, u32[]{:S(2)}, u32[]{:S(2)}) collective-permute-start(f32[14,8,128]{2,1,0:T(8,128)S(1)} %get-tuple-element.86), channel_id=1, source_target_pairs={{0,1},{1,0},{2,3},{3,2},{4,5},{5,4},{6,7},{7,6},{8,9},{9,8},{10,11... | collective-permute-start | bytes 172040 | tf_op jit(solution)/shard_map/ppermute | solution.py:548
  27.6 0.0 collective-permute-start.11
  27.6 0.9 %volume_kernel.5 = (f32[25,16,128]{2,1,0:T(8,128)S(1)}, f32[25,16,128]{2,1,0:T(8,128)S(1)}) custom-call(f32[21,21,128]{2,1,0:T(8,128)S(1)} %get-tuple-element.62.coupling, f32[25,16,128]{2,1,0:T(8,128)S(1)} %get-tuple-element.81.state, f32[25,16,128]{2,1,0:T(8,128)S(1)} %get-tuple-element.55.state.start, f32[3,16,128]{2,1,0:T(8,128)S(1)} %get-tuple-element.63.walls, ...), custom_call_target="tpu_custom_call" | custom-call | tf_op jit(solution)/shard_map/volume_kernel/pallas_call | solution.py:513
  28.6 0.8 %back_volume_kernel.3.inner = f32[25,16,128]{2,1,0:T(8,128)S(1)} custom-call(f32[21,21,128]{2,1,0:T(8,128)S(1)} %get-tuple-element.62.coupling, f32[25,16,128]{2,1,0:T(8,128)S(1)} %get-tuple-element.81.state, f32[25,16,128]{2,1,0:T(8,128)S(1)} %get-tuple-element.83.lam, f32[25,16,128]{2,1,0:T(8,128)S(1)} %get-tuple-element.84.near, ...), custom_call_target="tpu_custom_call" | custom-call | tf_op jit(solution)/shard_map/back_volume_kernel/pallas_call | solution.py:513
  29.4 1.1 %collective-permute-done.9.refs_1_ = f32[14,8,128]{2,1,0:T(8,128)S(1)} collective-permute-done((f32[14,8,128]{2,1,0:T(8,128)S(1)}, f32[14,8,128]{2,1,0:T(8,128)S(1)}, u32[]{:S(2)}, u32[]{:S(2)}) %collective-permute-start.9) | collective-permute-done | bytes 57376 | tf_op jit(solution)/shard_map/ppermute | solution.py:548
  30.5 0.9 %turn_kernel.1 = (f32[25,16,128]{2,1,0:T(8,128)S(1)}, f32[25,16,128]{2,1,0:T(8,128)S(1)}, f32[25,16,128]{2,1,0:T(8,128)S(1)}, f32[25,16,128]{2,1,0:T(8,128)S(1)}...) custom-call(f32[25,16,128]{2,1,0:T(8,128)S(1)} %get-tuple-element.81.sta, ...), custom_call_target="tpu_custom_call" | custom-call | tf_op jit(solution)/shard_map/turn_kernel/pallas_call | solution.py:513
  31.4 3.9 %collective-permute-start.12 = (f32[100,128]{1,0:T(8,128)S(1)}, f32[100,128]{1,0:T(8,128)S(1)}, u32[]{:S(2)}, u32[]{:S(2)}) collective-permute-start(f32[100,128]{1,0:T(8,128)S(1)} %get-tuple-element.95), channel_id=1, source_target_pairs={{0,32},{1,2},{2,1},{3,4},{4,3},{5,6},{6,5},{7,8},{8,7},{9,10},{10,... | collective-permute-start | bytes 153608 | tf_op jit(solution)/shard_map/ppermute | solution.py:548
  35.3 2.3 %collective-permute-start.13 = (f32[7,8,128]{2,1,0:T(8,128)S(1)}, f32[7,8,128]{2,1,0:T(8,128)S(1)}, u32[]{:S(2)}, u32[]{:S(2)}) collective-permute-start(f32[7,8,128]{2,1,0:T(8,128)S(1)} %get-tuple-element.96), channel_id=1, source_target_pairs={{0,1},{1,0},{2,3},{3,2},{4,5},{5,4},{6,7},{7,6},{8,9},{9,8},{10,11... | collective-permute-start | bytes 86024 | tf_op jit(solution)/shard_map/ppermute | solution.py:548
  37.6 0.8 %back_volume_kernel.4.inner = f32[25,16,128]{2,1,0:T(8,128)S(1)} custom-call(f32[21,21,128]{2,1,0:T(8,128)S(1)} %get-tuple-element.62.coupling, f32[25,16,128]{2,1,0:T(8,128)S(1)} %get-tuple-element.71.state, f32[25,16,128]{2,1,0:T(8,128)S(1)} %get-tuple-element.91.lam, f32[25,16,128]{2,1,0:T(8,128)S(1)} %get-tuple-element.92.near, ...), custom_call_target="tpu_custom_call" | custom-call | tf_op jit(solution)/shard_map/back_volume_kernel/pallas_call | solution.py:513
  38.5 2.3 %collective-permute-done.13.refs_1_ = f32[7,8,128]{2,1,0:T(8,128)S(1)} collective-permute-done((f32[7,8,128]{2,1,0:T(8,128)S(1)}, f32[7,8,128]{2,1,0:T(8,128)S(1)}, u32[]{:S(2)}, u32[]{:S(2)}) %collective-permute-start.13) | collective-permute-done | bytes 28704 | tf_op jit(solution)/shard_map/ppermute | solution.py:548
  40.8 0.7 %middle_kernel.1 = (f32[25,16,128]{2,1,0:T(8,128)S(1)}, f32[100,128]{1,0:T(8,128)S(1)}, f32[7,8,128]{2,1,0:T(8,128)S(1)}, f32[100,128]{1,0:T(8,128)S(1)}, f32[7,8,128]{2,1,0:T(8,128)S(1)}) custom-call(f32[25,16,128]{2,1,0:T(8,128)S(1)} %get-tuple-element.71.state, f32[25,16,128]{2,1,0:T(8,128)S(1)} %get-tuple-element.91.lam, ...), custom_call_target="tpu_custom_call" | custom-call | tf_op jit(solution)/shard_map/middle_kernel/pallas_call | solution.py:513
  41.5 2.2 %collective-permute-start.16 = (f32[100,128]{1,0:T(8,128)S(1)}, f32[100,128]{1,0:T(8,128)S(1)}, u32[]{:S(2)}, u32[]{:S(2)}) collective-permute-start(f32[100,128]{1,0:T(8,128)S(1)} %get-tuple-element.104), channel_id=1, source_target_pairs={{0,32},{1,2},{2,1},{3,4},{4,3},{5,6},{6,5},{7,8},{8,7},{9,10},{10,... | collective-permute-start | bytes 153608 | tf_op jit(solution)/shard_map/ppermute | solution.py:548
  43.7 3.1 %collective-permute-start.17 = (f32[7,8,128]{2,1,0:T(8,128)S(1)}, f32[7,8,128]{2,1,0:T(8,128)S(1)}, u32[]{:S(2)}, u32[]{:S(2)}) collective-permute-start(f32[7,8,128]{2,1,0:T(8,128)S(1)} %get-tuple-element.105), channel_id=1, source_target_pairs={{0,1},{1,0},{2,3},{3,2},{4,5},{5,4},{6,7},{7,6},{8,9},{9,8},{10,11... | collective-permute-start | bytes 86024 | tf_op jit(solution)/shard_map/ppermute | solution.py:548
  46.8 1.0 %face_kernel.5 = f32[25,16,128]{2,1,0:T(8,128)} custom-call(f32[25,16,128]{2,1,0:T(8,128)S(1)} %get-tuple-element.81.state, f32[25,16,128]{2,1,0:T(8,128)S(1)} %get-tuple-element.82.inner, f32[3,16,128]{2,1,0:T(8,128)S(1)} %get-tuple-element.63.walls, f32[3,16,128]{2,1,0:T(8,128)S(1)} %get-tuple-element.66.factors, bf16[256,128]{1,0:T(8,128)(2,1)S(1)} %copy-done.1, ...), custom_call_target="tpu_custom_call" | custom-call | tf_op jit(solution)/shard_map/face_kernel/pallas_call | solution.py:513
  47.8 0.8 %back_volume_kernel.5.inner = f32[25,16,128]{2,1,0:T(8,128)S(1)} custom-call(f32[21,21,128]{2,1,0:T(8,128)S(1)} %get-tuple-element.62.coupling, f32[25,16,128]{2,1,0:T(8,128)S(1)} %get-tuple-element.55.state.start, f32[25,16,128]{2,1,0:T(8,128)S(1)} %get-tuple-element.99.lam, f32[25,16,128]{2,1,0:T(8,128)S(1)} %get-tuple-element.100.near, ...), custom_call_target="tpu_custom_call" | custom-call | tf_op jit(solution)/shard_map/back_volume_kernel/pallas_call | solution.py:513
  48.6 0.5 collective-permute-done.17.lb
  49.1 1.1 %end_kernel.1 = f32[25,16,128]{2,1,0:T(8,128)} custom-call(f32[25,16,128]{2,1,0:T(8,128)S(1)} %get-tuple-element.55.state.start, f32[25,16,128]{2,1,0:T(8,128)S(1)} %get-tuple-element.99.lam, f32[25,16,128]{2,1,0:T(8,128)S(1)} %back_volume_kernel.5.inner, f32[25,16,128]{2,1,0:T(8,128)S(1)} %get-tuple-element.101.near_x, ...), custom_call_target="tpu_custom_call" | custom-call | tf_op jit(solution)/shard_map/end_kernel/pallas_call | solution.py:513
  (26 shorter events, 0.1 us)
Async XLA Ops:
  1.9 9.8 %collective-permute-start = (f32[100,128]{1,0:T(8,128)S(1)}, f32[100,128]{1,0:T(8,128)S(1)}, u32[]{:S(2)}, u32[]{:S(2)}) collective-permute-start(f32[100,128]{1,0:T(8,128)S(1)} %get-tuple-element.67), channel_id=1, source_target_pairs={{0,32},{1,2},{2,1},{3,4},{4,3},{5,6},{6,5},{7,8},{8,7},{9,10},{10,... | collective-permute-start | bytes 153608 | tf_op jit(solution)/shard_map/ppermute | solution.py:548
  6.0 5.7 %collective-permute-start.2 = (f32[100,128]{1,0:T(8,128)S(1)}, f32[100,128]{1,0:T(8,128)S(1)}, u32[]{:S(2)}, u32[]{:S(2)}) collective-permute-start(f32[100,128]{1,0:T(8,128)S(1)} %get-tuple-element.69), channel_id=1, source_target_pairs={{0,1},{1,0},{2,3},{3,2},{4,5},{5,4},{6,7},{7,6},{8,9},{9,8},{10,11... | collective-permute-start | bytes 153608 | tf_op jit(solution)/shard_map/ppermute | solution.py:548
  6.0 5.7 %collective-permute-start.1 = (f32[7,8,128]{2,1,0:T(8,128)S(1)}, f32[7,8,128]{2,1,0:T(8,128)S(1)}, u32[]{:S(2)}, u32[]{:S(2)}) collective-permute-start(f32[7,8,128]{2,1,0:T(8,128)S(1)} %get-tuple-element.68), channel_id=1, source_target_pairs={{0,1},{1,0},{2,3},{3,2},{4,5},{5,4},{6,7},{7,6},{8,9},{9,8},{10,11... | collective-permute-start | bytes 86024 | tf_op jit(solution)/shard_map/ppermute | solution.py:548
  10.2 1.6 %collective-permute-start.3 = (f32[7,8,128]{2,1,0:T(8,128)S(1)}, f32[7,8,128]{2,1,0:T(8,128)S(1)}, u32[]{:S(2)}, u32[]{:S(2)}) collective-permute-start(f32[7,8,128]{2,1,0:T(8,128)S(1)} %get-tuple-element.70), channel_id=1, source_target_pairs={{0,32},{1,33},{2,34},{3,35},{4,36},{5,37},{6,38},{7,39},{8,40},{9,... | collective-permute-start | bytes 86024 | tf_op jit(solution)/shard_map/ppermute | solution.py:548
  10.7 1.1 %copy-start.1 = (bf16[256,128]{1,0:T(8,128)(2,1)S(1)}, bf16[256,128]{1,0:T(8,128)(2,1)}, u32[]{:S(2)}) copy-start(bf16[256,128]{1,0:T(8,128)(2,1)} %constant.10.clone.mean) | copy-start | bytes 196612
  12.4 8.2 %collective-permute-start.4 = (f32[100,128]{1,0:T(8,128)S(1)}, f32[100,128]{1,0:T(8,128)S(1)}, u32[]{:S(2)}, u32[]{:S(2)}) collective-permute-start(f32[100,128]{1,0:T(8,128)S(1)} %get-tuple-element.73), channel_id=1, source_target_pairs={{0,32},{1,2},{2,1},{3,4},{4,3},{5,6},{6,5},{7,8},{8,7},{9,10},{10,... | collective-permute-start | bytes 153608 | tf_op jit(solution)/shard_map/ppermute | solution.py:548
  15.0 5.6 %collective-permute-start.6 = (f32[100,128]{1,0:T(8,128)S(1)}, f32[100,128]{1,0:T(8,128)S(1)}, u32[]{:S(2)}, u32[]{:S(2)}) collective-permute-start(f32[100,128]{1,0:T(8,128)S(1)} %get-tuple-element.75), channel_id=1, source_target_pairs={{0,1},{1,0},{2,3},{3,2},{4,5},{5,4},{6,7},{7,6},{8,9},{9,8},{10,11... | collective-permute-start | bytes 153608 | tf_op jit(solution)/shard_map/ppermute | solution.py:548
  15.2 5.4 %collective-permute-start.5 = (f32[7,8,128]{2,1,0:T(8,128)S(1)}, f32[7,8,128]{2,1,0:T(8,128)S(1)}, u32[]{:S(2)}, u32[]{:S(2)}) collective-permute-start(f32[7,8,128]{2,1,0:T(8,128)S(1)} %get-tuple-element.74), channel_id=1, source_target_pairs={{0,1},{1,0},{2,3},{3,2},{4,5},{5,4},{6,7},{7,6},{8,9},{9,8},{10,11... | collective-permute-start | bytes 86024 | tf_op jit(solution)/shard_map/ppermute | solution.py:548
  18.8 1.8 %collective-permute-start.7 = (f32[7,8,128]{2,1,0:T(8,128)S(1)}, f32[7,8,128]{2,1,0:T(8,128)S(1)}, u32[]{:S(2)}, u32[]{:S(2)}) collective-permute-start(f32[7,8,128]{2,1,0:T(8,128)S(1)} %get-tuple-element.76), channel_id=1, source_target_pairs={{0,32},{1,33},{2,34},{3,35},{4,36},{5,37},{6,38},{7,39},{8,40},{9,... | collective-permute-start | bytes 86024 | tf_op jit(solution)/shard_map/ppermute | solution.py:548
  21.2 9.3 %collective-permute-start.8 = (f32[200,128]{1,0:T(8,128)S(1)}, f32[200,128]{1,0:T(8,128)S(1)}, u32[]{:S(2)}, u32[]{:S(2)}) collective-permute-start(f32[200,128]{1,0:T(8,128)S(1)} %get-tuple-element.85), channel_id=1, source_target_pairs={{0,32},{1,2},{2,1},{3,4},{4,3},{5,6},{6,5},{7,8},{8,7},{9,10},{10,... | collective-permute-start | bytes 307208 | tf_op jit(solution)/shard_map/ppermute | solution.py:548
  24.8 5.7 %collective-permute-start.10 = (f32[200,128]{1,0:T(8,128)S(1)}, f32[200,128]{1,0:T(8,128)S(1)}, u32[]{:S(2)}, u32[]{:S(2)}) collective-permute-start(f32[200,128]{1,0:T(8,128)S(1)} %get-tuple-element.87), channel_id=1, source_target_pairs={{0,1},{1,0},{2,3},{3,2},{4,5},{5,4},{6,7},{7,6},{8,9},{9,8},{10,11... | collective-permute-start | bytes 307208 | tf_op jit(solution)/shard_map/ppermute | solution.py:548
  24.8 5.7 %collective-permute-start.9 = (f32[14,8,128]{2,1,0:T(8,128)S(1)}, f32[14,8,128]{2,1,0:T(8,128)S(1)}, u32[]{:S(2)}, u32[]{:S(2)}) collective-permute-start(f32[14,8,128]{2,1,0:T(8,128)S(1)} %get-tuple-element.86), channel_id=1, source_target_pairs={{0,1},{1,0},{2,3},{3,2},{4,5},{5,4},{6,7},{7,6},{8,9},{9,8},{10,11... | collective-permute-start | bytes 172040 | tf_op jit(solution)/shard_map/ppermute | solution.py:548
  27.6 2.9 %collective-permute-start.11 = (f32[14,8,128]{2,1,0:T(8,128)S(1)}, f32[14,8,128]{2,1,0:T(8,128)S(1)}, u32[]{:S(2)}, u32[]{:S(2)}) collective-permute-start(f32[14,8,128]{2,1,0:T(8,128)S(1)} %get-tuple-element.88), channel_id=1, source_target_pairs={{0,32},{1,33},{2,34},{3,35},{4,36},{5,37},{6,38},{7,39},{8,40},{9,... | collective-permute-start | bytes 172040 | tf_op jit(solution)/shard_map/ppermute | solution.py:548
  27.6 0.9 %copy-start = (bf16[2,128,384]{2,1,0:T(8,128)(2,1)S(1)}, bf16[2,128,384]{2,1,0:T(8,128)(2,1)}, u32[]{:S(2)}) copy-start(bf16[2,128,384]{2,1,0:T(8,128)(2,1)} %constant.9.clone.table) | copy-start | bytes 589828
  31.4 9.3 %collective-permute-start.12 = (f32[100,128]{1,0:T(8,128)S(1)}, f32[100,128]{1,0:T(8,128)S(1)}, u32[]{:S(2)}, u32[]{:S(2)}) collective-permute-start(f32[100,128]{1,0:T(8,128)S(1)} %get-tuple-element.95), channel_id=1, source_target_pairs={{0,32},{1,2},{2,1},{3,4},{4,3},{5,6},{6,5},{7,8},{8,7},{9,10},{10,... | collective-permute-start | bytes 153608 | tf_op jit(solution)/shard_map/ppermute | solution.py:548
  35.3 5.4 %collective-permute-start.14 = (f32[100,128]{1,0:T(8,128)S(1)}, f32[100,128]{1,0:T(8,128)S(1)}, u32[]{:S(2)}, u32[]{:S(2)}) collective-permute-start(f32[100,128]{1,0:T(8,128)S(1)} %get-tuple-element.97), channel_id=1, source_target_pairs={{0,1},{1,0},{2,3},{3,2},{4,5},{5,4},{6,7},{7,6},{8,9},{9,8},{10,11... | collective-permute-start | bytes 153608 | tf_op jit(solution)/shard_map/ppermute | solution.py:548
  35.3 5.4 %collective-permute-start.13 = (f32[7,8,128]{2,1,0:T(8,128)S(1)}, f32[7,8,128]{2,1,0:T(8,128)S(1)}, u32[]{:S(2)}, u32[]{:S(2)}) collective-permute-start(f32[7,8,128]{2,1,0:T(8,128)S(1)} %get-tuple-element.96), channel_id=1, source_target_pairs={{0,1},{1,0},{2,3},{3,2},{4,5},{5,4},{6,7},{7,6},{8,9},{9,8},{10,11... | collective-permute-start | bytes 86024 | tf_op jit(solution)/shard_map/ppermute | solution.py:548
  37.6 3.1 %collective-permute-start.15 = (f32[7,8,128]{2,1,0:T(8,128)S(1)}, f32[7,8,128]{2,1,0:T(8,128)S(1)}, u32[]{:S(2)}, u32[]{:S(2)}) collective-permute-start(f32[7,8,128]{2,1,0:T(8,128)S(1)} %get-tuple-element.98), channel_id=1, source_target_pairs={{0,32},{1,33},{2,34},{3,35},{4,36},{5,37},{6,38},{7,39},{8,40},{9,... | collective-permute-start | bytes 86024 | tf_op jit(solution)/shard_map/ppermute | solution.py:548
  41.5 7.6 %collective-permute-start.16 = (f32[100,128]{1,0:T(8,128)S(1)}, f32[100,128]{1,0:T(8,128)S(1)}, u32[]{:S(2)}, u32[]{:S(2)}) collective-permute-start(f32[100,128]{1,0:T(8,128)S(1)} %get-tuple-element.104), channel_id=1, source_target_pairs={{0,32},{1,2},{2,1},{3,4},{4,3},{5,6},{6,5},{7,8},{8,7},{9,10},{10,... | collective-permute-start | bytes 153608 | tf_op jit(solution)/shard_map/ppermute | solution.py:548
  43.7 5.4 %collective-permute-start.18 = (f32[100,128]{1,0:T(8,128)S(1)}, f32[100,128]{1,0:T(8,128)S(1)}, u32[]{:S(2)}, u32[]{:S(2)}) collective-permute-start(f32[100,128]{1,0:T(8,128)S(1)} %get-tuple-element.106), channel_id=1, source_target_pairs={{0,1},{1,0},{2,3},{3,2},{4,5},{5,4},{6,7},{7,6},{8,9},{9,8},{10,11... | collective-permute-start | bytes 153608 | tf_op jit(solution)/shard_map/ppermute | solution.py:548
  43.7 5.4 %collective-permute-start.17 = (f32[7,8,128]{2,1,0:T(8,128)S(1)}, f32[7,8,128]{2,1,0:T(8,128)S(1)}, u32[]{:S(2)}, u32[]{:S(2)}) collective-permute-start(f32[7,8,128]{2,1,0:T(8,128)S(1)} %get-tuple-element.105), channel_id=1, source_target_pairs={{0,1},{1,0},{2,3},{3,2},{4,5},{5,4},{6,7},{7,6},{8,9},{9,8},{10,11... | collective-permute-start | bytes 86024 | tf_op jit(solution)/shard_map/ppermute | solution.py:548
  46.8 2.3 %collective-permute-start.19 = (f32[7,8,128]{2,1,0:T(8,128)S(1)}, f32[7,8,128]{2,1,0:T(8,128)S(1)}, u32[]{:S(2)}, u32[]{:S(2)}) collective-permute-start(f32[7,8,128]{2,1,0:T(8,128)S(1)} %get-tuple-element.107), channel_id=1, source_target_pairs={{0,32},{1,33},{2,34},{3,35},{4,36},{5,37},{6,38},{7,39},{8,40},{9,... | collective-permute-start | bytes 86024 | tf_op jit(solution)/shard_map/ppermute | solution.py:548

commit v5 on v4

--- a/solution.py
+++ b/solution.py
@@ -455,7 +455,7 @@
         out[var] = lam[var] + STEP * change
 
 
-def back_faces(state, lam, near_x, near_y, walls, received, inner, out):
+def back_faces(state, lam, near_x, near_y, walls, received, inner, out, carry=None):
     gas = Gas(lambda v: state[v], (0, 1))
     faces = (Face(walls[0], 0), Face(walls[1], 1))
     nears = (near_x, near_y)
@@ -474,7 +474,8 @@
         out[var] = part
     back.close()
     for var in range(VARS):
-        out[var] = out[var] + STEP * back.rest(var)
+        total = out[var] + STEP * back.rest(var)
+        out[var] = total if carry is None else total + carry[var]
 
 
 def turn_kernel(state, lam, inner, walls, factors, mean_t, *refs):
@@ -500,9 +501,7 @@
 
 
 def end_kernel(state, lam, inner, near_x, near_y, carry, walls, la, lb, lc, ld, out):
-    back_faces(state, lam, near_x, near_y, walls, Received((la, lb, lc, ld)), inner, out)
-    for var in range(VARS):
-        out[var] = out[var] + carry[var]
+    back_faces(state, lam, near_x, near_y, walls, Received((la, lb, lc, ld)), inner, out, carry)
 
 
 FIELD = (VARS, ROWS, LANES)
@@ -567,7 +566,7 @@
     work = [pltpu.VMEM(FIELD, F32)]
 
     held = [q0, adjoint, reaction_rates, face_codes, limiter_flags, limiter_scales]
-    held += [mean_t, forward]
+    held += [mean_t]
     got = pl.pallas_call(
         functools.partial(start_kernel, len(held)),
         in_specs=[pl.BlockSpec(memory_space=pltpu.HBM)] * len(held),
@@ -578,7 +577,7 @@
         compiler_params=pltpu.CompilerParams(vmem_limit_bytes=8 << 20),
         name="start_kernel",
     )(*[pltpu.with_memory_space_constraint(v, pltpu.HBM) for v in held])
-    q0, adjoint, rates, codes, flags, scales, mean_t, forward = got[: len(held)]
+    q0, adjoint, rates, codes, flags, scales, mean_t = got[: len(held)]
     got = exchange(got[len(held) :])
     size = functools.partial(setup_kernel, lax.axis_size("gx"), lax.axis_size("gy"))
     lam3, *along, walls, factors, coupling = call(

time: 50.4 us -> 50.3 us (level)
  no operation moved by 1% of the time
where the time goes in v5:
time: 50.3 us; the launch traced here: 50.1 us
  starting transfers between devices  32.6 us (65%)
  Pallas kernels  11.8 us (23%)
  waiting for transfers between devices  4.88 us (10%)
  between operations  0.79 us (2%)
    ppermute x20, starting transfers between devices, swap(): return lax.ppermute(values, ('gx', 'gy'), moves)  32.6 us
    pallas_call x13, Pallas kernels, call(): pl.pallas_call(kernel, in_specs=[pl.BlockSpec(memory_space=pltpu.VMEM)] *...  10.6 us
    ppermute x20, waiting for transfers between devices, swap(): return lax.ppermute(values, ('gx', 'gy'), moves)  4.88 us
    pallas_call x1, Pallas kernels, per_device(): pl.pallas_call(functools.partial(start_kernel, len(held)), in_specs=[pl.B...  1.2 us
  transfers between devices with their start and end apart: 20, of which 5 were waited for; matrix products, arithmetic and copies ran while one was open for 0% of the time, Pallas kernels for 13%

profile of v5, /device:TPU:89, one launch (start us, length us, event | category | flops | bytes accessed | tf_op | source)
XLA Modules:
  0.0 50.1 jit_solution(6196276288229132545)
XLA Ops:
  0.6 1.2 %start_kernel.1 = (f32[25,16,128]{2,1,0:T(8,128)S(1)}, f32[25,16,128]{2,1,0:T(8,128)S(1)}, f32[21,21]{1,0:T(8,128)S(1)}, s32[2,1,16]{2,1,0:T(1,128)S(1)}, s32[3,...) custom-call(f32[25,16,128]{2,1,0:T(8,128)} %bitcast.5, ...), custom_call_target="tpu_custom_call" | custom-call | tf_op jit(solution)/shard_map/start_kernel/pallas_call | solution.py:570
  1.8 0.0 copy-start.1
  1.9 4.1 %collective-permute-start = (f32[100,128]{1,0:T(8,128)S(1)}, f32[100,128]{1,0:T(8,128)S(1)}, u32[]{:S(2)}, u32[]{:S(2)}) collective-permute-start(f32[100,128]{1,0:T(8,128)S(1)} %get-tuple-element.65), channel_id=1, source_target_pairs={{0,32},{1,2},{2,1},{3,4},{4,3},{5,6},{6,5},{7,8},{8,7},{9,10},{10,... | collective-permute-start | bytes 153608 | tf_op jit(solution)/shard_map/ppermute | solution.py:547
  6.0 4.1 %collective-permute-start.1 = (f32[7,8,128]{2,1,0:T(8,128)S(1)}, f32[7,8,128]{2,1,0:T(8,128)S(1)}, u32[]{:S(2)}, u32[]{:S(2)}) collective-permute-start(f32[7,8,128]{2,1,0:T(8,128)S(1)} %get-tuple-element.66), channel_id=1, source_target_pairs={{0,1},{1,0},{2,3},{3,2},{4,5},{5,4},{6,7},{7,6},{8,9},{9,8},{10,11... | collective-permute-start | bytes 86024 | tf_op jit(solution)/shard_map/ppermute | solution.py:547
  10.1 0.5 setup_kernel.1
  10.6 0.0 copy-start.2
  10.6 0.9 %volume_kernel.3 = (f32[25,16,128]{2,1,0:T(8,128)S(1)}, f32[25,16,128]{2,1,0:T(8,128)S(1)}) custom-call(f32[21,21,128]{2,1,0:T(8,128)S(1)} %get-tuple-element.61.coupling, f32[25,16,128]{2,1,0:T(8,128)S(1)} %get-tuple-element.54.state.start, f32[25,16,128]{2,1,0:T(8,128)S(1)} %get-tuple-element.54.state.start, f32[3,16,128]{2,1,0:T(8,128)S(1)} %get-tuple-element.62.walls, ...), custom_call_target="tpu_custom_call" | custom-call | tf_op jit(solution)/shard_map/volume_kernel/pallas_call | solution.py:512
  11.5 0.2 collective-permute-done.1.refs_1_
  11.7 0.6 %face_kernel.3 = (f32[25,16,128]{2,1,0:T(8,128)S(1)}, f32[25,16,128]{2,1,0:T(8,128)S(1)}, f32[25,16,128]{2,1,0:T(8,128)S(1)}, f32[100,128]{1,0:T(8,128)S(1)}, f3...) custom-call(f32[25,16,128]{2,1,0:T(8,128)S(1)} %get-tuple-element.54.state.start, ...), custom_call_target="tpu_custom_call" | custom-call | tf_op jit(solution)/shard_map/face_kernel/pallas_call | solution.py:512
  12.3 2.7 %collective-permute-start.4 = (f32[100,128]{1,0:T(8,128)S(1)}, f32[100,128]{1,0:T(8,128)S(1)}, u32[]{:S(2)}, u32[]{:S(2)}) collective-permute-start(f32[100,128]{1,0:T(8,128)S(1)} %get-tuple-element.71), channel_id=1, source_target_pairs={{0,32},{1,2},{2,1},{3,4},{4,3},{5,6},{6,5},{7,8},{8,7},{9,10},{10,... | collective-permute-start | bytes 153608 | tf_op jit(solution)/shard_map/ppermute | solution.py:547
  15.0 0.1 collective-permute-start.6
  15.1 3.6 %collective-permute-start.5 = (f32[7,8,128]{2,1,0:T(8,128)S(1)}, f32[7,8,128]{2,1,0:T(8,128)S(1)}, u32[]{:S(2)}, u32[]{:S(2)}) collective-permute-start(f32[7,8,128]{2,1,0:T(8,128)S(1)} %get-tuple-element.72), channel_id=1, source_target_pairs={{0,1},{1,0},{2,3},{3,2},{4,5},{5,4},{6,7},{7,6},{8,9},{9,8},{10,11... | collective-permute-start | bytes 86024 | tf_op jit(solution)/shard_map/ppermute | solution.py:547
  18.8 0.9 %volume_kernel.4 = (f32[25,16,128]{2,1,0:T(8,128)S(1)}, f32[25,16,128]{2,1,0:T(8,128)S(1)}) custom-call(f32[21,21,128]{2,1,0:T(8,128)S(1)} %get-tuple-element.61.coupling, f32[25,16,128]{2,1,0:T(8,128)S(1)} %get-tuple-element.69.state, f32[25,16,128]{2,1,0:T(8,128)S(1)} %get-tuple-element.54.state.start, f32[3,16,128]{2,1,0:T(8,128)S(1)} %get-tuple-element.62.walls, ...), custom_call_target="tpu_custom_call" | custom-call | tf_op jit(solution)/shard_map/volume_kernel/pallas_call | solution.py:512
  19.7 0.8 %collective-permute-done.5.refs_1_ = f32[7,8,128]{2,1,0:T(8,128)S(1)} collective-permute-done((f32[7,8,128]{2,1,0:T(8,128)S(1)}, f32[7,8,128]{2,1,0:T(8,128)S(1)}, u32[]{:S(2)}, u32[]{:S(2)}) %collective-permute-start.5) | collective-permute-done | bytes 28704 | tf_op jit(solution)/shard_map/ppermute | solution.py:547
  20.5 0.6 %face_kernel.4 = (f32[25,16,128]{2,1,0:T(8,128)S(1)}, f32[25,16,128]{2,1,0:T(8,128)S(1)}, f32[25,16,128]{2,1,0:T(8,128)S(1)}, f32[200,128]{1,0:T(8,128)S(1)}, f3...) custom-call(f32[25,16,128]{2,1,0:T(8,128)S(1)} %get-tuple-element.69.state, ...), custom_call_target="tpu_custom_call" | custom-call | tf_op jit(solution)/shard_map/face_kernel/pallas_call | solution.py:512
  21.1 3.6 %collective-permute-start.8 = (f32[200,128]{1,0:T(8,128)S(1)}, f32[200,128]{1,0:T(8,128)S(1)}, u32[]{:S(2)}, u32[]{:S(2)}) collective-permute-start(f32[200,128]{1,0:T(8,128)S(1)} %get-tuple-element.83), channel_id=1, source_target_pairs={{0,32},{1,2},{2,1},{3,4},{4,3},{5,6},{6,5},{7,8},{8,7},{9,10},{10,... | collective-permute-start | bytes 307208 | tf_op jit(solution)/shard_map/ppermute | solution.py:547
  24.7 2.8 %collective-permute-start.9 = (f32[14,8,128]{2,1,0:T(8,128)S(1)}, f32[14,8,128]{2,1,0:T(8,128)S(1)}, u32[]{:S(2)}, u32[]{:S(2)}) collective-permute-start(f32[14,8,128]{2,1,0:T(8,128)S(1)} %get-tuple-element.84), channel_id=1, source_target_pairs={{0,1},{1,0},{2,3},{3,2},{4,5},{5,4},{6,7},{7,6},{8,9},{9,8},{10,11... | collective-permute-start | bytes 172040 | tf_op jit(solution)/shard_map/ppermute | solution.py:547
  27.5 0.9 %volume_kernel.5 = (f32[25,16,128]{2,1,0:T(8,128)S(1)}, f32[25,16,128]{2,1,0:T(8,128)S(1)}) custom-call(f32[21,21,128]{2,1,0:T(8,128)S(1)} %get-tuple-element.61.coupling, f32[25,16,128]{2,1,0:T(8,128)S(1)} %get-tuple-element.79.state, f32[25,16,128]{2,1,0:T(8,128)S(1)} %get-tuple-element.54.state.start, f32[3,16,128]{2,1,0:T(8,128)S(1)} %get-tuple-element.62.walls, ...), custom_call_target="tpu_custom_call" | custom-call | tf_op jit(solution)/shard_map/volume_kernel/pallas_call | solution.py:512
  28.5 0.8 %back_volume_kernel.3.inner = f32[25,16,128]{2,1,0:T(8,128)S(1)} custom-call(f32[21,21,128]{2,1,0:T(8,128)S(1)} %get-tuple-element.61.coupling, f32[25,16,128]{2,1,0:T(8,128)S(1)} %get-tuple-element.79.state, f32[25,16,128]{2,1,0:T(8,128)S(1)} %get-tuple-element.81.lam, f32[25,16,128]{2,1,0:T(8,128)S(1)} %get-tuple-element.82.near, ...), custom_call_target="tpu_custom_call" | custom-call | tf_op jit(solution)/shard_map/back_volume_kernel/pallas_call | solution.py:512
  29.3 1.1 %collective-permute-done.9.refs_1_ = f32[14,8,128]{2,1,0:T(8,128)S(1)} collective-permute-done((f32[14,8,128]{2,1,0:T(8,128)S(1)}, f32[14,8,128]{2,1,0:T(8,128)S(1)}, u32[]{:S(2)}, u32[]{:S(2)}) %collective-permute-start.9) | collective-permute-done | bytes 57376 | tf_op jit(solution)/shard_map/ppermute | solution.py:547
  30.4 0.9 %turn_kernel.1 = (f32[25,16,128]{2,1,0:T(8,128)S(1)}, f32[25,16,128]{2,1,0:T(8,128)S(1)}, f32[25,16,128]{2,1,0:T(8,128)S(1)}, f32[25,16,128]{2,1,0:T(8,128)S(1)}...) custom-call(f32[25,16,128]{2,1,0:T(8,128)S(1)} %get-tuple-element.79.sta, ...), custom_call_target="tpu_custom_call" | custom-call | tf_op jit(solution)/shard_map/turn_kernel/pallas_call | solution.py:512
  31.3 3.9 %collective-permute-start.12 = (f32[100,128]{1,0:T(8,128)S(1)}, f32[100,128]{1,0:T(8,128)S(1)}, u32[]{:S(2)}, u32[]{:S(2)}) collective-permute-start(f32[100,128]{1,0:T(8,128)S(1)} %get-tuple-element.93), channel_id=1, source_target_pairs={{0,32},{1,2},{2,1},{3,4},{4,3},{5,6},{6,5},{7,8},{8,7},{9,10},{10,... | collective-permute-start | bytes 153608 | tf_op jit(solution)/shard_map/ppermute | solution.py:547
  35.3 2.3 %collective-permute-start.13 = (f32[7,8,128]{2,1,0:T(8,128)S(1)}, f32[7,8,128]{2,1,0:T(8,128)S(1)}, u32[]{:S(2)}, u32[]{:S(2)}) collective-permute-start(f32[7,8,128]{2,1,0:T(8,128)S(1)} %get-tuple-element.94), channel_id=1, source_target_pairs={{0,1},{1,0},{2,3},{3,2},{4,5},{5,4},{6,7},{7,6},{8,9},{9,8},{10,11... | collective-permute-start | bytes 86024 | tf_op jit(solution)/shard_map/ppermute | solution.py:547
  37.6 0.8 %back_volume_kernel.4.inner = f32[25,16,128]{2,1,0:T(8,128)S(1)} custom-call(f32[21,21,128]{2,1,0:T(8,128)S(1)} %get-tuple-element.61.coupling, f32[25,16,128]{2,1,0:T(8,128)S(1)} %get-tuple-element.69.state, f32[25,16,128]{2,1,0:T(8,128)S(1)} %get-tuple-element.89.lam, f32[25,16,128]{2,1,0:T(8,128)S(1)} %get-tuple-element.90.near, ...), custom_call_target="tpu_custom_call" | custom-call | tf_op jit(solution)/shard_map/back_volume_kernel/pallas_call | solution.py:512
  38.4 2.2 %collective-permute-done.13.refs_1_ = f32[7,8,128]{2,1,0:T(8,128)S(1)} collective-permute-done((f32[7,8,128]{2,1,0:T(8,128)S(1)}, f32[7,8,128]{2,1,0:T(8,128)S(1)}, u32[]{:S(2)}, u32[]{:S(2)}) %collective-permute-start.13) | collective-permute-done | bytes 28704 | tf_op jit(solution)/shard_map/ppermute | solution.py:547
  40.7 0.7 %middle_kernel.1 = (f32[25,16,128]{2,1,0:T(8,128)S(1)}, f32[100,128]{1,0:T(8,128)S(1)}, f32[7,8,128]{2,1,0:T(8,128)S(1)}, f32[100,128]{1,0:T(8,128)S(1)}, f32[7,8,128]{2,1,0:T(8,128)S(1)}) custom-call(f32[25,16,128]{2,1,0:T(8,128)S(1)} %get-tuple-element.69.state, f32[25,16,128]{2,1,0:T(8,128)S(1)} %get-tuple-element.89.lam, ...), custom_call_target="tpu_custom_call" | custom-call | tf_op jit(solution)/shard_map/middle_kernel/pallas_call | solution.py:512
  41.4 2.2 %collective-permute-start.16 = (f32[100,128]{1,0:T(8,128)S(1)}, f32[100,128]{1,0:T(8,128)S(1)}, u32[]{:S(2)}, u32[]{:S(2)}) collective-permute-start(f32[100,128]{1,0:T(8,128)S(1)} %get-tuple-element.102), channel_id=1, source_target_pairs={{0,32},{1,2},{2,1},{3,4},{4,3},{5,6},{6,5},{7,8},{8,7},{9,10},{10,... | collective-permute-start | bytes 153608 | tf_op jit(solution)/shard_map/ppermute | solution.py:547
  43.6 3.1 %collective-permute-start.17 = (f32[7,8,128]{2,1,0:T(8,128)S(1)}, f32[7,8,128]{2,1,0:T(8,128)S(1)}, u32[]{:S(2)}, u32[]{:S(2)}) collective-permute-start(f32[7,8,128]{2,1,0:T(8,128)S(1)} %get-tuple-element.103), channel_id=1, source_target_pairs={{0,1},{1,0},{2,3},{3,2},{4,5},{5,4},{6,7},{7,6},{8,9},{9,8},{10,11... | collective-permute-start | bytes 86024 | tf_op jit(solution)/shard_map/ppermute | solution.py:547
  46.7 1.0 %face_kernel.5 = f32[25,16,128]{2,1,0:T(8,128)} custom-call(f32[25,16,128]{2,1,0:T(8,128)S(1)} %get-tuple-element.79.state, f32[25,16,128]{2,1,0:T(8,128)S(1)} %get-tuple-element.80.inner, f32[3,16,128]{2,1,0:T(8,128)S(1)} %get-tuple-element.62.walls, f32[3,16,128]{2,1,0:T(8,128)S(1)} %get-tuple-element.64.factors, bf16[256,128]{1,0:T(8,128)(2,1)S(1)} %copy-done.2, ...), custom_call_target="tpu_custom_call" | custom-call | tf_op jit(solution)/shard_map/face_kernel/pallas_call | solution.py:512
  47.7 0.8 %back_volume_kernel.5.inner = f32[25,16,128]{2,1,0:T(8,128)S(1)} custom-call(f32[21,21,128]{2,1,0:T(8,128)S(1)} %get-tuple-element.61.coupling, f32[25,16,128]{2,1,0:T(8,128)S(1)} %get-tuple-element.54.state.start, f32[25,16,128]{2,1,0:T(8,128)S(1)} %get-tuple-element.97.lam, f32[25,16,128]{2,1,0:T(8,128)S(1)} %get-tuple-element.98.near, ...), custom_call_target="tpu_custom_call" | custom-call | tf_op jit(solution)/shard_map/back_volume_kernel/pallas_call | solution.py:512
  48.5 0.5 collective-permute-done.17.lb
  49.0 1.1 %end_kernel.1 = f32[25,16,128]{2,1,0:T(8,128)} custom-call(f32[25,16,128]{2,1,0:T(8,128)S(1)} %get-tuple-element.54.state.start, f32[25,16,128]{2,1,0:T(8,128)S(1)} %get-tuple-element.97.lam, f32[25,16,128]{2,1,0:T(8,128)S(1)} %back_volume_kernel.5.inner, f32[25,16,128]{2,1,0:T(8,128)S(1)} %get-tuple-element.99.near_x, ...), custom_call_target="tpu_custom_call" | custom-call | tf_op jit(solution)/shard_map/end_kernel/pallas_call | solution.py:512
  (28 shorter events, 0.1 us)
Async XLA Ops:
  1.8 8.7 %copy-start.1 = (bf16[2,384,128]{2,1,0:T(8,128)(2,1)S(1)}, bf16[2,384,128]{2,1,0:T(8,128)(2,1)}, u32[]{:S(2)}) copy-start(bf16[2,384,128]{2,1,0:T(8,128)(2,1)} %constant.8.clone.table) | copy-start | bytes 589828
  1.9 9.8 %collective-permute-start = (f32[100,128]{1,0:T(8,128)S(1)}, f32[100,128]{1,0:T(8,128)S(1)}, u32[]{:S(2)}, u32[]{:S(2)}) collective-permute-start(f32[100,128]{1,0:T(8,128)S(1)} %get-tuple-element.65), channel_id=1, source_target_pairs={{0,32},{1,2},{2,1},{3,4},{4,3},{5,6},{6,5},{7,8},{8,7},{9,10},{10,... | collective-permute-start | bytes 153608 | tf_op jit(solution)/shard_map/ppermute | solution.py:547
  5.9 5.7 %collective-permute-start.2 = (f32[100,128]{1,0:T(8,128)S(1)}, f32[100,128]{1,0:T(8,128)S(1)}, u32[]{:S(2)}, u32[]{:S(2)}) collective-permute-start(f32[100,128]{1,0:T(8,128)S(1)} %get-tuple-element.67), channel_id=1, source_target_pairs={{0,1},{1,0},{2,3},{3,2},{4,5},{5,4},{6,7},{7,6},{8,9},{9,8},{10,11... | collective-permute-start | bytes 153608 | tf_op jit(solution)/shard_map/ppermute | solution.py:547
  6.0 5.7 %collective-permute-start.1 = (f32[7,8,128]{2,1,0:T(8,128)S(1)}, f32[7,8,128]{2,1,0:T(8,128)S(1)}, u32[]{:S(2)}, u32[]{:S(2)}) collective-permute-start(f32[7,8,128]{2,1,0:T(8,128)S(1)} %get-tuple-element.66), channel_id=1, source_target_pairs={{0,1},{1,0},{2,3},{3,2},{4,5},{5,4},{6,7},{7,6},{8,9},{9,8},{10,11... | collective-permute-start | bytes 86024 | tf_op jit(solution)/shard_map/ppermute | solution.py:547
  10.1 1.6 %collective-permute-start.3 = (f32[7,8,128]{2,1,0:T(8,128)S(1)}, f32[7,8,128]{2,1,0:T(8,128)S(1)}, u32[]{:S(2)}, u32[]{:S(2)}) collective-permute-start(f32[7,8,128]{2,1,0:T(8,128)S(1)} %get-tuple-element.68), channel_id=1, source_target_pairs={{0,32},{1,33},{2,34},{3,35},{4,36},{5,37},{6,38},{7,39},{8,40},{9,... | collective-permute-start | bytes 86024 | tf_op jit(solution)/shard_map/ppermute | solution.py:547
  10.6 1.1 %copy-start.2 = (bf16[256,128]{1,0:T(8,128)(2,1)S(1)}, bf16[256,128]{1,0:T(8,128)(2,1)}, u32[]{:S(2)}) copy-start(bf16[256,128]{1,0:T(8,128)(2,1)} %constant.10.clone.mean) | copy-start | bytes 196612
  12.3 8.2 %collective-permute-start.4 = (f32[100,128]{1,0:T(8,128)S(1)}, f32[100,128]{1,0:T(8,128)S(1)}, u32[]{:S(2)}, u32[]{:S(2)}) collective-permute-start(f32[100,128]{1,0:T(8,128)S(1)} %get-tuple-element.71), channel_id=1, source_target_pairs={{0,32},{1,2},{2,1},{3,4},{4,3},{5,6},{6,5},{7,8},{8,7},{9,10},{10,... | collective-permute-start | bytes 153608 | tf_op jit(solution)/shard_map/ppermute | solution.py:547
  15.0 5.6 %collective-permute-start.6 = (f32[100,128]{1,0:T(8,128)S(1)}, f32[100,128]{1,0:T(8,128)S(1)}, u32[]{:S(2)}, u32[]{:S(2)}) collective-permute-start(f32[100,128]{1,0:T(8,128)S(1)} %get-tuple-element.73), channel_id=1, source_target_pairs={{0,1},{1,0},{2,3},{3,2},{4,5},{5,4},{6,7},{7,6},{8,9},{9,8},{10,11... | collective-permute-start | bytes 153608 | tf_op jit(solution)/shard_map/ppermute | solution.py:547
  15.1 5.4 %collective-permute-start.5 = (f32[7,8,128]{2,1,0:T(8,128)S(1)}, f32[7,8,128]{2,1,0:T(8,128)S(1)}, u32[]{:S(2)}, u32[]{:S(2)}) collective-permute-start(f32[7,8,128]{2,1,0:T(8,128)S(1)} %get-tuple-element.72), channel_id=1, source_target_pairs={{0,1},{1,0},{2,3},{3,2},{4,5},{5,4},{6,7},{7,6},{8,9},{9,8},{10,11... | collective-permute-start | bytes 86024 | tf_op jit(solution)/shard_map/ppermute | solution.py:547
  18.8 1.8 %collective-permute-start.7 = (f32[7,8,128]{2,1,0:T(8,128)S(1)}, f32[7,8,128]{2,1,0:T(8,128)S(1)}, u32[]{:S(2)}, u32[]{:S(2)}) collective-permute-start(f32[7,8,128]{2,1,0:T(8,128)S(1)} %get-tuple-element.74), channel_id=1, source_target_pairs={{0,32},{1,33},{2,34},{3,35},{4,36},{5,37},{6,38},{7,39},{8,40},{9,... | collective-permute-start | bytes 86024 | tf_op jit(solution)/shard_map/ppermute | solution.py:547
  21.1 9.3 %collective-permute-start.8 = (f32[200,128]{1,0:T(8,128)S(1)}, f32[200,128]{1,0:T(8,128)S(1)}, u32[]{:S(2)}, u32[]{:S(2)}) collective-permute-start(f32[200,128]{1,0:T(8,128)S(1)} %get-tuple-element.83), channel_id=1, source_target_pairs={{0,32},{1,2},{2,1},{3,4},{4,3},{5,6},{6,5},{7,8},{8,7},{9,10},{10,... | collective-permute-start | bytes 307208 | tf_op jit(solution)/shard_map/ppermute | solution.py:547
  24.7 5.7 %collective-permute-start.10 = (f32[200,128]{1,0:T(8,128)S(1)}, f32[200,128]{1,0:T(8,128)S(1)}, u32[]{:S(2)}, u32[]{:S(2)}) collective-permute-start(f32[200,128]{1,0:T(8,128)S(1)} %get-tuple-element.85), channel_id=1, source_target_pairs={{0,1},{1,0},{2,3},{3,2},{4,5},{5,4},{6,7},{7,6},{8,9},{9,8},{10,11... | collective-permute-start | bytes 307208 | tf_op jit(solution)/shard_map/ppermute | solution.py:547
  24.7 5.7 %collective-permute-start.9 = (f32[14,8,128]{2,1,0:T(8,128)S(1)}, f32[14,8,128]{2,1,0:T(8,128)S(1)}, u32[]{:S(2)}, u32[]{:S(2)}) collective-permute-start(f32[14,8,128]{2,1,0:T(8,128)S(1)} %get-tuple-element.84), channel_id=1, source_target_pairs={{0,1},{1,0},{2,3},{3,2},{4,5},{5,4},{6,7},{7,6},{8,9},{9,8},{10,11... | collective-permute-start | bytes 172040 | tf_op jit(solution)/shard_map/ppermute | solution.py:547
  27.5 2.9 %collective-permute-start.11 = (f32[14,8,128]{2,1,0:T(8,128)S(1)}, f32[14,8,128]{2,1,0:T(8,128)S(1)}, u32[]{:S(2)}, u32[]{:S(2)}) collective-permute-start(f32[14,8,128]{2,1,0:T(8,128)S(1)} %get-tuple-element.86), channel_id=1, source_target_pairs={{0,32},{1,33},{2,34},{3,35},{4,36},{5,37},{6,38},{7,39},{8,40},{9,... | collective-permute-start | bytes 172040 | tf_op jit(solution)/shard_map/ppermute | solution.py:547
  27.5 0.9 %copy-start = (bf16[2,128,384]{2,1,0:T(8,128)(2,1)S(1)}, bf16[2,128,384]{2,1,0:T(8,128)(2,1)}, u32[]{:S(2)}) copy-start(bf16[2,128,384]{2,1,0:T(8,128)(2,1)} %constant.9.clone.table) | copy-start | bytes 589828
  31.3 9.3 %collective-permute-start.12 = (f32[100,128]{1,0:T(8,128)S(1)}, f32[100,128]{1,0:T(8,128)S(1)}, u32[]{:S(2)}, u32[]{:S(2)}) collective-permute-start(f32[100,128]{1,0:T(8,128)S(1)} %get-tuple-element.93), channel_id=1, source_target_pairs={{0,32},{1,2},{2,1},{3,4},{4,3},{5,6},{6,5},{7,8},{8,7},{9,10},{10,... | collective-permute-start | bytes 153608 | tf_op jit(solution)/shard_map/ppermute | solution.py:547
  35.3 5.4 %collective-permute-start.14 = (f32[100,128]{1,0:T(8,128)S(1)}, f32[100,128]{1,0:T(8,128)S(1)}, u32[]{:S(2)}, u32[]{:S(2)}) collective-permute-start(f32[100,128]{1,0:T(8,128)S(1)} %get-tuple-element.95), channel_id=1, source_target_pairs={{0,1},{1,0},{2,3},{3,2},{4,5},{5,4},{6,7},{7,6},{8,9},{9,8},{10,11... | collective-permute-start | bytes 153608 | tf_op jit(solution)/shard_map/ppermute | solution.py:547
  35.3 5.4 %collective-permute-start.13 = (f32[7,8,128]{2,1,0:T(8,128)S(1)}, f32[7,8,128]{2,1,0:T(8,128)S(1)}, u32[]{:S(2)}, u32[]{:S(2)}) collective-permute-start(f32[7,8,128]{2,1,0:T(8,128)S(1)} %get-tuple-element.94), channel_id=1, source_target_pairs={{0,1},{1,0},{2,3},{3,2},{4,5},{5,4},{6,7},{7,6},{8,9},{9,8},{10,11... | collective-permute-start | bytes 86024 | tf_op jit(solution)/shard_map/ppermute | solution.py:547
  37.6 3.1 %collective-permute-start.15 = (f32[7,8,128]{2,1,0:T(8,128)S(1)}, f32[7,8,128]{2,1,0:T(8,128)S(1)}, u32[]{:S(2)}, u32[]{:S(2)}) collective-permute-start(f32[7,8,128]{2,1,0:T(8,128)S(1)} %get-tuple-element.96), channel_id=1, source_target_pairs={{0,32},{1,33},{2,34},{3,35},{4,36},{5,37},{6,38},{7,39},{8,40},{9,... | collective-permute-start | bytes 86024 | tf_op jit(solution)/shard_map/ppermute | solution.py:547
  41.4 7.6 %collective-permute-start.16 = (f32[100,128]{1,0:T(8,128)S(1)}, f32[100,128]{1,0:T(8,128)S(1)}, u32[]{:S(2)}, u32[]{:S(2)}) collective-permute-start(f32[100,128]{1,0:T(8,128)S(1)} %get-tuple-element.102), channel_id=1, source_target_pairs={{0,32},{1,2},{2,1},{3,4},{4,3},{5,6},{6,5},{7,8},{8,7},{9,10},{10,... | collective-permute-start | bytes 153608 | tf_op jit(solution)/shard_map/ppermute | solution.py:547
  43.6 5.4 %collective-permute-start.18 = (f32[100,128]{1,0:T(8,128)S(1)}, f32[100,128]{1,0:T(8,128)S(1)}, u32[]{:S(2)}, u32[]{:S(2)}) collective-permute-start(f32[100,128]{1,0:T(8,128)S(1)} %get-tuple-element.104), channel_id=1, source_target_pairs={{0,1},{1,0},{2,3},{3,2},{4,5},{5,4},{6,7},{7,6},{8,9},{9,8},{10,11... | collective-permute-start | bytes 153608 | tf_op jit(solution)/shard_map/ppermute | solution.py:547
  43.6 5.4 %collective-permute-start.17 = (f32[7,8,128]{2,1,0:T(8,128)S(1)}, f32[7,8,128]{2,1,0:T(8,128)S(1)}, u32[]{:S(2)}, u32[]{:S(2)}) collective-permute-start(f32[7,8,128]{2,1,0:T(8,128)S(1)} %get-tuple-element.103), channel_id=1, source_target_pairs={{0,1},{1,0},{2,3},{3,2},{4,5},{5,4},{6,7},{7,6},{8,9},{9,8},{10,11... | collective-permute-start | bytes 86024 | tf_op jit(solution)/shard_map/ppermute | solution.py:547
  46.7 2.3 %collective-permute-start.19 = (f32[7,8,128]{2,1,0:T(8,128)S(1)}, f32[7,8,128]{2,1,0:T(8,128)S(1)}, u32[]{:S(2)}, u32[]{:S(2)}) collective-permute-start(f32[7,8,128]{2,1,0:T(8,128)S(1)} %get-tuple-element.105), channel_id=1, source_target_pairs={{0,32},{1,33},{2,34},{3,35},{4,36},{5,37},{6,38},{7,39},{8,40},{9,... | collective-permute-start | bytes 86024 | tf_op jit(solution)/shard_map/ppermute | solution.py:547
